TPU v7x, 768 devices: a whole 4x8x12 slice. The times are simulated.
768 devices in a mesh: grp: 16 (over y, core), own: 48 (over x, z).
Axes of the slice: x: 4, y: 8, z: 12, core: 2. Of those that a mesh axis runs over, the one named last changes fastest.
Arguments:
- fields: bfloat16 [192, 256, 128], P(None, 'grp'), may hold values from -6 to 6
- labels: int32 [192], replicated, may hold values 0 or 1
- pair_first: int32 [16, 48, 16], P('grp', 'own'), may hold values from 0 to 255, as said below
- pair_second: int32 [16, 48, 16], P(None, 'own'), may hold values from 0 to 255, as said below
- pair_count: int32 [16, 48], P('grp', 'own'), may hold values from 4 to 16, as said below
- pair_mats: float32 [16, 48, 16, 128, 128], P('grp', 'own'), may hold values from -6 to 6
Outputs:
- logits: float32 [192], replicated
- field_grad: float32 [192, 256, 128], P('own', 'grp')
- new_mats: float32 [16, 48, 16, 128, 128], P('grp', 'own')
Inputs may be any that keep to these rules, and one draw needn't show every extreme that they name: pair_first[g, o, s] lies in the block of fields g * 16 to (g + 1) * 16 - 1. `pair_second`: on every device (g, o), each block of 16 fields holds the second field of exactly 1 of the 16 slots; the second field is never the first. `pair_count`: slots at and beyond the count hold no pair; one device has all 16 slots live.
All inputs are finite; a program needn't handle non-finite values.
Results may differ from a plain program's by a relative error of at most 0.0003.
Values may be sent and summed in bfloat16 or wider, within the bound.
No kernel may reach another device: no remote copies, remote signals or barrier semaphores. Data moves between devices by JAX's collectives and lax.ppermute only.
A program may use at most 32 MiB of HBM per device.

v0:
```python
import math

import jax
import jax.numpy as jnp
from jax import lax
from jax.sharding import PartitionSpec as P

STEPS = 2


logit_gain = 1.5
step_size = 1000.0
highest = lax.Precision.HIGHEST


def logit_errors(partial_value, targets, logit_scale):
    total_sum = lax.psum(partial_value, ("grp", "own"))
    logits = logit_scale * total_sum
    errors = jax.nn.sigmoid(logits) - targets
    return (logits, errors)


def on_device(fields, labels, pair_first, pair_second, pair_count, pair_mats):
    groups = lax.axis_size("grp")
    owners = lax.axis_size("own")
    my_group = lax.axis_index("grp")
    samples, per_block, feature = fields.shape
    slot_count = pair_first.shape[2]
    capacity = slot_count // groups
    second_table = pair_second[:, 0, :]
    block_ids = second_table // per_block
    offsets = second_table % per_block
    member = (block_ids[:, :, None] == jnp.arange(groups, dtype=jnp.int32)[None, None, :]).astype(
        jnp.int32
    )
    slot_ranks = jnp.sum((jnp.cumsum(member, axis=1) - 1) * member, axis=2)
    places = block_ids * capacity + slot_ranks
    chosen = (block_ids[:, :, None] == my_group) & (
        slot_ranks[:, :, None] == jnp.arange(capacity, dtype=jnp.int32)[None, None, :]
    )
    served = jnp.sum(jnp.where(chosen, offsets[:, :, None], 0), axis=1).reshape(-1)
    outgoing = jnp.take(fields, served, axis=1)
    incoming = lax.all_to_all(outgoing, "grp", split_axis=1, concat_axis=1, tiled=True)
    my_places = lax.dynamic_index_in_dim(places, my_group, 0, keepdims=False)
    second_vec = jnp.take(incoming, my_places, axis=1).astype(jnp.float32)
    first_local = pair_first[0, 0] - my_group * per_block
    first_vec = jnp.take(fields, first_local, axis=1).astype(jnp.float32)
    live_mask = (jnp.arange(slot_count, dtype=jnp.int32) < pair_count[0, 0]).astype(jnp.float32)
    matrices = pair_mats[0, 0]
    targets = labels.astype(jnp.float32)
    logit_scale = logit_gain / math.sqrt(groups * owners * slot_count)
    root_width = math.sqrt(feature)
    logits = jnp.zeros((samples,), jnp.float32)
    grad_first = jnp.zeros(first_vec.shape, jnp.float32)
    grad_second = jnp.zeros(first_vec.shape, jnp.float32)
    for step_index in range(STEPS):
        mixed = jnp.einsum("bsk,skl->bsl", first_vec, matrices, precision=highest)
        partial_value = jnp.sum(
            jnp.sum(mixed * second_vec, axis=2) / feature * live_mask[None, :], axis=1
        )
        logits, errors = logit_errors(partial_value, targets, logit_scale)
        if step_index == STEPS - 1:
            grad_first = (
                errors[:, None, None]
                * jnp.einsum("skl,bsl->bsk", matrices, second_vec, precision=highest)
                / root_width
                * live_mask[None, :, None]
            )
            grad_second = errors[:, None, None] * mixed / root_width * live_mask[None, :, None]
        gradient = jnp.einsum(
            "bsk,bsl->skl", first_vec * errors[:, None, None], second_vec, precision=highest
        )
        matrices = (
            matrices
            - step_size * logit_scale / (samples * feature) * live_mask[:, None, None] * gradient
        )
    slot_iota = jnp.arange(slot_count, dtype=jnp.int32)
    slot_of = jnp.sum(
        jnp.where(my_places[None, :] == slot_iota[:, None], slot_iota[None, :], 0), axis=1
    )
    returned = lax.all_to_all(
        jnp.take(grad_second, slot_of, axis=1), "grp", split_axis=1, concat_axis=1, tiled=True
    )
    block_iota = jnp.arange(per_block, dtype=jnp.int32)
    pick_second = (served[:, None] == block_iota[None, :]).astype(jnp.float32)
    pick_first = (first_local[:, None] == block_iota[None, :]).astype(jnp.float32)
    dense_grad = jnp.einsum("bsk,sf->bfk", grad_first, pick_first, precision=highest)
    dense_grad = dense_grad + jnp.einsum("bpk,pf->bfk", returned, pick_second, precision=highest)
    field_grad = lax.psum_scatter(dense_grad, "own", scatter_dimension=0, tiled=True)
    return (logits, field_grad, matrices[None, None])


def solution(mesh):
    in_specs = (
        P(None, "grp", None),
        P(),
        P("grp", "own", None),
        P(None, "own", None),
        P("grp", "own"),
        P("grp", "own", None, None, None),
    )
    out_specs = (P(), P("own", "grp", None), P("grp", "own", None, None, None))
    return jax.shard_map(
        on_device, mesh=mesh, in_specs=in_specs, out_specs=out_specs, check_vma=False
    )
```

profile of v0, /device:TPU:1, one launch (start us, length us, event | category | flops | bytes accessed | tf_op | source)
XLA Modules:
  0.0 749.8 jit_solution(11128761640576148177)
XLA Ops:
  7.2 0.8 copy.22
  8.0 0.5 fusion.49
  8.5 0.7 compare_and_fusion.2
  9.2 2.9 gather_fusion.2
  12.1 0.1 select_bitcast_fusion.1
  12.2 1.1 copy.24
  13.3 13.9 %all-to-all-start = ((bf16[192,16,128]{2,0,1:T(8,128)(2,1)}), bf16[192,16,128]{2,0,1:T(8,128)(2,1)S(1)}, u32[]{:S(2)}, u32[]{:S(2)}) async-start(bf16[192,16,128]{2,0,1:T(8,128)(2,1)} %copy.24), calls=%async_computation | async-start | bytes 1572864 | tf_op jit(solution)/shard_map/all_to_all | solution.py:43
  27.9 2.9 gather_fusion.1
  30.8 0.2 fusion.34
  31.0 0.1 select_reduce_fusion
  31.1 18.8 %all-to-all-done = bf16[192,16,128]{2,0,1:T(8,128)(2,1)S(1)} async-done(((bf16[192,16,128]{2,0,1:T(8,128)(2,1)}), bf16[192,16,128]{2,0,1:T(8,128)(2,1)S(1)}, u32[]{:S(2)}, u32[]{:S(2)}) %all-to-all-start) | async-done | bytes 786464 | tf_op jit(solution)/shard_map/all_to_all | solution.py:43
  50.0 0.7 gather_fusion.3
  50.7 2.7 fusion.2
  53.4 0.1 multiply_reduce_fusion.1
  53.5 111.4 %psum.14 = f32[192]{0:T(256)S(1)} all-reduce(f32[192]{0:T(256)S(1)} %multiply_reduce_fusion.1), channel_id=1, replica_groups=mesh['grp'=16,'own'=48] {'grp','own'}, use_global_device_ids=true, to_apply=%region_5.7 | all-reduce | flops 192 | bytes 1536 | tf_op jit(solution)/shard_map/psum | solution.py:17
  164.9 3.3 fusion.15
  168.2 3.0 fusion.3
  171.2 0.1 multiply_reduce_fusion
  171.3 103.7 %psum.15 = f32[192]{0:T(256)S(1)} all-reduce(f32[192]{0:T(256)S(1)} %multiply_reduce_fusion), channel_id=1, replica_groups=mesh['grp'=16,'own'=48] {'grp','own'}, use_global_device_ids=true, to_apply=%region_8.10 | all-reduce | flops 192 | bytes 1536 | tf_op jit(solution)/shard_map/psum | solution.py:17
  275.0 0.6 divide_subtract_fusion
  275.5 1.4 fusion.4
  276.9 2.1 gather_fusion
  279.0 1.4 select_bitcast_fusion
  280.3 5.7 all-to-all-start.1
  286.0 0.0 reduce-scatter.2.cloned.1.call-start
  286.1 2.4 multiply_bitcast_fusion
  288.5 36.1 %all-to-all-done.1 = f32[192,16,128]{2,0,1:T(8,128)} async-done(((f32[192,16,128]{2,0,1:T(8,128)}), f32[192,16,128]{2,0,1:T(8,128)}, u32[]{:S(2)}, u32[]{:S(2)}) %all-to-all-start.1) | async-done | bytes 1572896 | tf_op jit(solution)/shard_map/all_to_all | solution.py:81
  324.6 3.0 fusion.5
  327.6 2.9 add_bitcast_fusion
  330.6 1.2 copy-done.2
  331.8 4.1 fusion.13
  335.9 407.0 %reduce-scatter.2.cloned.1.call-done = f32[4,16,128]{2,1,0:T(8,128)} async-done(((f32[192,16,128]{2,1,0:T(8,128)}), f32[4,16,128]{2,1,0:T(8,128)}) %reduce-scatter.2.cloned.1.call-update) | async-done | bytes 32784 | tf_op jit(solution)/shard_map/reduce_scatter | solution.py:89
  (26 shorter events, 0.2 us)
Async XLA Ops:
  7.2 2.1 copy-start
  13.3 36.6 %all-to-all-start = ((bf16[192,16,128]{2,0,1:T(8,128)(2,1)}), bf16[192,16,128]{2,0,1:T(8,128)(2,1)S(1)}, u32[]{:S(2)}, u32[]{:S(2)}) async-start(bf16[192,16,128]{2,0,1:T(8,128)(2,1)} %copy.24), calls=%async_computation | async-start | bytes 1572864 | tf_op jit(solution)/shard_map/all_to_all | solution.py:43
  30.8 134.1 %copy-start.3 = (bf16[16,192,128]{2,0,1:T(8,128)(2,1)}, bf16[16,192,128]{2,0,1:T(8,128)(2,1)S(1)}, u32[]{:S(2)}) copy-start(bf16[16,192,128]{2,0,1:T(8,128)(2,1)S(1)} %gather_fusion.1) | copy-start | bytes 2359300
  50.7 114.2 %copy-start.4 = (s32[192]{0:T(256)S(1)}, s32[192]{0:T(256)}, u32[]{:S(2)}) copy-start(s32[192]{0:T(256)} %param.9) | copy-start | bytes 2308
  168.1 3.0 copy-start.1
  280.3 44.2 %all-to-all-start.1 = ((f32[192,16,128]{2,0,1:T(8,128)}), f32[192,16,128]{2,0,1:T(8,128)}, u32[]{:S(2)}, u32[]{:S(2)}) async-start(f32[192,16,128]{2,0,1:T(8,128)} %select_bitcast_fusion), calls=%async_computation.1 | async-start | bytes 3145728 | tf_op jit(solution)/shard_map/all_to_all | solution.py:81
  286.0 456.9 %reduce-scatter.2.cloned.1.call-start = ((), (), s32[]{:S(2)}) async-start(), calls=%async_computation.3 | async-start | bytes 1605632 | tf_op jit(solution)/shard_map/reduce_scatter | solution.py:89
  330.6 1.2 copy-start.2
Sparse Core Ops, SparseCore 0:
  330.7 412.1 reduce-scatter.1
where the time goes:
time: 758 us; the launch traced here: 750 us
  waiting for transfers between devices  462 us (61%)
  blocking collectives  215 us (28%)
  matrix products  21.5 us (3%)
  starting transfers between devices  19.6 us (3%)
  between operations  14.9 us (2%)
  local copies, waits for them, and re-layouts  11.6 us (2%)
    reduce_scatter x1, waiting for transfers between devices, on_device(): lax.psum_scatter(dense_grad, 'own', scatter_dimension=0, tiled=True)  407 us
    psum x2, blocking collectives, logit_errors(): total_sum = lax.psum(partial_value, ('grp', 'own'))  215 us
    all_to_all x1, waiting for transfers between devices, on_device(): lax.all_to_all(jnp.take(grad_second, slot_of, axis=1), 'grp', split_axis=...  36.1 us
    all_to_all x1, waiting for transfers between devices, on_device(): lax.all_to_all(outgoing, 'grp', split_axis=1, concat_axis=1, tiled=True)  18.8 us
  transfers between devices with their start and end apart: 3, of which 3 were waited for; matrix products, arithmetic and copies ran while one was open for 1% of the time, Pallas kernels for 0%

commit v1 on v0

v1 whole, which is shorter than its diff:
```python
import functools
import math

import jax
import jax.numpy as jnp
from jax import lax
from jax.experimental import pallas as pl
from jax.experimental.pallas import tpu as pltpu
from jax.sharding import Mesh
from jax.sharding import PartitionSpec as P

GRP = ("y", "core")
OWN = ("x", "z")
logit_gain = 1.5
step_size = 1000.0
f32 = jnp.float32
bf16 = jnp.bfloat16

SLOT, FIRST, LIVE, SERVED, ME = range(5)


def split(x):
    hi = x.astype(bf16)
    return hi, (x - hi.astype(f32)).astype(bf16)


def dot(a, b, dims):
    return lax.dot_general(a, b, (dims, ((), ())), preferred_element_type=f32)


def dot_rhs(a, pair, dims):
    return dot(a, pair[0], dims) + dot(a, pair[1], dims)


def dot_lhs(pair, b, dims):
    return dot(pair[0], b, dims) + dot(pair[1], b, dims)


AB, ABT, ATB = ((1,), (0,)), ((1,), (1,)), ((0,), (0,))


def row_sums(acc):
    ones = jnp.ones((8, 128), f32)
    exact = functools.partial(
        lax.dot_general,
        dimension_numbers=(ABT, ((), ())),
        precision=lax.Precision.HIGHEST,
        preferred_element_type=f32,
    )
    low = exact(ones, acc[:128])
    rest = acc[128:]
    high = exact(ones, jnp.concatenate([rest, jnp.zeros((256 - acc.shape[0], 128), f32)], axis=0))
    rows = lax.broadcasted_iota(jnp.int32, (8, 128), 0)
    return jnp.where(rows < 4, low, high)


def spread(chunk, samples):
    low = jnp.transpose(jnp.broadcast_to(chunk[0:1], (128, 128)))
    high = jnp.transpose(jnp.broadcast_to(chunk[4:5], (128, 128)))
    return jnp.concatenate([low, high[: samples - 128]], axis=0)


def gather_kernel(tab, ft, out):
    @pl.loop(0, out.shape[0])
    def _(j):
        out[j] = ft[tab[SERVED, j]]


def partial_kernel(tab, ft, second, mats, out, acc):
    acc[...] = jnp.zeros_like(acc)

    def step(j, carry):
        live = tab[LIVE, j].astype(f32)
        mixed = dot_rhs(ft[tab[FIRST, j]], split(mats[tab[SLOT, j]] * live), AB)
        acc[...] += mixed * second[j].astype(f32)
        return carry

    lax.fori_loop(0, second.shape[0], step, 0, unroll=4)
    chunk = row_sums(acc[...] * (1.0 / 128.0))
    for i in range(out.shape[0]):
        out[i] = chunk


def sum_kernel(parts, out):
    total = parts[0]
    for i in range(1, parts.shape[0]):
        total = total + parts[i]
    for i in range(out.shape[0]):
        out[i] = total


def total_of(parts, lo):
    total = parts[0, lo : lo + 8]
    for i in range(1, parts.shape[0]):
        total = total + parts[i, lo : lo + 8]
    return total


def terms_kernel(
    scale, rate, tab, ft, second, mats, sums, labels, moved, out, dense, acc, errs
):
    samples = second.shape[1]
    n_x, rows = dense.shape[0], samples // dense.shape[0]
    errors = jax.nn.sigmoid(scale * total_of(sums, 0)) - labels[...]
    errs[...] = spread(errors, samples)
    acc[...] = jnp.zeros_like(acc)
    dense[...] = jnp.zeros_like(dense)

    def step(j, carry):
        live = tab[LIVE, j].astype(f32)
        slot, first = tab[SLOT, j], tab[FIRST, j]
        va, vb = ft[first], second[j]
        gradient = dot_lhs(split(va.astype(f32) * errs[...]), vb, ATB)
        updated = mats[slot] - (rate * live) * gradient
        moved[j] = updated
        pair = split(updated * live)
        mixed = dot_rhs(va, pair, AB)
        acc[...] += mixed * vb.astype(f32)
        out[j, 0:samples] = mixed
        toward = dot_rhs(vb, pair, ABT)
        at = pl.ds(pl.multiple_of(first * rows, 8), rows)
        for i in range(n_x):
            dense[i, at] += toward[i * rows : (i + 1) * rows]
        return carry

    lax.fori_loop(0, second.shape[0], step, 0, unroll=2)
    chunk = row_sums(acc[...] * (1.0 / 128.0))
    for i in range(out.shape[0]):
        out[i, samples : samples + 8] = chunk


def dense_kernel(tab, got, dense_in, dense):
    dense[...] = dense_in[...]
    samples = got.shape[1] - 8
    n_x, rows = dense.shape[0], samples // dense.shape[0]
    last = dense.shape[1] - 8

    @pl.loop(0, got.shape[0])
    def _(j):
        at = pl.ds(pl.multiple_of(tab[SERVED, j] * rows, 8), rows)
        for i in range(n_x):
            dense[i, at] += got[j, i * rows : (i + 1) * rows]

    chunk = total_of(got, samples)
    for i in range(n_x):
        dense[i, last : last + 8] = chunk


def across_kernel(got, out):
    n_z, few = out.shape[0], (out.shape[1] - 8) // 16
    rows = n_z * few
    for f in range(16):
        total = got[0, f * rows : (f + 1) * rows]
        for i in range(1, got.shape[0]):
            total = total + got[i, f * rows : (f + 1) * rows]
        for k in range(n_z):
            out[k, f * few : (f + 1) * few] = total[k * few : (k + 1) * few]
    chunk = total_of(got, 16 * rows)
    for k in range(n_z):
        out[k, 16 * few :] = chunk


def last_kernel(
    scale, rate, tab, ft, second, moved, got, labels, logits, grads, mats, errs, sums
):
    samples = second.shape[1]
    few = grads.shape[0]
    value = scale * total_of(got, 16 * few)
    logits[...] = value
    errs[...] = spread(jax.nn.sigmoid(value) - labels[...], samples)
    total = got[0, : 16 * few]
    for i in range(1, got.shape[0]):
        total = total + got[i, : 16 * few]
    sums[...] = total * (1.0 / math.sqrt(128.0))
    for b in range(few):
        mine = errs[pl.ds(tab[ME, 0] * few + b, 1)]
        grads[b] = sums[pl.ds(b, 16, stride=few)] * mine

    def step(j, carry):
        live = tab[LIVE, j].astype(f32)
        weighted = split(ft[tab[FIRST, j]].astype(f32) * errs[...])
        mats[tab[SLOT, j]] = moved[j] - (rate * live) * dot_lhs(weighted, second[j], ATB)
        return carry

    lax.fori_loop(0, second.shape[0], step, 0, unroll=4)


def call(kernel, outs, n_in, scratch=(), smem=True):
    specs = [pl.BlockSpec(memory_space=pltpu.VMEM)] * n_in
    if smem:
        specs[0] = pl.BlockSpec(memory_space=pltpu.SMEM)
    out_specs = [pl.BlockSpec(memory_space=pltpu.VMEM)] * len(outs)
    return pl.pallas_call(
        kernel,
        out_shape=outs,
        in_specs=specs,
        out_specs=out_specs,
        scratch_shapes=list(scratch),
        compiler_params=pltpu.CompilerParams(vmem_limit_bytes=40 << 20),
    )


def shape(dims, dtype=f32):
    return jax.ShapeDtypeStruct(dims, dtype)


def swap(x, axes):
    return lax.all_to_all(x, axes, split_axis=0, concat_axis=0, tiled=True)


def chunk_of(values):
    padded = jnp.pad(values, (0, 256 - values.shape[0])).reshape(2, 1, 128)
    return jnp.broadcast_to(padded, (2, 4, 128)).reshape(8, 128)


def on_device(fields, labels, pair_first, pair_second, pair_count, pair_mats):
    groups, owners = lax.axis_size(GRP), lax.axis_size(OWN)
    n_x, n_z = lax.axis_size("x"), lax.axis_size("z")
    me = lax.axis_index(GRP)
    samples, per_block, feature = fields.shape
    slots = pair_first.shape[2]
    scale = logit_gain / math.sqrt(groups * owners * slots)
    rate = step_size * scale / (samples * feature)
    few = samples // owners

    table = pair_second[:, 0, :]
    blocks = table // per_block
    served = jnp.sum(jnp.where(blocks == me, table - me * per_block, 0), axis=1)
    mine = lax.dynamic_index_in_dim(blocks, me, 0, keepdims=False)
    picked = mine[:, None] == jnp.arange(slots, dtype=jnp.int32)[None, :]
    slot_ids = jnp.arange(slots, dtype=jnp.int32)[:, None]
    slot_of = jnp.sum(jnp.where(picked, slot_ids, 0), axis=0)
    first_of = jnp.sum(jnp.where(picked, (pair_first[0, 0] - me * per_block)[:, None], 0), axis=0)
    live = (slot_of < pair_count[0, 0]).astype(jnp.int32)
    where_am_i = jnp.full((slots,), lax.axis_index(OWN), jnp.int32)
    tab = jnp.stack([slot_of, first_of, live, served, where_am_i])

    ft = jnp.transpose(fields, (1, 0, 2))
    mats = pair_mats[0, 0]
    targets = chunk_of(labels.astype(f32))

    sent = call(gather_kernel, [shape((slots, samples, feature), bf16)], 2)(tab, ft)[0]
    second = swap(sent, GRP)
    acc = pltpu.VMEM((samples, 128), f32)
    part = call(partial_kernel, [shape((groups, 8, 128))], 4, [acc])(tab, ft, second, mats)[0]
    part = call(sum_kernel, [shape((owners, 8, 128))], 1, smem=False)(swap(part, GRP))[0]
    sums = swap(part, OWN)

    moved, out, dense = call(
        functools.partial(terms_kernel, scale, rate),
        [
            shape(mats.shape),
            shape((slots, samples + 8, feature)),
            shape((n_x, per_block * (samples // n_x) + 8, feature)),
        ],
        6,
        [acc, acc],
    )(tab, ft, second, mats, sums, targets)
    got = swap(out, GRP)
    dense = call(dense_kernel, [shape(dense.shape)], 3)(tab, got, dense)[0]
    got = swap(dense, "x")
    got = call(across_kernel, [shape((n_z, per_block * few + 8, feature))], 1, smem=False)(got)[0]
    got = swap(got, "z")
    logits, grads, mats = call(
        functools.partial(last_kernel, scale, rate),
        [shape((8, 128)), shape((few, per_block, feature)), shape(mats.shape)],
        6,
        [acc, pltpu.VMEM((per_block * few, 128), f32)],
    )(tab, ft, second, moved, got, targets)
    logits = jnp.concatenate([logits[0], logits[4, : samples - 128]])
    return logits, grads, mats[None, None]


def solution(mesh):
    n_grp, n_own = mesh.devices.shape
    sizes = (n_grp // 2, 2, 4, n_own // 4) if n_own % 12 == 0 else (n_grp // 2, 2, 2, n_own // 2)
    split_mesh = Mesh(mesh.devices.reshape(sizes), ("y", "core", "x", "z"))
    in_specs = (
        P(None, GRP, None),
        P(),
        P(GRP, OWN, None),
        P(None, OWN, None),
        P(GRP, OWN),
        P(GRP, OWN, None, None, None),
    )
    out_specs = (P(), P(OWN, GRP, None), P(GRP, OWN, None, None, None))
    return jax.shard_map(
        on_device, mesh=split_mesh, in_specs=in_specs, out_specs=out_specs, check_vma=False
    )
```

time: 758 us -> 186 us (0.25)
  waiting for transfers between devices: 462 us -> 14.5 us
  blocking collectives: 215 us -> 138 us
  matrix products: 21.5 us -> 0 us
  between operations: 14.9 us -> 1.39 us
  Pallas kernels: 0 us -> 13.1 us
  local copies, waits for them, and re-layouts: 11.6 us -> 1.4 us
    reduce_scatter x1 -> x0, waiting for transfers between devices: 407 us -> none  [on_device(): lax.psum_scatter(dense_grad, 'own', scatter_dimension=0, tiled=True)]
    psum x2 -> x0, blocking collectives: 215 us -> none  [logit_errors(): total_sum = lax.psum(partial_value, ('grp', 'own'))]
    all_to_all x0 -> x5, blocking collectives: none -> 138 us  [swap(): return lax.all_to_all(x, axes, split_axis=0, concat_axis=0, tiled=True)]
    all_to_all x2 -> x1, waiting for transfers between devices: 54.9 us -> 14.5 us  [swap(): return lax.all_to_all(x, axes, split_axis=0, concat_axis=0, tiled=True)]
    dot_general x7 -> x0, matrix products: 21.5 us -> none  [the longest x2 7.41 us: on_device(): jnp.einsum('bsk,bsl->skl', first_vec * errors[:, None, None], second_vec,...]
    pallas_call x0 -> x7, Pallas kernels: none -> 13.1 us  [the longest x1 5.61 us: on_device(): call(functools.partial(terms_kernel, scale, rate), [shape(mats.shape), sh...]
    gather x4 -> x0, local copies, waits for them, and re-layouts: 8.45 us -> none  [the longest x1 2.85 us: on_device(): outgoing = jnp.take(fields, served, axis=1)]
    all_to_all x2 -> x1, starting transfers between devices: 19.6 us -> 13.4 us  [swap(): return lax.all_to_all(x, axes, split_axis=0, concat_axis=0, tiled=True)]
  transfers between devices with their start and end apart: 3 -> 1, of which waited for: 3 -> 1; matrix products, arithmetic and copies ran while one was open for 1% -> 0% of each run, Pallas kernels for 0% -> 0%
where the time goes in v1:
time: 186 us; the launch traced here: 184 us
  blocking collectives  138 us (74%)
  waiting for transfers between devices  14.5 us (8%)
  starting transfers between devices  13.4 us (7%)
  Pallas kernels  13.1 us (7%)
  other arithmetic  2.14 us (1%)
    all_to_all x5, blocking collectives, swap(): return lax.all_to_all(x, axes, split_axis=0, concat_axis=0, tiled=True)  138 us
    all_to_all x1, waiting for transfers between devices, swap(): return lax.all_to_all(x, axes, split_axis=0, concat_axis=0, tiled=True)  14.5 us
    all_to_all x1, starting transfers between devices, swap(): return lax.all_to_all(x, axes, split_axis=0, concat_axis=0, tiled=True)  13.4 us
    pallas_call x1, Pallas kernels, on_device(): call(functools.partial(terms_kernel, scale, rate), [shape(mats.shape), sh...  5.61 us
  transfers between devices with their start and end apart: 1, of which 1 were waited for; matrix products, arithmetic and copies ran while one was open for 0% of the time, Pallas kernels for 0%

profile of v1, /device:TPU:1, one launch (start us, length us, event | category | flops | bytes accessed | tf_op | source)
XLA Modules:
  0.0 183.8 jit_solution(1075912401558683417)
XLA Ops:
  1.3 0.7 subtract_bitcast_fusion
  2.0 0.8 select_reduce_fusion
  2.8 1.3 copy.11
  4.1 0.1 select_reduce_fusion.1
  4.2 0.0 copy-start
  4.3 0.8 shard_map.85
  5.1 36.1 %all_to_all.30.second = bf16[16,192,128]{2,1,0:T(8,128)(2,1)S(1)} all-to-all(bf16[16,192,128]{2,1,0:T(8,128)(2,1)S(1)} %shard_map.85), channel_id=1, replica_groups=mesh['y'=8,'core'=2,'x'=4,'z'=12] {'y','core'}, dimensions={0} | all-to-all | bytes 1572864 | tf_op jit(solution)/shard_map/all_to_all | solution.py:208
  41.2 0.0 copy-done
  41.2 0.0 copy-start.1
  41.2 1.9 %shard_map.86 = f32[16,8,128]{2,1,0:T(8,128)S(1)} custom-call(s32[5,16]{1,0:T(8,128)S(1)} %stack.16.tab, bf16[16,192,128]{2,1,0:T(8,128)(2,1)S(1)} %bitcast.24, bf16[16,192,128]{2,1,0:T(8,128)(2,1)S(1)} %all_to_all.30.second, f32[16,128,128]{2,1,0:T(8,128)S(1)} %bitcast.27), custom_call_target="tpu_custom_call" | custom-call | tf_op jit(solution)/shard_map/pallas_call | solution.py:245
  43.1 10.4 %all_to_all.31.parts = f32[16,8,128]{2,1,0:T(8,128)S(1)} all-to-all(f32[16,8,128]{2,1,0:T(8,128)S(1)} %shard_map.86), channel_id=1, replica_groups=mesh['y'=8,'core'=2,'x'=4,'z'=12] {'y','core'}, dimensions={0} | all-to-all | bytes 131072 | tf_op jit(solution)/shard_map/all_to_all | solution.py:208
  53.4 0.7 shard_map.87
  54.1 13.4 %all-to-all-start.2 = ((f32[48,8,128]{2,1,0:T(8,128)}), f32[48,8,128]{2,1,0:T(8,128)S(1)}, u32[]{:S(2)}, u32[]{:S(2)}) async-start(f32[48,8,128]{2,1,0:T(8,128)} %shard_map.87), calls=%async_computation.2 | async-start | bytes 393216 | tf_op jit(solution)/shard_map/all_to_all | solution.py:208
  67.6 0.0 copy-done.1
  67.6 14.5 %all-to-all-done.2.sums = f32[48,8,128]{2,1,0:T(8,128)S(1)} async-done(((f32[48,8,128]{2,1,0:T(8,128)}), f32[48,8,128]{2,1,0:T(8,128)S(1)}, u32[]{:S(2)}, u32[]{:S(2)}) %all-to-all-start.2) | async-done | bytes 196640 | tf_op jit(solution)/shard_map/all_to_all | solution.py:208
  82.2 5.6 %shard_map.88 = (f32[16,128,128]{2,1,0:T(8,128)S(1)}, f32[16,200,128]{2,1,0:T(8,128)S(1)}, f32[4,776,128]{2,1,0:T(8,128)S(1)}) custom-call(s32[5,16]{1,0:T(8,128)S(1)} %stack.16.tab, bf16[16,192,128]{2,1,0:T(8,128)(2,1)S(1)} %bitcast.25, bf16[16,192,128]{2,1,0:T(8,128)(2,1)S(1)} %all_to_all.30.second, f32[16,128,128]{2,1,0:T(8,128)S(1)} %bitcast.28, ...), custom_call_target="tpu_custom_call" | custom-call | tf_op jit(solution)/shard_map/pallas_call | solution.py:249
  87.8 46.2 %all_to_all.32.got = f32[16,200,128]{2,1,0:T(8,128)S(1)} all-to-all(f32[16,200,128]{2,1,0:T(8,128)S(1)} %get-tuple-element.10), channel_id=1, replica_groups=mesh['y'=8,'core'=2,'x'=4,'z'=12] {'y','core'}, dimensions={0} | all-to-all | bytes 3276800 | tf_op jit(solution)/shard_map/all_to_all | solution.py:208
  133.9 1.0 shard_map.89
  134.9 23.2 %all_to_all.33.got = f32[4,776,128]{2,1,0:T(8,128)S(1)} all-to-all(f32[4,776,128]{2,1,0:T(8,128)S(1)} %shard_map.89), channel_id=1, replica_groups=mesh['y'=8,'core'=2,'x'=4,'z'=12] {'x'}, dimensions={0} | all-to-all | bytes 3178496 | tf_op jit(solution)/shard_map/all_to_all | solution.py:208
  158.1 0.1 shard_map.90
  158.2 21.9 %all_to_all.34.got = f32[12,72,128]{2,1,0:T(8,128)S(1)} all-to-all(f32[12,72,128]{2,1,0:T(8,128)S(1)} %shard_map.90), channel_id=1, replica_groups=mesh['y'=8,'core'=2,'x'=4,'z'=12] {'z'}, dimensions={0} | all-to-all | bytes 884736 | tf_op jit(solution)/shard_map/all_to_all | solution.py:208
  180.1 3.1 %shard_map.91 = (f32[8,128]{1,0:T(8,128)S(1)}, f32[4,16,128]{2,1,0:T(8,128)}, f32[16,128,128]{2,1,0:T(8,128)}) custom-call(s32[5,16]{1,0:T(8,128)S(1)} %stack.16.tab, bf16[16,192,128]{2,1,0:T(8,128)(2,1)S(1)} %bitcast.26, bf16[16,192,128]{2,1,0:T(8,128)(2,1)S(1)} %all_to_all.30.second, f32[16,128,128]{2,1,0:T(8,128)S(1)} %get-tuple-element.9.moved, ...), custom_call_target="tpu_custom_call" | custom-call | tf_op jit(solution)/shard_map/pallas_call | solution.py:264
  183.2 0.6 pad_maximum_fusion
  (9 shorter events, 0.1 us)
Async XLA Ops:
  4.2 36.9 %copy-start = (f32[1,1,16,128,128]{4,3,2,1,0:T(8,128)S(1)}, f32[1,1,16,128,128]{4,3,2,1,0:T(8,128)}, u32[]{:S(2)}) copy-start(f32[1,1,16,128,128]{4,3,2,1,0:T(8,128)} %param.11) | copy-start | bytes 3145732
  41.2 26.4 %copy-start.1 = (s32[192]{0:T(256)S(1)}, s32[192]{0:T(256)}, u32[]{:S(2)}) copy-start(s32[192]{0:T(256)} %param.7) | copy-start | bytes 2308
  54.1 28.0 %all-to-all-start.2 = ((f32[48,8,128]{2,1,0:T(8,128)}), f32[48,8,128]{2,1,0:T(8,128)S(1)}, u32[]{:S(2)}, u32[]{:S(2)}) async-start(f32[48,8,128]{2,1,0:T(8,128)} %shard_map.87), calls=%async_computation.2 | async-start | bytes 393216 | tf_op jit(solution)/shard_map/all_to_all | solution.py:208

commit v2 on v1

--- a/solution.py
+++ b/solution.py
@@ -96,8 +96,67 @@
     return total
 
 
+LEVELS = 32000.0
+OCTAVE = 64.0
+
+
+def exponent(peak):
+    return jnp.ceil(OCTAVE * jnp.log2(jnp.maximum(peak, 1e-30)))
+
+
+def scale_of(k):
+    return jnp.exp2(k * (1.0 / OCTAVE))
+
+
+def whole(x):
+    return jnp.round(x).astype(jnp.int32).astype(jnp.int16)
+
+
+def real(x):
+    return x.astype(jnp.int32).astype(f32)
+
+
+def peaks(x):
+    return jnp.max(jnp.abs(x), axis=1, keepdims=True)
+
+
+def iota(dims, axis):
+    return lax.broadcasted_iota(jnp.int32, dims, axis)
+
+
+def rows_of(named):
+    rows = iota((16, 128), 0)
+    out = jnp.zeros((16, 128), f32)
+    for r, value in named.items():
+        out = jnp.where(rows == r, value, out)
+    return out
+
+
+def digits(low, high, at):
+    k = exponent(jnp.maximum(peaks(low), peaks(high)))
+    up = LEVELS * scale_of(-k)
+    a, b = low * up, high * up
+    named = {at: jnp.round(a), at + 1: jnp.round(b)}
+    named[at + 2] = (a - named[at]) * LEVELS
+    named[at + 3] = (b - named[at + 1]) * LEVELS
+    named[at + 4] = jnp.broadcast_to(k, (1, 128))
+    return named
+
+
+def undigit(tile, at):
+    s = scale_of(tile[at + 4 : at + 5]) * (1.0 / LEVELS)
+    low = s * (tile[at : at + 1] + tile[at + 2 : at + 3] * (1.0 / LEVELS))
+    high = s * (tile[at + 1 : at + 2] + tile[at + 3 : at + 4] * (1.0 / LEVELS))
+    return low, high
+
+
+def upright(rows, height):
+    tall = jnp.concatenate(rows + [jnp.zeros((128 - len(rows), 128), f32)], axis=0)
+    return jnp.transpose(tall)[:height]
+
+
 def terms_kernel(
-    scale, rate, tab, ft, second, mats, sums, labels, moved, out, dense, acc, errs
+    scale, rate, tab, ft, second, mats, sums, labels, moved, out, dense, acc, errs, stash, tops
 ):
     samples = second.shape[1]
     n_x, rows = dense.shape[0], samples // dense.shape[0]
@@ -105,6 +164,8 @@
     errs[...] = spread(errors, samples)
     acc[...] = jnp.zeros_like(acc)
     dense[...] = jnp.zeros_like(dense)
+    tops[...] = jnp.zeros_like(tops)
+    lanes = iota((samples, 128), 1)
 
     def step(j, carry):
         live = tab[LIVE, j].astype(f32)
@@ -116,7 +177,8 @@
         pair = split(updated * live)
         mixed = dot_rhs(va, pair, AB)
         acc[...] += mixed * vb.astype(f32)
-        out[j, 0:samples] = mixed
+        stash[j] = mixed
+        tops[...] = jnp.where(lanes == j, peaks(mixed), tops[...])
         toward = dot_rhs(vb, pair, ABT)
         at = pl.ds(pl.multiple_of(first * rows, 8), rows)
         for i in range(n_x):
@@ -124,40 +186,100 @@
         return carry
 
     lax.fori_loop(0, second.shape[0], step, 0, unroll=2)
+    k = exponent(tops[...])
+    up = LEVELS * scale_of(-k)
+    low = jnp.transpose(k[:128])
+    high = jnp.transpose(
+        jnp.concatenate([k[128:], jnp.zeros((256 - samples, 128), f32)], axis=0)
+    )
     chunk = row_sums(acc[...] * (1.0 / 128.0))
-    for i in range(out.shape[0]):
-        out[i, samples : samples + 8] = chunk
-
-
-def dense_kernel(tab, got, dense_in, dense):
+    tile = rows_of(digits(chunk[0:1], chunk[4:5], 0))
+    rows = iota((16, 128), 0)
+    for j in range(out.shape[0]):
+        out[j, 0:samples] = whole(stash[j] * up[:, j : j + 1])
+        mine = jnp.where(rows == 6, high[j : j + 1], tile)
+        out[j, samples : samples + 16] = whole(jnp.where(rows == 5, low[j : j + 1], mine))
+
+
+def dense_kernel(tab, got, dense_in, out, dense):
+    samples = got.shape[1] - 16
+    n_x, rows = dense.shape[0], samples // dense.shape[0]
+    size = dense.shape[1]
+    parts = size // 128
+    tiles = [real(got[j, samples : samples + 16]) for j in range(got.shape[0])]
+    low = upright([t[5:6] for t in tiles], 128)
+    high = upright([t[6:7] for t in tiles], samples - 128)
+    down = scale_of(jnp.concatenate([low, high], axis=0)) * (1.0 / LEVELS)
     dense[...] = dense_in[...]
-    samples = got.shape[1] - 8
-    n_x, rows = dense.shape[0], samples // dense.shape[0]
-    last = dense.shape[1] - 8
-
-    @pl.loop(0, got.shape[0])
-    def _(j):
+    sums = [undigit(t, 0) for t in tiles]
+    total = sums[0]
+    for j in range(got.shape[0]):
         at = pl.ds(pl.multiple_of(tab[SERVED, j] * rows, 8), rows)
+        value = real(got[j, 0:samples]) * down[:, j : j + 1]
         for i in range(n_x):
-            dense[i, at] += got[j, i * rows : (i + 1) * rows]
-
-    chunk = total_of(got, samples)
+            dense[i, at] += value[i * rows : (i + 1) * rows]
+        if j:
+            total = (total[0] + sums[j][0], total[1] + sums[j][1])
+
+    lanes = iota((128, 128), 1)
+    tops = jnp.zeros((128, 128), f32)
     for i in range(n_x):
-        dense[i, last : last + 8] = chunk
-
-
-def across_kernel(got, out):
-    n_z, few = out.shape[0], (out.shape[1] - 8) // 16
+        for t in range(parts):
+            top = peaks(dense[i, t * 128 : (t + 1) * 128])
+            tops = jnp.where(lanes == i * parts + t, top, tops)
+    k = exponent(tops)
+    up = LEVELS * scale_of(-k)
+    lying = jnp.transpose(k)
+    common = digits(total[0], total[1], parts)
+    for i in range(n_x):
+        named = dict(common)
+        for t in range(parts):
+            lane = i * parts + t
+            part = dense[i, t * 128 : (t + 1) * 128]
+            out[i, t * 128 : (t + 1) * 128] = whole(part * up[:, lane : lane + 1])
+            named[t] = lying[lane : lane + 1]
+        out[i, size : size + 16] = whole(rows_of(named))
+
+
+def across_kernel(got, out, sums, parted):
+    n_z, wide = out.shape[0], out.shape[1] - 16
+    few = wide // 16
     rows = n_z * few
+    size = 16 * rows
+    parts = size // 128
+    tiles = [real(got[i, size : size + 16]) for i in range(got.shape[0])]
+    exps = upright([t[r : r + 1] for t in tiles for r in range(parts)], 128)
+    down = scale_of(exps) * (1.0 / LEVELS)
+    for t in range(parts):
+        total = real(got[0, t * 128 : (t + 1) * 128]) * down[:, t : t + 1]
+        for i in range(1, got.shape[0]):
+            lane = i * parts + t
+            total = total + real(got[i, t * 128 : (t + 1) * 128]) * down[:, lane : lane + 1]
+        sums[t * 128 : (t + 1) * 128] = total
+    pair = undigit(tiles[0], parts)
+    for t in tiles[1:]:
+        more = undigit(t, parts)
+        pair = (pair[0] + more[0], pair[1] + more[1])
     for f in range(16):
-        total = got[0, f * rows : (f + 1) * rows]
-        for i in range(1, got.shape[0]):
-            total = total + got[i, f * rows : (f + 1) * rows]
-        for k in range(n_z):
-            out[k, f * few : (f + 1) * few] = total[k * few : (k + 1) * few]
-    chunk = total_of(got, 16 * rows)
-    for k in range(n_z):
-        out[k, 16 * few :] = chunk
+        for z in range(n_z):
+            start = f * rows + z * few
+            parted[z, f * few : (f + 1) * few] = sums[start : start + few]
+    lanes = iota((wide, 128), 1)
+    tops = jnp.zeros((wide, 128), f32)
+    for z in range(n_z):
+        tops = jnp.where(lanes == z, peaks(parted[z]), tops)
+    k = exponent(tops)
+    up = LEVELS * scale_of(-k)
+    if wide < 128:
+        k = jnp.concatenate([k, jnp.zeros((128 - wide, 128), f32)], axis=0)
+    lying = [jnp.transpose(k[n * 128 : (n + 1) * 128]) for n in range(k.shape[0] // 128)]
+    common = digits(pair[0], pair[1], len(lying))
+    for z in range(n_z):
+        out[z, 0:wide] = whole(parted[z] * up[:, z : z + 1])
+        named = dict(common)
+        for n, part in enumerate(lying):
+            named[n] = part[z : z + 1]
+        out[z, wide : wide + 16] = whole(rows_of(named))
 
 
 def last_kernel(
@@ -165,12 +287,21 @@
 ):
     samples = second.shape[1]
     few = grads.shape[0]
-    value = scale * total_of(got, 16 * few)
+    wide = 16 * few
+    tiles = [real(got[i, wide : wide + 16]) for i in range(got.shape[0])]
+    high = -(-wide // 128)
+    exps = [upright([t[n : n + 1] for t in tiles], min(wide, 128)) for n in range(high)]
+    down = scale_of(jnp.concatenate(exps, axis=0)) * (1.0 / LEVELS)
+    pair = undigit(tiles[0], high)
+    for t in tiles[1:]:
+        more = undigit(t, high)
+        pair = (pair[0] + more[0], pair[1] + more[1])
+    value = scale * jnp.where(iota((8, 128), 0) < 4, pair[0], pair[1])
     logits[...] = value
     errs[...] = spread(jax.nn.sigmoid(value) - labels[...], samples)
-    total = got[0, : 16 * few]
+    total = real(got[0, 0:wide]) * down[:, 0:1]
     for i in range(1, got.shape[0]):
-        total = total + got[i, : 16 * few]
+        total = total + real(got[i, 0:wide]) * down[:, i : i + 1]
     sums[...] = total * (1.0 / math.sqrt(128.0))
     for b in range(few):
         mine = errs[pl.ds(tab[ME, 0] * few + b, 1)]
@@ -246,20 +377,24 @@
     part = call(sum_kernel, [shape((owners, 8, 128))], 1, smem=False)(swap(part, GRP))[0]
     sums = swap(part, OWN)
 
+    size, wide = per_block * (samples // n_x), per_block * few
     moved, out, dense = call(
         functools.partial(terms_kernel, scale, rate),
         [
             shape(mats.shape),
-            shape((slots, samples + 8, feature)),
-            shape((n_x, per_block * (samples // n_x) + 8, feature)),
+            shape((slots, samples + 16, feature), jnp.int16),
+            shape((n_x, size, feature)),
         ],
         6,
-        [acc, acc],
+        [acc, acc, pltpu.VMEM((slots, samples, feature), f32), acc],
     )(tab, ft, second, mats, sums, targets)
     got = swap(out, GRP)
-    dense = call(dense_kernel, [shape(dense.shape)], 3)(tab, got, dense)[0]
-    got = swap(dense, "x")
-    got = call(across_kernel, [shape((n_z, per_block * few + 8, feature))], 1, smem=False)(got)[0]
+    out = [shape((n_x, size + 16, feature), jnp.int16)]
+    got = call(dense_kernel, out, 3, [pltpu.VMEM((n_x, size, feature), f32)])(tab, got, dense)[0]
+    got = swap(got, "x")
+    out = [shape((n_z, wide + 16, feature), jnp.int16)]
+    room = [pltpu.VMEM((size, feature), f32), pltpu.VMEM((n_z, wide, feature), f32)]
+    got = call(across_kernel, out, 1, room, smem=False)(got)[0]
     got = swap(got, "z")
     logits, grads, mats = call(
         functools.partial(last_kernel, scale, rate),
@@ -273,7 +408,7 @@
 
 def solution(mesh):
     n_grp, n_own = mesh.devices.shape
-    sizes = (n_grp // 2, 2, 4, n_own // 4) if n_own % 12 == 0 else (n_grp // 2, 2, 2, n_own // 2)
+    sizes = (n_grp // 2, 2, 4, n_own // 4)
     split_mesh = Mesh(mesh.devices.reshape(sizes), ("y", "core", "x", "z"))
     in_specs = (
         P(None, GRP, None),

time: 186 us -> 158 us (0.85)
  blocking collectives: 138 us -> 108 us
  Pallas kernels: 13.1 us -> 16.7 us
    all_to_all x5, blocking collectives: 138 us -> 108 us  [swap(): return lax.all_to_all(x, axes, split_axis=0, concat_axis=0, tiled=True)]
    pallas_call x2, Pallas kernels: 1.03 us -> 3.56 us  [the longest x1 2.45 us: on_device(): call(dense_kernel, out, 3, [pltpu.VMEM((n_x, size, feature), f32)])]
where the time goes in v2:
time: 158 us
  blocking collectives  108 us (68%)
  Pallas kernels  16.7 us (11%)
  waiting for transfers between devices  14.5 us (9%)
  starting transfers between devices  13.4 us (8%)
  other arithmetic  2.14 us (1%)
    all_to_all x5, blocking collectives, swap(): return lax.all_to_all(x, axes, split_axis=0, concat_axis=0, tiled=True)  108 us
    all_to_all x1, waiting for transfers between devices, swap(): return lax.all_to_all(x, axes, split_axis=0, concat_axis=0, tiled=True)  14.5 us
    all_to_all x1, starting transfers between devices, swap(): return lax.all_to_all(x, axes, split_axis=0, concat_axis=0, tiled=True)  13.4 us
    pallas_call x1, Pallas kernels, on_device(): call(functools.partial(terms_kernel, scale, rate), [shape(mats.shape), sh...  6.43 us
    pallas_call x1, Pallas kernels, on_device(): call(functools.partial(last_kernel, scale, rate), [shape((8, 128)), shape...  3.38 us
  transfers between devices with their start and end apart: 1, of which 1 were waited for; matrix products, arithmetic and copies ran while one was open for 0% of the time, Pallas kernels for 0%

profile of v2, /device:TPU:1, one launch (start us, length us, event | category | flops | bytes accessed | tf_op | source)
XLA Modules:
  0.0 157.6 jit_solution(5988719221630361320)
XLA Ops:
  1.3 0.7 subtract_bitcast_fusion
  2.0 0.8 select_reduce_fusion
  2.8 1.3 copy.11
  4.1 0.1 select_reduce_fusion.1
  4.3 0.0 copy-start
  4.3 0.8 shard_map.85
  5.1 36.1 %all_to_all.30.second = bf16[16,192,128]{2,1,0:T(8,128)(2,1)S(1)} all-to-all(bf16[16,192,128]{2,1,0:T(8,128)(2,1)S(1)} %shard_map.85), channel_id=1, replica_groups=mesh['y'=8,'core'=2,'x'=4,'z'=12] {'y','core'}, dimensions={0} | all-to-all | bytes 1572864 | tf_op jit(solution)/shard_map/all_to_all | solution.py:339
  41.2 0.0 copy-done
  41.2 0.0 copy-start.1
  41.2 1.9 %shard_map.86 = f32[16,8,128]{2,1,0:T(8,128)S(1)} custom-call(s32[5,16]{1,0:T(8,128)S(1)} %stack.16.tab, bf16[16,192,128]{2,1,0:T(8,128)(2,1)S(1)} %bitcast.24, bf16[16,192,128]{2,1,0:T(8,128)(2,1)S(1)} %all_to_all.30.second, f32[16,128,128]{2,1,0:T(8,128)S(1)} %bitcast.27), custom_call_target="tpu_custom_call" | custom-call | tf_op jit(solution)/shard_map/pallas_call | solution.py:376
  43.1 10.4 %all_to_all.31.parts = f32[16,8,128]{2,1,0:T(8,128)S(1)} all-to-all(f32[16,8,128]{2,1,0:T(8,128)S(1)} %shard_map.86), channel_id=1, replica_groups=mesh['y'=8,'core'=2,'x'=4,'z'=12] {'y','core'}, dimensions={0} | all-to-all | bytes 131072 | tf_op jit(solution)/shard_map/all_to_all | solution.py:339
  53.4 0.7 shard_map.87
  54.1 13.4 %all-to-all-start.2 = ((f32[48,8,128]{2,1,0:T(8,128)}), f32[48,8,128]{2,1,0:T(8,128)S(1)}, u32[]{:S(2)}, u32[]{:S(2)}) async-start(f32[48,8,128]{2,1,0:T(8,128)} %shard_map.87), calls=%async_computation.2 | async-start | bytes 393216 | tf_op jit(solution)/shard_map/all_to_all | solution.py:339
  67.6 0.0 copy-done.1
  67.6 14.5 %all-to-all-done.2.sums = f32[48,8,128]{2,1,0:T(8,128)S(1)} async-done(((f32[48,8,128]{2,1,0:T(8,128)}), f32[48,8,128]{2,1,0:T(8,128)S(1)}, u32[]{:S(2)}, u32[]{:S(2)}) %all-to-all-start.2) | async-done | bytes 196640 | tf_op jit(solution)/shard_map/all_to_all | solution.py:339
  82.2 6.4 %shard_map.88 = (f32[16,128,128]{2,1,0:T(8,128)S(1)}, s16[16,208,128]{2,1,0:T(8,128)(2,1)S(1)}, f32[4,768,128]{2,1,0:T(8,128)S(1)}) custom-call(s32[5,16]{1,0:T(8,128)S(1)} %stack.16.tab, bf16[16,192,128]{2,1,0:T(8,128)(2,1)S(1)} %bitcast.25, bf16[16,192,128]{2,1,0:T(8,128)(2,1)S(1)} %all_to_all.30.second, f32[16,128,128]{2,1,0:T(8,128)S(1)} %bitcast.28, ...), custom_call_target="tpu_custom_call" | custom-call | tf_op jit(solution)/shard_map/pallas_call | solution.py:381
  88.6 29.1 %all_to_all.32.got = s16[16,208,128]{2,1,0:T(8,128)(2,1)S(1)} all-to-all(s16[16,208,128]{2,1,0:T(8,128)(2,1)S(1)} %get-tuple-element.10), channel_id=1, replica_groups=mesh['y'=8,'core'=2,'x'=4,'z'=12] {'y','core'}, dimensions={0} | all-to-all | bytes 1703936 | tf_op jit(solution)/shard_map/all_to_all | solution.py:339
  117.7 2.5 %shard_map.89 = s16[4,784,128]{2,1,0:T(8,128)(2,1)S(1)} custom-call(s32[5,16]{1,0:T(8,128)S(1)} %stack.16.tab, s16[16,208,128]{2,1,0:T(8,128)(2,1)S(1)} %all_to_all.32.got, f32[4,768,128]{2,1,0:T(8,128)S(1)} %get-tuple-element.11.dense_in), custom_call_target="tpu_custom_call" | custom-call | tf_op jit(solution)/shard_map/pallas_call | solution.py:393
  120.1 15.4 %all_to_all.33.got = s16[4,784,128]{2,1,0:T(8,128)(2,1)S(1)} all-to-all(s16[4,784,128]{2,1,0:T(8,128)(2,1)S(1)} %shard_map.89), channel_id=1, replica_groups=mesh['y'=8,'core'=2,'x'=4,'z'=12] {'x'}, dimensions={0} | all-to-all | bytes 1605632 | tf_op jit(solution)/shard_map/all_to_all | solution.py:339
  135.5 1.1 shard_map.90
  136.6 17.0 %all_to_all.34.got = s16[12,80,128]{2,1,0:T(8,128)(2,1)S(1)} all-to-all(s16[12,80,128]{2,1,0:T(8,128)(2,1)S(1)} %shard_map.90), channel_id=1, replica_groups=mesh['y'=8,'core'=2,'x'=4,'z'=12] {'z'}, dimensions={0} | all-to-all | bytes 491520 | tf_op jit(solution)/shard_map/all_to_all | solution.py:339
  153.7 3.4 %shard_map.91 = (f32[8,128]{1,0:T(8,128)S(1)}, f32[4,16,128]{2,1,0:T(8,128)}, f32[16,128,128]{2,1,0:T(8,128)}) custom-call(s32[5,16]{1,0:T(8,128)S(1)} %stack.16.tab, bf16[16,192,128]{2,1,0:T(8,128)(2,1)S(1)} %bitcast.26, bf16[16,192,128]{2,1,0:T(8,128)(2,1)S(1)} %all_to_all.30.second, f32[16,128,128]{2,1,0:T(8,128)S(1)} %get-tuple-element.9.moved, ...), custom_call_target="tpu_custom_call" | custom-call | tf_op jit(solution)/shard_map/pallas_call | solution.py:399
  157.1 0.6 pad_maximum_fusion
  (9 shorter events, 0.1 us)
Async XLA Ops:
  4.3 36.9 %copy-start = (f32[1,1,16,128,128]{4,3,2,1,0:T(8,128)S(1)}, f32[1,1,16,128,128]{4,3,2,1,0:T(8,128)}, u32[]{:S(2)}) copy-start(f32[1,1,16,128,128]{4,3,2,1,0:T(8,128)} %param.11) | copy-start | bytes 3145732
  41.2 26.4 %copy-start.1 = (s32[192]{0:T(256)S(1)}, s32[192]{0:T(256)}, u32[]{:S(2)}) copy-start(s32[192]{0:T(256)} %param.7) | copy-start | bytes 2308
  54.1 28.0 %all-to-all-start.2 = ((f32[48,8,128]{2,1,0:T(8,128)}), f32[48,8,128]{2,1,0:T(8,128)S(1)}, u32[]{:S(2)}, u32[]{:S(2)}) async-start(f32[48,8,128]{2,1,0:T(8,128)} %shard_map.87), calls=%async_computation.2 | async-start | bytes 393216 | tf_op jit(solution)/shard_map/all_to_all | solution.py:339

commit v3 on v2

--- a/solution.py
+++ b/solution.py
@@ -50,13 +50,12 @@
     low = exact(ones, acc[:128])
     rest = acc[128:]
     high = exact(ones, jnp.concatenate([rest, jnp.zeros((256 - acc.shape[0], 128), f32)], axis=0))
-    rows = lax.broadcasted_iota(jnp.int32, (8, 128), 0)
-    return jnp.where(rows < 4, low, high)
+    return jnp.concatenate([low[0:1], high[0:1]], axis=0)
 
 
 def spread(chunk, samples):
     low = jnp.transpose(jnp.broadcast_to(chunk[0:1], (128, 128)))
-    high = jnp.transpose(jnp.broadcast_to(chunk[4:5], (128, 128)))
+    high = jnp.transpose(jnp.broadcast_to(chunk[1:2], (128, 128)))
     return jnp.concatenate([low, high[: samples - 128]], axis=0)
 
 
@@ -82,17 +81,15 @@
 
 
 def sum_kernel(parts, out):
+    total = total_of(parts)
+    for i in range(out.shape[0]):
+        out[i] = total
+
+
+def total_of(parts):
     total = parts[0]
     for i in range(1, parts.shape[0]):
         total = total + parts[i]
-    for i in range(out.shape[0]):
-        out[i] = total
-
-
-def total_of(parts, lo):
-    total = parts[0, lo : lo + 8]
-    for i in range(1, parts.shape[0]):
-        total = total + parts[i, lo : lo + 8]
     return total
 
 
@@ -160,7 +157,7 @@
 ):
     samples = second.shape[1]
     n_x, rows = dense.shape[0], samples // dense.shape[0]
-    errors = jax.nn.sigmoid(scale * total_of(sums, 0)) - labels[...]
+    errors = jax.nn.sigmoid(scale * total_of(sums)) - labels[...]
     errs[...] = spread(errors, samples)
     acc[...] = jnp.zeros_like(acc)
     dense[...] = jnp.zeros_like(dense)
@@ -193,7 +190,7 @@
         jnp.concatenate([k[128:], jnp.zeros((256 - samples, 128), f32)], axis=0)
     )
     chunk = row_sums(acc[...] * (1.0 / 128.0))
-    tile = rows_of(digits(chunk[0:1], chunk[4:5], 0))
+    tile = rows_of(digits(chunk[0:1], chunk[1:2], 0))
     rows = iota((16, 128), 0)
     for j in range(out.shape[0]):
         out[j, 0:samples] = whole(stash[j] * up[:, j : j + 1])
@@ -296,7 +293,7 @@
     for t in tiles[1:]:
         more = undigit(t, high)
         pair = (pair[0] + more[0], pair[1] + more[1])
-    value = scale * jnp.where(iota((8, 128), 0) < 4, pair[0], pair[1])
+    value = scale * jnp.concatenate(pair, axis=0)
     logits[...] = value
     errs[...] = spread(jax.nn.sigmoid(value) - labels[...], samples)
     total = real(got[0, 0:wide]) * down[:, 0:1]
@@ -339,11 +336,6 @@
     return lax.all_to_all(x, axes, split_axis=0, concat_axis=0, tiled=True)
 
 
-def chunk_of(values):
-    padded = jnp.pad(values, (0, 256 - values.shape[0])).reshape(2, 1, 128)
-    return jnp.broadcast_to(padded, (2, 4, 128)).reshape(8, 128)
-
-
 def on_device(fields, labels, pair_first, pair_second, pair_count, pair_mats):
     groups, owners = lax.axis_size(GRP), lax.axis_size(OWN)
     n_x, n_z = lax.axis_size("x"), lax.axis_size("z")
@@ -368,14 +360,14 @@
 
     ft = jnp.transpose(fields, (1, 0, 2))
     mats = pair_mats[0, 0]
-    targets = chunk_of(labels.astype(f32))
+    targets = jnp.pad(labels.astype(f32), (0, 256 - samples)).reshape(2, 128)
 
     sent = call(gather_kernel, [shape((slots, samples, feature), bf16)], 2)(tab, ft)[0]
     second = swap(sent, GRP)
     acc = pltpu.VMEM((samples, 128), f32)
-    part = call(partial_kernel, [shape((groups, 8, 128))], 4, [acc])(tab, ft, second, mats)[0]
-    part = call(sum_kernel, [shape((owners, 8, 128))], 1, smem=False)(swap(part, GRP))[0]
-    sums = swap(part, OWN)
+    part = call(partial_kernel, [shape((groups * n_x, 2, 128))], 4, [acc])(tab, ft, second, mats)[0]
+    part = call(sum_kernel, [shape((n_z, 2, 128))], 1, smem=False)(swap(part, GRP + ("x",)))[0]
+    sums = swap(part, "z")
 
     size, wide = per_block * (samples // n_x), per_block * few
     moved, out, dense = call(
@@ -398,12 +390,11 @@
     got = swap(got, "z")
     logits, grads, mats = call(
         functools.partial(last_kernel, scale, rate),
-        [shape((8, 128)), shape((few, per_block, feature)), shape(mats.shape)],
+        [shape((2, 128)), shape((few, per_block, feature)), shape(mats.shape)],
         6,
         [acc, pltpu.VMEM((per_block * few, 128), f32)],
     )(tab, ft, second, moved, got, targets)
-    logits = jnp.concatenate([logits[0], logits[4, : samples - 128]])
-    return logits, grads, mats[None, None]
+    return logits.reshape(256)[:samples], grads, mats[None, None]
 
 
 def solution(mesh):

time: 158 us -> 154 us (0.975)
  blocking collectives: 108 us -> 97.6 us
  starting transfers between devices: 13.4 us -> 16.8 us
  waiting for transfers between devices: 14.5 us -> 17.5 us
    all_to_all x5 -> x4, blocking collectives: 108 us -> 97.6 us  [swap(): return lax.all_to_all(x, axes, split_axis=0, concat_axis=0, tiled=True)]
    all_to_all x1 -> x2, starting transfers between devices: 13.4 us -> 16.8 us  [swap(): return lax.all_to_all(x, axes, split_axis=0, concat_axis=0, tiled=True)]
    all_to_all x1 -> x2, waiting for transfers between devices: 14.5 us -> 17.5 us  [swap(): return lax.all_to_all(x, axes, split_axis=0, concat_axis=0, tiled=True)]
  transfers between devices with their start and end apart: 1 -> 2, of which waited for: 1 -> 2; matrix products, arithmetic and copies ran while one was open for 0% -> 0% of each run, Pallas kernels for 0% -> 0%
where the time goes in v3:
time: 154 us
  blocking collectives  97.6 us (63%)
  waiting for transfers between devices  17.5 us (11%)
  Pallas kernels  17.4 us (11%)
  starting transfers between devices  16.8 us (11%)
  other arithmetic  1.57 us (1%)
    all_to_all x4, blocking collectives, swap(): return lax.all_to_all(x, axes, split_axis=0, concat_axis=0, tiled=True)  97.6 us
    all_to_all x2, waiting for transfers between devices, swap(): return lax.all_to_all(x, axes, split_axis=0, concat_axis=0, tiled=True)  17.5 us
    all_to_all x2, starting transfers between devices, swap(): return lax.all_to_all(x, axes, split_axis=0, concat_axis=0, tiled=True)  16.8 us
    pallas_call x1, Pallas kernels, on_device(): call(functools.partial(terms_kernel, scale, rate), [shape(mats.shape), sh...  6.39 us
    pallas_call x1, Pallas kernels, on_device(): call(functools.partial(last_kernel, scale, rate), [shape((2, 128)), shape...  3.38 us
  transfers between devices with their start and end apart: 2, of which 2 were waited for; matrix products, arithmetic and copies ran while one was open for 0% of the time, Pallas kernels for 0%

profile of v3, /device:TPU:1, one launch (start us, length us, event | category | flops | bytes accessed | tf_op | source)
XLA Modules:
  0.0 153.5 jit_solution(1798843627113118985)
XLA Ops:
  1.3 0.7 subtract_bitcast_fusion
  2.0 0.8 select_reduce_fusion
  2.8 1.3 copy.11
  4.1 0.1 select_reduce_fusion.1
  4.3 0.0 copy-start
  4.3 0.8 shard_map.85
  5.1 36.1 %all_to_all.30.second = bf16[16,192,128]{2,1,0:T(8,128)(2,1)S(1)} all-to-all(bf16[16,192,128]{2,1,0:T(8,128)(2,1)S(1)} %shard_map.85), channel_id=1, replica_groups=mesh['y'=8,'core'=2,'x'=4,'z'=12] {'y','core'}, dimensions={0} | all-to-all | bytes 1572864 | tf_op jit(solution)/shard_map/all_to_all | solution.py:336
  41.2 0.0 copy-start.1
  41.2 0.0 copy-done
  41.2 2.6 %shard_map.86 = f32[64,2,128]{2,1,0:T(2,128)} custom-call(s32[5,16]{1,0:T(8,128)S(1)} %stack.16.tab, bf16[16,192,128]{2,1,0:T(8,128)(2,1)S(1)} %bitcast.21, bf16[16,192,128]{2,1,0:T(8,128)(2,1)S(1)} %all_to_all.30.second, f32[16,128,128]{2,1,0:T(8,128)S(1)} %bitcast.24), custom_call_target="tpu_custom_call" | custom-call | tf_op jit(solution)/shard_map/pallas_call | solution.py:368
  43.8 4.2 %all-to-all-start.1 = ((f32[64,2,128]{2,1,0:T(2,128)}), f32[64,2,128]{2,1,0:T(2,128)S(1)}, u32[]{:S(2)}, u32[]{:S(2)}) async-start(f32[64,2,128]{2,1,0:T(2,128)} %shard_map.86), calls=%async_computation.1 | async-start | bytes 131072 | tf_op jit(solution)/shard_map/all_to_all | solution.py:336
  48.0 0.0 copy-done.1
  48.0 8.5 %all-to-all-done.1.parts = f32[64,2,128]{2,1,0:T(2,128)S(1)} async-done(((f32[64,2,128]{2,1,0:T(2,128)}), f32[64,2,128]{2,1,0:T(2,128)S(1)}, u32[]{:S(2)}, u32[]{:S(2)}) %all-to-all-start.1) | async-done | bytes 65568 | tf_op jit(solution)/shard_map/all_to_all | solution.py:336
  56.5 0.7 shard_map.87
  57.2 12.6 %all-to-all-start.2 = ((f32[12,2,128]{2,1,0:T(2,128)}), f32[12,2,128]{2,1,0:T(2,128)S(1)}, u32[]{:S(2)}, u32[]{:S(2)}) async-start(f32[12,2,128]{2,1,0:T(2,128)} %shard_map.87), calls=%async_computation.2 | async-start | bytes 24576 | tf_op jit(solution)/shard_map/all_to_all | solution.py:336
  69.8 9.0 %all-to-all-done.2.sums = f32[12,2,128]{2,1,0:T(2,128)S(1)} async-done(((f32[12,2,128]{2,1,0:T(2,128)}), f32[12,2,128]{2,1,0:T(2,128)S(1)}, u32[]{:S(2)}, u32[]{:S(2)}) %all-to-all-start.2) | async-done | bytes 12320 | tf_op jit(solution)/shard_map/all_to_all | solution.py:336
  78.7 6.4 %shard_map.88 = (f32[16,128,128]{2,1,0:T(8,128)S(1)}, s16[16,208,128]{2,1,0:T(8,128)(2,1)S(1)}, f32[4,768,128]{2,1,0:T(8,128)S(1)}) custom-call(s32[5,16]{1,0:T(8,128)S(1)} %stack.16.tab, bf16[16,192,128]{2,1,0:T(8,128)(2,1)S(1)} %bitcast.22, bf16[16,192,128]{2,1,0:T(8,128)(2,1)S(1)} %all_to_all.30.second, f32[16,128,128]{2,1,0:T(8,128)S(1)} %bitcast.25, ...), custom_call_target="tpu_custom_call" | custom-call | tf_op jit(solution)/shard_map/pallas_call | solution.py:373
  85.1 29.6 %all_to_all.31.got = s16[16,208,128]{2,1,0:T(8,128)(2,1)S(1)} all-to-all(s16[16,208,128]{2,1,0:T(8,128)(2,1)S(1)} %get-tuple-element.10), channel_id=1, replica_groups=mesh['y'=8,'core'=2,'x'=4,'z'=12] {'y','core'}, dimensions={0} | all-to-all | bytes 1703936 | tf_op jit(solution)/shard_map/all_to_all | solution.py:336
  114.7 2.4 %shard_map.89 = s16[4,784,128]{2,1,0:T(8,128)(2,1)S(1)} custom-call(s32[5,16]{1,0:T(8,128)S(1)} %stack.16.tab, s16[16,208,128]{2,1,0:T(8,128)(2,1)S(1)} %all_to_all.31.got, f32[4,768,128]{2,1,0:T(8,128)S(1)} %get-tuple-element.11.dense_in), custom_call_target="tpu_custom_call" | custom-call | tf_op jit(solution)/shard_map/pallas_call | solution.py:385
  117.2 14.8 %all_to_all.32.got = s16[4,784,128]{2,1,0:T(8,128)(2,1)S(1)} all-to-all(s16[4,784,128]{2,1,0:T(8,128)(2,1)S(1)} %shard_map.89), channel_id=1, replica_groups=mesh['y'=8,'core'=2,'x'=4,'z'=12] {'x'}, dimensions={0} | all-to-all | bytes 1605632 | tf_op jit(solution)/shard_map/all_to_all | solution.py:336
  132.0 1.1 shard_map.90
  133.1 17.0 %all_to_all.33.got = s16[12,80,128]{2,1,0:T(8,128)(2,1)S(1)} all-to-all(s16[12,80,128]{2,1,0:T(8,128)(2,1)S(1)} %shard_map.90), channel_id=1, replica_groups=mesh['y'=8,'core'=2,'x'=4,'z'=12] {'z'}, dimensions={0} | all-to-all | bytes 491520 | tf_op jit(solution)/shard_map/all_to_all | solution.py:336
  150.1 3.4 %shard_map.91 = (f32[2,128]{1,0:T(2,128)}, f32[4,16,128]{2,1,0:T(8,128)}, f32[16,128,128]{2,1,0:T(8,128)}) custom-call(s32[5,16]{1,0:T(8,128)S(1)} %stack.16.tab, bf16[16,192,128]{2,1,0:T(8,128)(2,1)S(1)} %bitcast.23, bf16[16,192,128]{2,1,0:T(8,128)(2,1)S(1)} %all_to_all.30.second, f32[16,128,128]{2,1,0:T(8,128)S(1)} %get-tuple-element.9.moved, ...), custom_call_target="tpu_custom_call" | custom-call | tf_op jit(solution)/shard_map/pallas_call | solution.py:391
  (6 shorter events, 0.1 us)
Async XLA Ops:
  4.3 36.9 %copy-start = (f32[1,1,16,128,128]{4,3,2,1,0:T(8,128)S(1)}, f32[1,1,16,128,128]{4,3,2,1,0:T(8,128)}, u32[]{:S(2)}) copy-start(f32[1,1,16,128,128]{4,3,2,1,0:T(8,128)} %param.11) | copy-start | bytes 3145732
  41.2 6.8 %copy-start.1 = (s32[192]{0:T(256)S(1)}, s32[192]{0:T(256)}, u32[]{:S(2)}) copy-start(s32[192]{0:T(256)} %param.7) | copy-start | bytes 2308
  43.8 12.8 %all-to-all-start.1 = ((f32[64,2,128]{2,1,0:T(2,128)}), f32[64,2,128]{2,1,0:T(2,128)S(1)}, u32[]{:S(2)}, u32[]{:S(2)}) async-start(f32[64,2,128]{2,1,0:T(2,128)} %shard_map.86), calls=%async_computation.1 | async-start | bytes 131072 | tf_op jit(solution)/shard_map/all_to_all | solution.py:336
  57.2 21.5 %all-to-all-start.2 = ((f32[12,2,128]{2,1,0:T(2,128)}), f32[12,2,128]{2,1,0:T(2,128)S(1)}, u32[]{:S(2)}, u32[]{:S(2)}) async-start(f32[12,2,128]{2,1,0:T(2,128)} %shard_map.87), calls=%async_computation.2 | async-start | bytes 24576 | tf_op jit(solution)/shard_map/all_to_all | solution.py:336

commit v4 on v3

--- a/solution.py
+++ b/solution.py
@@ -16,7 +16,8 @@
 f32 = jnp.float32
 bf16 = jnp.bfloat16
 
-SLOT, FIRST, LIVE, SERVED, ME = range(5)
+SLOT, FIRST, LIVE, SERVED, MY_OWN, MY_GRP, MY_X = range(7)
+SPARE = 64
 
 
 def split(x):
@@ -76,14 +77,23 @@
 
     lax.fori_loop(0, second.shape[0], step, 0, unroll=4)
     chunk = row_sums(acc[...] * (1.0 / 128.0))
+    lanes = iota((2, 128), 1) + 128 * (1 - iota((2, 128), 0))
+    for j in range(second.shape[0]):
+        chunk = jnp.where(lanes == SPARE + j, tab[SERVED, j].astype(f32), chunk)
     for i in range(out.shape[0]):
         out[i] = chunk
 
 
-def sum_kernel(parts, out):
+def sum_kernel(tab, parts, out, served):
     total = total_of(parts)
     for i in range(out.shape[0]):
         out[i] = total
+    n_x = served.shape[0]
+    near = parts[pl.ds(tab[MY_GRP, 0] * n_x, n_x)]
+    lanes = iota((1, 128), 1)
+    mine = (lanes >= SPARE) & (lanes < SPARE + 16)
+    for i in range(n_x):
+        served[i : i + 1] = jnp.where(mine, near[i, 1:2], 0.0).astype(jnp.int32)
 
 
 def total_of(parts):
@@ -121,30 +131,28 @@
     return lax.broadcasted_iota(jnp.int32, dims, axis)
 
 
-def rows_of(named):
-    rows = iota((16, 128), 0)
-    out = jnp.zeros((16, 128), f32)
-    for r, value in named.items():
-        out = jnp.where(rows == r, value, out)
-    return out
-
-
-def digits(low, high, at):
-    k = exponent(jnp.maximum(peaks(low), peaks(high)))
-    up = LEVELS * scale_of(-k)
-    a, b = low * up, high * up
-    named = {at: jnp.round(a), at + 1: jnp.round(b)}
-    named[at + 2] = (a - named[at]) * LEVELS
-    named[at + 3] = (b - named[at + 1]) * LEVELS
-    named[at + 4] = jnp.broadcast_to(k, (1, 128))
-    return named
+def tile_of(height, pieces):
+    used = sum(p.shape[0] for p in pieces)
+    return jnp.concatenate(pieces + [jnp.zeros((height - used, 128), f32)], axis=0)
+
+
+def digits(pair):
+    k = exponent(jnp.max(peaks(pair), axis=0, keepdims=True))
+    wide = pair * (LEVELS * scale_of(-k))
+    high = jnp.round(wide)
+    return [high, (wide - high) * LEVELS, jnp.broadcast_to(k, (1, 128))]
 
 
 def undigit(tile, at):
     s = scale_of(tile[at + 4 : at + 5]) * (1.0 / LEVELS)
-    low = s * (tile[at : at + 1] + tile[at + 2 : at + 3] * (1.0 / LEVELS))
-    high = s * (tile[at + 1 : at + 2] + tile[at + 3 : at + 4] * (1.0 / LEVELS))
-    return low, high
+    return s * (tile[at : at + 2] + tile[at + 2 : at + 4] * (1.0 / LEVELS))
+
+
+def undigits(tiles, at):
+    total = undigit(tiles[0], at)
+    for t in tiles[1:]:
+        total = total + undigit(t, at)
+    return total
 
 
 def upright(rows, height):
@@ -153,10 +161,12 @@
 
 
 def terms_kernel(
-    scale, rate, tab, ft, second, mats, sums, labels, moved, out, dense, acc, errs, stash, tops
+    scale, rate, tab, ft, second, mats, sums, labels,
+    moved, out, own, to_1, to_2, to_3, acc, errs, stash, tops, dense,
 ):
     samples = second.shape[1]
-    n_x, rows = dense.shape[0], samples // dense.shape[0]
+    n_x, size = dense.shape[0], dense.shape[1]
+    rows, parts = samples // n_x, size // 128
     errors = jax.nn.sigmoid(scale * total_of(sums)) - labels[...]
     errs[...] = spread(errors, samples)
     acc[...] = jnp.zeros_like(acc)
@@ -183,80 +193,65 @@
         return carry
 
     lax.fori_loop(0, second.shape[0], step, 0, unroll=2)
+
     k = exponent(tops[...])
     up = LEVELS * scale_of(-k)
-    low = jnp.transpose(k[:128])
-    high = jnp.transpose(
-        jnp.concatenate([k[128:], jnp.zeros((256 - samples, 128), f32)], axis=0)
-    )
-    chunk = row_sums(acc[...] * (1.0 / 128.0))
-    tile = rows_of(digits(chunk[0:1], chunk[1:2], 0))
-    rows = iota((16, 128), 0)
-    for j in range(out.shape[0]):
-        out[j, 0:samples] = whole(stash[j] * up[:, j : j + 1])
-        mine = jnp.where(rows == 6, high[j : j + 1], tile)
-        out[j, samples : samples + 16] = whole(jnp.where(rows == 5, low[j : j + 1], mine))
-
-
-def dense_kernel(tab, got, dense_in, out, dense):
-    samples = got.shape[1] - 16
-    n_x, rows = dense.shape[0], samples // dense.shape[0]
-    size = dense.shape[1]
-    parts = size // 128
-    tiles = [real(got[j, samples : samples + 16]) for j in range(got.shape[0])]
-    low = upright([t[5:6] for t in tiles], 128)
-    high = upright([t[6:7] for t in tiles], samples - 128)
-    down = scale_of(jnp.concatenate([low, high], axis=0)) * (1.0 / LEVELS)
-    dense[...] = dense_in[...]
-    sums = [undigit(t, 0) for t in tiles]
-    total = sums[0]
-    for j in range(got.shape[0]):
-        at = pl.ds(pl.multiple_of(tab[SERVED, j] * rows, 8), rows)
-        value = real(got[j, 0:samples]) * down[:, j : j + 1]
-        for i in range(n_x):
-            dense[i, at] += value[i * rows : (i + 1) * rows]
-        if j:
-            total = (total[0] + sums[j][0], total[1] + sums[j][1])
-
+    common = digits(row_sums(acc[...] * (1.0 / 128.0)))
+    for i in range(n_x):
+        part = slice(i * rows, (i + 1) * rows)
+        lying = jnp.transpose(tile_of(128, [k[part]]))
+        for j in range(second.shape[0]):
+            d = j * n_x + i
+            out[d, 0:rows] = whole(stash[j, part] * up[part, j : j + 1])
+            out[d, rows : rows + 8] = whole(tile_of(8, [lying[j : j + 1]] + common))
+
+    x = tab[MY_X, 0]
+    own[...] = dense[x]
     lanes = iota((128, 128), 1)
-    tops = jnp.zeros((128, 128), f32)
-    for i in range(n_x):
+    far = [lax.rem(x + r, n_x) for r in range(1, n_x)]
+    high = jnp.zeros((128, 128), f32)
+    for i, to in enumerate(far):
         for t in range(parts):
-            top = peaks(dense[i, t * 128 : (t + 1) * 128])
-            tops = jnp.where(lanes == i * parts + t, top, tops)
-    k = exponent(tops)
+            top = peaks(dense[to, t * 128 : (t + 1) * 128])
+            high = jnp.where(lanes == i * parts + t, top, high)
+    k = exponent(high)
     up = LEVELS * scale_of(-k)
     lying = jnp.transpose(k)
-    common = digits(total[0], total[1], parts)
-    for i in range(n_x):
-        named = dict(common)
+    for i, (to, ref) in enumerate(zip(far, (to_1, to_2, to_3))):
         for t in range(parts):
             lane = i * parts + t
-            part = dense[i, t * 128 : (t + 1) * 128]
-            out[i, t * 128 : (t + 1) * 128] = whole(part * up[:, lane : lane + 1])
-            named[t] = lying[lane : lane + 1]
-        out[i, size : size + 16] = whole(rows_of(named))
-
-
-def across_kernel(got, out, sums, parted):
-    n_z, wide = out.shape[0], out.shape[1] - 16
+            part = dense[to, t * 128 : (t + 1) * 128]
+            ref[t * 128 : (t + 1) * 128] = whole(part * up[:, lane : lane + 1])
+        mine = lying[i * parts : (i + 1) * parts]
+        ref[size : size + 8] = whole(tile_of(8, [mine]))
+
+
+def across_kernel(served, got, own, from_1, from_2, from_3, out, sums, parted):
+    n_x, n_z = served.shape[0], out.shape[0]
+    wide = out.shape[1] - 16
     few = wide // 16
-    rows = n_z * few
-    size = 16 * rows
+    size, rows = own.shape[0], n_z * few
     parts = size // 128
-    tiles = [real(got[i, size : size + 16]) for i in range(got.shape[0])]
-    exps = upright([t[r : r + 1] for t in tiles for r in range(parts)], 128)
-    down = scale_of(exps) * (1.0 / LEVELS)
+
+    sides = (from_1, from_2, from_3)
+    exps = [real(ref[size : size + 8])[0:parts] for ref in sides]
+    down = jnp.transpose(tile_of(128, exps))
+    down = scale_of(down) * (1.0 / LEVELS)
     for t in range(parts):
-        total = real(got[0, t * 128 : (t + 1) * 128]) * down[:, t : t + 1]
-        for i in range(1, got.shape[0]):
+        part = slice(t * 128, (t + 1) * 128)
+        total = own[part]
+        for i, ref in enumerate(sides):
             lane = i * parts + t
-            total = total + real(got[i, t * 128 : (t + 1) * 128]) * down[:, lane : lane + 1]
-        sums[t * 128 : (t + 1) * 128] = total
-    pair = undigit(tiles[0], parts)
-    for t in tiles[1:]:
-        more = undigit(t, parts)
-        pair = (pair[0] + more[0], pair[1] + more[1])
+            total = total + real(ref[part]) * down[:, lane : lane + 1]
+        sums[part] = total
+
+    tiles = [real(got[d, rows : rows + 8]) for d in range(got.shape[0])]
+    down = scale_of(upright([t[0:1] for t in tiles], rows)) * (1.0 / LEVELS)
+    for d in range(got.shape[0]):
+        field = served[d % n_x, SPARE + d // n_x]
+        at = pl.ds(pl.multiple_of(field * rows, 8), rows)
+        sums[at] += real(got[d, 0:rows]) * down[:, d : d + 1]
+
     for f in range(16):
         for z in range(n_z):
             start = f * rows + z * few
@@ -268,15 +263,13 @@
     k = exponent(tops)
     up = LEVELS * scale_of(-k)
     if wide < 128:
-        k = jnp.concatenate([k, jnp.zeros((128 - wide, 128), f32)], axis=0)
+        k = tile_of(128, [k])
     lying = [jnp.transpose(k[n * 128 : (n + 1) * 128]) for n in range(k.shape[0] // 128)]
-    common = digits(pair[0], pair[1], len(lying))
+    common = digits(undigits(tiles, 1))
     for z in range(n_z):
         out[z, 0:wide] = whole(parted[z] * up[:, z : z + 1])
-        named = dict(common)
-        for n, part in enumerate(lying):
-            named[n] = part[z : z + 1]
-        out[z, wide : wide + 16] = whole(rows_of(named))
+        mine = [part[z : z + 1] for part in lying]
+        out[z, wide : wide + 16] = whole(tile_of(16, mine + common))
 
 
 def last_kernel(
@@ -289,11 +282,7 @@
     high = -(-wide // 128)
     exps = [upright([t[n : n + 1] for t in tiles], min(wide, 128)) for n in range(high)]
     down = scale_of(jnp.concatenate(exps, axis=0)) * (1.0 / LEVELS)
-    pair = undigit(tiles[0], high)
-    for t in tiles[1:]:
-        more = undigit(t, high)
-        pair = (pair[0] + more[0], pair[1] + more[1])
-    value = scale * jnp.concatenate(pair, axis=0)
+    value = scale * undigits(tiles, high)
     logits[...] = value
     errs[...] = spread(jax.nn.sigmoid(value) - labels[...], samples)
     total = real(got[0, 0:wide]) * down[:, 0:1]
@@ -301,7 +290,7 @@
         total = total + real(got[i, 0:wide]) * down[:, i : i + 1]
     sums[...] = total * (1.0 / math.sqrt(128.0))
     for b in range(few):
-        mine = errs[pl.ds(tab[ME, 0] * few + b, 1)]
+        mine = errs[pl.ds(tab[MY_OWN, 0] * few + b, 1)]
         grads[b] = sums[pl.ds(b, 16, stride=few)] * mine
 
     def step(j, carry):
@@ -324,7 +313,7 @@
         in_specs=specs,
         out_specs=out_specs,
         scratch_shapes=list(scratch),
-        compiler_params=pltpu.CompilerParams(vmem_limit_bytes=40 << 20),
+        compiler_params=pltpu.CompilerParams(vmem_limit_bytes=16 << 20),
     )
 
 
@@ -355,8 +344,9 @@
     slot_of = jnp.sum(jnp.where(picked, slot_ids, 0), axis=0)
     first_of = jnp.sum(jnp.where(picked, (pair_first[0, 0] - me * per_block)[:, None], 0), axis=0)
     live = (slot_of < pair_count[0, 0]).astype(jnp.int32)
-    where_am_i = jnp.full((slots,), lax.axis_index(OWN), jnp.int32)
-    tab = jnp.stack([slot_of, first_of, live, served, where_am_i])
+    places = [lax.axis_index(OWN), me, lax.axis_index("x")]
+    places = [jnp.full((slots,), place, jnp.int32) for place in places]
+    tab = jnp.stack([slot_of, first_of, live, served] + places)
 
     ft = jnp.transpose(fields, (1, 0, 2))
     mats = pair_mats[0, 0]
@@ -366,27 +356,40 @@
     second = swap(sent, GRP)
     acc = pltpu.VMEM((samples, 128), f32)
     part = call(partial_kernel, [shape((groups * n_x, 2, 128))], 4, [acc])(tab, ft, second, mats)[0]
-    part = call(sum_kernel, [shape((n_z, 2, 128))], 1, smem=False)(swap(part, GRP + ("x",)))[0]
+    out = [shape((n_z, 2, 128)), shape((n_x, 128), jnp.int32)]
+    part, near = call(sum_kernel, out, 2)(tab, swap(part, GRP + ("x",)))
     sums = swap(part, "z")
 
-    size, wide = per_block * (samples // n_x), per_block * few
-    moved, out, dense = call(
+    rows, wide = samples // n_x, per_block * few
+    size = per_block * rows
+    side = shape((size + 8, feature), jnp.int16)
+    moved, out, own, *sides = call(
         functools.partial(terms_kernel, scale, rate),
         [
             shape(mats.shape),
-            shape((slots, samples + 16, feature), jnp.int16),
-            shape((n_x, size, feature)),
+            shape((groups * n_x, rows + 8, feature), jnp.int16),
+            shape((size, feature)),
+            side,
+            side,
+            side,
         ],
         6,
-        [acc, acc, pltpu.VMEM((slots, samples, feature), f32), acc],
+        [
+            acc,
+            acc,
+            pltpu.VMEM((slots, samples, feature), f32),
+            acc,
+            pltpu.VMEM((n_x, size, feature), f32),
+        ],
     )(tab, ft, second, mats, sums, targets)
-    got = swap(out, GRP)
-    out = [shape((n_x, size + 16, feature), jnp.int16)]
-    got = call(dense_kernel, out, 3, [pltpu.VMEM((n_x, size, feature), f32)])(tab, got, dense)[0]
-    got = swap(got, "x")
+    got = swap(out, GRP + ("x",))
+    sides = [
+        lax.ppermute(side, "x", [(i, (i + r) % n_x) for i in range(n_x)])
+        for r, side in enumerate(sides, 1)
+    ]
     out = [shape((n_z, wide + 16, feature), jnp.int16)]
     room = [pltpu.VMEM((size, feature), f32), pltpu.VMEM((n_z, wide, feature), f32)]
-    got = call(across_kernel, out, 1, room, smem=False)(got)[0]
+    got = call(across_kernel, out, 6, room)(near, got, own, *sides)[0]
     got = swap(got, "z")
     logits, grads, mats = call(
         functools.partial(last_kernel, scale, rate),

time: 154 us -> 145 us (0.942)
  blocking collectives: 97.6 us -> 51.9 us
  starting transfers between devices: 16.8 us -> 34.3 us
  waiting for transfers between devices: 17.5 us -> 31.4 us
  local copies, waits for them, and re-layouts: 1.39 us -> 5.36 us
    all_to_all x4 -> x2, blocking collectives: 97.6 us -> 51.9 us  [swap(): return lax.all_to_all(x, axes, split_axis=0, concat_axis=0, tiled=True)]
    ppermute x0 -> x3, waiting for transfers between devices: none -> 11.3 us  [on_device(): lax.ppermute(side, 'x', [(i, (i + r) % n_x) for i in range(n_x)])]
    ppermute x0 -> x3, starting transfers between devices: none -> 10.7 us  [on_device(): lax.ppermute(side, 'x', [(i, (i + r) % n_x) for i in range(n_x)])]
    all_to_all x2 -> x3, starting transfers between devices: 16.8 us -> 23.7 us  [swap(): return lax.all_to_all(x, axes, split_axis=0, concat_axis=0, tiled=True)]
    unnamed x5 -> x21, local copies, waits for them, and re-layouts: 1.35 us -> 5.31 us
    all_to_all x2 -> x3, waiting for transfers between devices: 17.5 us -> 20.1 us  [swap(): return lax.all_to_all(x, axes, split_axis=0, concat_axis=0, tiled=True)]
    pallas_call x1, Pallas kernels: 6.39 us -> 8.3 us  [on_device(): call(functools.partial(terms_kernel, scale, rate), [shape(mats.shape), sh...]
    pallas_call x3 -> x2, Pallas kernels: 4.22 us -> 3.33 us  [the longest x1 2.06 us: on_device(): got = call(across_kernel, out, 6, room)(near, got, own, *sides)[0]]
  transfers between devices with their start and end apart: 2 -> 6, of which waited for: 2 -> 5; matrix products, arithmetic and copies ran while one was open for 0% -> 0% of each run, Pallas kernels for 0% -> 0%
where the time goes in v4:
time: 145 us; the launch traced here: 143 us
  blocking collectives  51.9 us (36%)
  starting transfers between devices  34.3 us (24%)
  waiting for transfers between devices  31.4 us (22%)
  Pallas kernels  18.4 us (13%)
  local copies, waits for them, and re-layouts  5.36 us (4%)
  between operations  1.5 us (1%)
    all_to_all x2, blocking collectives, swap(): return lax.all_to_all(x, axes, split_axis=0, concat_axis=0, tiled=True)  51.9 us
    all_to_all x3, starting transfers between devices, swap(): return lax.all_to_all(x, axes, split_axis=0, concat_axis=0, tiled=True)  23.7 us
    all_to_all x3, waiting for transfers between devices, swap(): return lax.all_to_all(x, axes, split_axis=0, concat_axis=0, tiled=True)  20.1 us
    ppermute x3, waiting for transfers between devices, on_device(): lax.ppermute(side, 'x', [(i, (i + r) % n_x) for i in range(n_x)])  11.3 us
    ppermute x3, starting transfers between devices, on_device(): lax.ppermute(side, 'x', [(i, (i + r) % n_x) for i in range(n_x)])  10.7 us
    pallas_call x1, Pallas kernels, on_device(): call(functools.partial(terms_kernel, scale, rate), [shape(mats.shape), sh...  8.3 us
    unnamed x21, local copies, waits for them, and re-layouts  5.31 us
    pallas_call x1, Pallas kernels, on_device(): call(functools.partial(last_kernel, scale, rate), [shape((2, 128)), shape...  3.37 us
  transfers between devices with their start and end apart: 6, of which 5 were waited for; matrix products, arithmetic and copies ran while one was open for 0% of the time, Pallas kernels for 0%

profile of v4, /device:TPU:1, one launch (start us, length us, event | category | flops | bytes accessed | tf_op | source)
XLA Modules:
  0.0 143.1 jit_solution(6425146987887738773)
XLA Ops:
  0.6 0.0 copy-start.7
  0.7 0.0 copy-start.9
  1.4 0.1 select_reduce_fusion
  1.5 1.3 copy.11
  2.9 0.1 select_reduce_fusion.1
  3.0 0.8 shard_map.85
  3.8 0.0 copy-start
  3.8 36.2 %all_to_all.25.second = bf16[16,192,128]{2,1,0:T(8,128)(2,1)S(1)} all-to-all(bf16[16,192,128]{2,1,0:T(8,128)(2,1)S(1)} %shard_map.85), channel_id=1, replica_groups=mesh['y'=8,'core'=2,'x'=4,'z'=12] {'y','core'}, dimensions={0} | all-to-all | bytes 1572864 | tf_op jit(solution)/shard_map/all_to_all | solution.py:325
  40.0 2.6 %shard_map.86 = f32[64,2,128]{2,1,0:T(2,128)} custom-call(s32[7,16]{1,0:T(8,128)S(1)} %stack.16.tab, bf16[16,192,128]{2,1,0:T(8,128)(2,1)S(1)} %bitcast.21, bf16[16,192,128]{2,1,0:T(8,128)(2,1)S(1)} %all_to_all.25.second, f32[16,128,128]{2,1,0:T(8,128)S(1)} %bitcast.24), custom_call_target="tpu_custom_call" | custom-call | tf_op jit(solution)/shard_map/pallas_call | solution.py:358
  42.7 4.3 %all-to-all-start.1 = ((f32[64,2,128]{2,1,0:T(2,128)}), f32[64,2,128]{2,1,0:T(2,128)S(1)}, u32[]{:S(2)}, u32[]{:S(2)}) async-start(f32[64,2,128]{2,1,0:T(2,128)} %shard_map.86), calls=%async_computation.1 | async-start | bytes 131072 | tf_op jit(solution)/shard_map/all_to_all | solution.py:325
  47.0 8.5 %all-to-all-done.1.parts = f32[64,2,128]{2,1,0:T(2,128)S(1)} async-done(((f32[64,2,128]{2,1,0:T(2,128)}), f32[64,2,128]{2,1,0:T(2,128)S(1)}, u32[]{:S(2)}, u32[]{:S(2)}) %all-to-all-start.1) | async-done | bytes 65568 | tf_op jit(solution)/shard_map/all_to_all | solution.py:325
  55.5 1.3 shard_map.87
  56.8 12.6 %all-to-all-start.2 = ((f32[12,2,128]{2,1,0:T(2,128)}), f32[12,2,128]{2,1,0:T(2,128)S(1)}, u32[]{:S(2)}, u32[]{:S(2)}) async-start(f32[12,2,128]{2,1,0:T(2,128)} %get-tuple-element.14), calls=%async_computation.2 | async-start | bytes 24576 | tf_op jit(solution)/shard_map/all_to_all | solution.py:325
  69.4 9.0 %all-to-all-done.2.sums = f32[12,2,128]{2,1,0:T(2,128)S(1)} async-done(((f32[12,2,128]{2,1,0:T(2,128)}), f32[12,2,128]{2,1,0:T(2,128)S(1)}, u32[]{:S(2)}, u32[]{:S(2)}) %all-to-all-start.2) | async-done | bytes 12320 | tf_op jit(solution)/shard_map/all_to_all | solution.py:325
  78.4 8.3 %shard_map.88 = (f32[16,128,128]{2,1,0:T(8,128)S(1)}, s16[64,56,128]{2,1,0:T(8,128)(2,1)}, f32[768,128]{1,0:T(8,128)S(1)}, s16[776,128]{1,0:T(8,128)(2,1)S(1)}, ...) custom-call(s32[7,16]{1,0:T(8,128)S(1)} %stack.16.tab, bf16[16,192,128]{2,1,0:T(8,128)(2,1)S(1)} %bitcast.22, ...), custom_call_target="tpu_custom_call" | custom-call | tf_op jit(solution)/shard_map/pallas_call | solution.py:366
  86.7 1.0 copy-done.1
  87.6 0.7 copy-done.6
  88.3 0.7 copy-done.5
  89.0 6.8 %all-to-all-start.3 = ((s16[64,56,128]{2,1,0:T(8,128)(2,1)}), s16[64,56,128]{2,1,0:T(8,128)(2,1)S(1)}, u32[]{:S(2)}, u32[]{:S(2)}) async-start(s16[64,56,128]{2,1,0:T(8,128)(2,1)} %get-tuple-element.17), calls=%async_computation.3 | async-start | bytes 1835008 | tf_op jit(solution)/shard_map/all_to_all | solution.py:325
  95.8 3.3 %collective-permute-start = (s16[776,128]{1,0:T(8,128)(2,1)}, s16[776,128]{1,0:T(8,128)(2,1)S(1)}, u32[]{:S(2)}, u32[]{:S(2)}) collective-permute-start(s16[776,128]{1,0:T(8,128)(2,1)} %copy-done.6), channel_id=1, source_target_pairs={{0,12},{12,24},{24,36},{36,0},{1,13},{13,25},{25,37},{37,1},{2,14}... | collective-permute-start | bytes 595976 | tf_op jit(solution)/shard_map/ppermute | solution.py:387
  99.1 4.3 %collective-permute-start.1 = (s16[776,128]{1,0:T(8,128)(2,1)}, s16[776,128]{1,0:T(8,128)(2,1)S(1)}, u32[]{:S(2)}, u32[]{:S(2)}) collective-permute-start(s16[776,128]{1,0:T(8,128)(2,1)} %copy-done.5), channel_id=1, source_target_pairs={{0,24},{12,36},{24,0},{36,12},{1,25},{13,37},{25,1},{37,13},{2,26}... | collective-permute-start | bytes 595976 | tf_op jit(solution)/shard_map/ppermute | solution.py:387
  103.4 3.1 %collective-permute-start.2 = (s16[776,128]{1,0:T(8,128)(2,1)S(1)}, s16[776,128]{1,0:T(8,128)(2,1)S(1)}, u32[]{:S(2)}, u32[]{:S(2)}) collective-permute-start(s16[776,128]{1,0:T(8,128)(2,1)S(1)} %get-tuple-element.21), channel_id=1, source_target_pairs={{0,36},{12,0},{24,12},{36,24},{1,37},{13,1},{25,13},{37,25},{2,38}... | collective-permute-start | bytes 595976 | tf_op jit(solution)/shard_map/ppermute | solution.py:387
  106.5 2.1 %collective-permute-done.from_1 = s16[776,128]{1,0:T(8,128)(2,1)S(1)} collective-permute-done((s16[776,128]{1,0:T(8,128)(2,1)}, s16[776,128]{1,0:T(8,128)(2,1)S(1)}, u32[]{:S(2)}, u32[]{:S(2)}) %collective-permute-start) | collective-permute-done | bytes 198688 | tf_op jit(solution)/shard_map/ppermute | solution.py:387
  108.6 9.2 %collective-permute-done.1.from_2 = s16[776,128]{1,0:T(8,128)(2,1)S(1)} collective-permute-done((s16[776,128]{1,0:T(8,128)(2,1)}, s16[776,128]{1,0:T(8,128)(2,1)S(1)}, u32[]{:S(2)}, u32[]{:S(2)}) %collective-permute-start.1) | collective-permute-done | bytes 198688 | tf_op jit(solution)/shard_map/ppermute | solution.py:387
  117.8 0.0 collective-permute-done.2.from_3
  117.8 0.7 copy-done.3
  118.5 2.6 %all-to-all-done.3.got = s16[64,56,128]{2,1,0:T(8,128)(2,1)S(1)} async-done(((s16[64,56,128]{2,1,0:T(8,128)(2,1)}), s16[64,56,128]{2,1,0:T(8,128)(2,1)S(1)}, u32[]{:S(2)}, u32[]{:S(2)}) %all-to-all-start.3) | async-done | bytes 917536 | tf_op jit(solution)/shard_map/all_to_all | solution.py:325
  121.0 0.9 copy-done.4
  122.0 2.1 %shard_map.89 = s16[12,80,128]{2,1,0:T(8,128)(2,1)S(1)} custom-call(s32[4,128]{1,0:T(4,128)S(1)} %get-tuple-element.16.served, s16[64,56,128]{2,1,0:T(8,128)(2,1)S(1)} %all-to-all-done.3.got, f32[768,128]{1,0:T(8,128)S(1)} %get-tuple-element.18.own, s16[776,128]{1,0:T(8,128)(2,1)S(1)} %collective-permute-done.from_1, ...), custom_call_target="tpu_custom_call" | custom-call | tf_op jit(solution)/shard_map/pallas_call | solution.py:392
  124.0 15.7 %all_to_all.26.got = s16[12,80,128]{2,1,0:T(8,128)(2,1)S(1)} all-to-all(s16[12,80,128]{2,1,0:T(8,128)(2,1)S(1)} %shard_map.89), channel_id=1, replica_groups=mesh['y'=8,'core'=2,'x'=4,'z'=12] {'z'}, dimensions={0} | all-to-all | bytes 491520 | tf_op jit(solution)/shard_map/all_to_all | solution.py:325
  139.7 0.0 copy-done.2
  139.7 3.4 %shard_map.90 = (f32[2,128]{1,0:T(2,128)}, f32[4,16,128]{2,1,0:T(8,128)}, f32[16,128,128]{2,1,0:T(8,128)}) custom-call(s32[7,16]{1,0:T(8,128)S(1)} %stack.16.tab, bf16[16,192,128]{2,1,0:T(8,128)(2,1)S(1)} %bitcast.23, bf16[16,192,128]{2,1,0:T(8,128)(2,1)S(1)} %all_to_all.25.second, f32[16,128,128]{2,1,0:T(8,128)S(1)} %copy-done.2, ...), custom_call_target="tpu_custom_call" | custom-call | tf_op jit(solution)/shard_map/pallas_call | solution.py:394
  (20 shorter events, 0.1 us)
Async XLA Ops:
  0.6 0.7 copy-start.7
  0.7 0.7 copy-start.9
  3.8 36.3 %copy-start = (f32[1,1,16,128,128]{4,3,2,1,0:T(8,128)S(1)}, f32[1,1,16,128,128]{4,3,2,1,0:T(8,128)}, u32[]{:S(2)}) copy-start(f32[1,1,16,128,128]{4,3,2,1,0:T(8,128)} %param.11) | copy-start | bytes 3145732
  42.7 4.3 %copy-start.8 = (s32[192]{0:T(256)S(1)}, s32[192]{0:T(256)}, u32[]{:S(2)}) copy-start(s32[192]{0:T(256)} %param.7) | copy-start | bytes 2308
  42.7 12.9 %all-to-all-start.1 = ((f32[64,2,128]{2,1,0:T(2,128)}), f32[64,2,128]{2,1,0:T(2,128)S(1)}, u32[]{:S(2)}, u32[]{:S(2)}) async-start(f32[64,2,128]{2,1,0:T(2,128)} %shard_map.86), calls=%async_computation.1 | async-start | bytes 131072 | tf_op jit(solution)/shard_map/all_to_all | solution.py:325
  56.8 21.5 %all-to-all-start.2 = ((f32[12,2,128]{2,1,0:T(2,128)}), f32[12,2,128]{2,1,0:T(2,128)S(1)}, u32[]{:S(2)}, u32[]{:S(2)}) async-start(f32[12,2,128]{2,1,0:T(2,128)} %get-tuple-element.14), calls=%async_computation.2 | async-start | bytes 24576 | tf_op jit(solution)/shard_map/all_to_all | solution.py:325
  86.7 1.0 copy-start.1
  87.6 0.7 copy-start.6
  88.3 0.7 copy-start.5
  89.0 32.0 %all-to-all-start.3 = ((s16[64,56,128]{2,1,0:T(8,128)(2,1)}), s16[64,56,128]{2,1,0:T(8,128)(2,1)S(1)}, u32[]{:S(2)}, u32[]{:S(2)}) async-start(s16[64,56,128]{2,1,0:T(8,128)(2,1)} %get-tuple-element.17), calls=%async_computation.3 | async-start | bytes 1835008 | tf_op jit(solution)/shard_map/all_to_all | solution.py:325
  95.8 12.8 %collective-permute-start = (s16[776,128]{1,0:T(8,128)(2,1)}, s16[776,128]{1,0:T(8,128)(2,1)S(1)}, u32[]{:S(2)}, u32[]{:S(2)}) collective-permute-start(s16[776,128]{1,0:T(8,128)(2,1)} %copy-done.6), channel_id=1, source_target_pairs={{0,12},{12,24},{24,36},{36,0},{1,13},{13,25},{25,37},{37,1},{2,14}... | collective-permute-start | bytes 595976 | tf_op jit(solution)/shard_map/ppermute | solution.py:387
  99.1 18.7 %collective-permute-start.1 = (s16[776,128]{1,0:T(8,128)(2,1)}, s16[776,128]{1,0:T(8,128)(2,1)S(1)}, u32[]{:S(2)}, u32[]{:S(2)}) collective-permute-start(s16[776,128]{1,0:T(8,128)(2,1)} %copy-done.5), channel_id=1, source_target_pairs={{0,24},{12,36},{24,0},{36,12},{1,25},{13,37},{25,1},{37,13},{2,26}... | collective-permute-start | bytes 595976 | tf_op jit(solution)/shard_map/ppermute | solution.py:387
  103.4 14.4 %collective-permute-start.2 = (s16[776,128]{1,0:T(8,128)(2,1)S(1)}, s16[776,128]{1,0:T(8,128)(2,1)S(1)}, u32[]{:S(2)}, u32[]{:S(2)}) collective-permute-start(s16[776,128]{1,0:T(8,128)(2,1)S(1)} %get-tuple-element.21), channel_id=1, source_target_pairs={{0,36},{12,0},{24,12},{36,24},{1,37},{13,1},{25,13},{37,25},{2,38}... | collective-permute-start | bytes 595976 | tf_op jit(solution)/shard_map/ppermute | solution.py:387
  117.8 0.7 copy-start.3
  121.0 0.9 copy-start.4
  122.0 17.8 %copy-start.2 = (f32[16,128,128]{2,1,0:T(8,128)S(1)}, f32[16,128,128]{2,1,0:T(8,128)}, u32[]{:S(2)}) copy-start(f32[16,128,128]{2,1,0:T(8,128)} %copy-done.1) | copy-start | bytes 3145732

commit v5 on v4

--- a/solution.py
+++ b/solution.py
@@ -162,7 +162,7 @@
 
 def terms_kernel(
     scale, rate, tab, ft, second, mats, sums, labels,
-    moved, out, own, to_1, to_2, to_3, acc, errs, stash, tops, dense,
+    out_hbm, own_hbm, to_1, to_2, to_3, acc, errs, stash, tops, dense, out, to_all, sems,
 ):
     samples = second.shape[1]
     n_x, size = dense.shape[0], dense.shape[1]
@@ -180,7 +180,6 @@
         va, vb = ft[first], second[j]
         gradient = dot_lhs(split(va.astype(f32) * errs[...]), vb, ATB)
         updated = mats[slot] - (rate * live) * gradient
-        moved[j] = updated
         pair = split(updated * live)
         mixed = dot_rhs(va, pair, AB)
         acc[...] += mixed * vb.astype(f32)
@@ -194,19 +193,9 @@
 
     lax.fori_loop(0, second.shape[0], step, 0, unroll=2)
 
-    k = exponent(tops[...])
-    up = LEVELS * scale_of(-k)
-    common = digits(row_sums(acc[...] * (1.0 / 128.0)))
-    for i in range(n_x):
-        part = slice(i * rows, (i + 1) * rows)
-        lying = jnp.transpose(tile_of(128, [k[part]]))
-        for j in range(second.shape[0]):
-            d = j * n_x + i
-            out[d, 0:rows] = whole(stash[j, part] * up[part, j : j + 1])
-            out[d, rows : rows + 8] = whole(tile_of(8, [lying[j : j + 1]] + common))
-
     x = tab[MY_X, 0]
-    own[...] = dense[x]
+    copies = [pltpu.make_async_copy(dense.at[x], own_hbm, sems.at[0])]
+    copies[0].start()
     lanes = iota((128, 128), 1)
     far = [lax.rem(x + r, n_x) for r in range(1, n_x)]
     high = jnp.zeros((128, 128), f32)
@@ -221,30 +210,61 @@
         for t in range(parts):
             lane = i * parts + t
             part = dense[to, t * 128 : (t + 1) * 128]
-            ref[t * 128 : (t + 1) * 128] = whole(part * up[:, lane : lane + 1])
+            to_all[i, t * 128 : (t + 1) * 128] = whole(part * up[:, lane : lane + 1])
         mine = lying[i * parts : (i + 1) * parts]
-        ref[size : size + 8] = whole(tile_of(8, [mine]))
-
-
-def across_kernel(served, got, own, from_1, from_2, from_3, out, sums, parted):
+        to_all[i, size : size + 8] = whole(tile_of(8, [mine]))
+        copies.append(pltpu.make_async_copy(to_all.at[i], ref, sems.at[1 + i]))
+        copies[-1].start()
+
+    k = exponent(tops[...])
+    up = LEVELS * scale_of(-k)
+    zero = jnp.zeros((1, 128), f32)
+    tail = tile_of(8, [zero] + digits(row_sums(acc[...] * (1.0 / 128.0))))
+    top_row = iota((8, 128), 0) == 0
+    for i in range(n_x):
+        part = slice(i * rows, (i + 1) * rows)
+        lying = jnp.transpose(tile_of(128, [k[part]]))
+        for j in range(second.shape[0]):
+            d = j * n_x + i
+            out[d, 0:rows] = whole(stash[j, part] * up[part, j : j + 1])
+            out[d, rows : rows + 8] = whole(jnp.where(top_row, lying[j : j + 1], tail))
+
+    copies.append(pltpu.make_async_copy(out, out_hbm, sems.at[n_x]))
+    copies[-1].start()
+    for copy in copies:
+        copy.wait()
+
+
+def across_kernel(
+    served, got_hbm, own_hbm, from_1, from_2, from_3, out, sums, parted, got, own, from_all, sems
+):
+    copies = [pltpu.make_async_copy(own_hbm, own, sems.at[0])]
+    for i, ref in enumerate((from_1, from_2, from_3)):
+        copies.append(pltpu.make_async_copy(ref, from_all.at[i], sems.at[1 + i]))
+    last = pltpu.make_async_copy(got_hbm, got, sems.at[4])
+    for copy in copies + [last]:
+        copy.start()
+    for copy in copies:
+        copy.wait()
     n_x, n_z = served.shape[0], out.shape[0]
     wide = out.shape[1] - 16
     few = wide // 16
     size, rows = own.shape[0], n_z * few
     parts = size // 128
 
-    sides = (from_1, from_2, from_3)
-    exps = [real(ref[size : size + 8])[0:parts] for ref in sides]
+    sides = range(from_all.shape[0])
+    exps = [real(from_all[i, size : size + 8])[0:parts] for i in sides]
     down = jnp.transpose(tile_of(128, exps))
     down = scale_of(down) * (1.0 / LEVELS)
     for t in range(parts):
         part = slice(t * 128, (t + 1) * 128)
         total = own[part]
-        for i, ref in enumerate(sides):
+        for i in sides:
             lane = i * parts + t
-            total = total + real(ref[part]) * down[:, lane : lane + 1]
+            total = total + real(from_all[i, part]) * down[:, lane : lane + 1]
         sums[part] = total
 
+    last.wait()
     tiles = [real(got[d, rows : rows + 8]) for d in range(got.shape[0])]
     down = scale_of(upright([t[0:1] for t in tiles], rows)) * (1.0 / LEVELS)
     for d in range(got.shape[0]):
@@ -273,7 +293,7 @@
 
 
 def last_kernel(
-    scale, rate, tab, ft, second, moved, got, labels, logits, grads, mats, errs, sums
+    scale, rate, tab, ft, second, mats_in, got, first_sums, labels, logits, grads, mats, errs, sums
 ):
     samples = second.shape[1]
     few = grads.shape[0]
@@ -284,7 +304,8 @@
     down = scale_of(jnp.concatenate(exps, axis=0)) * (1.0 / LEVELS)
     value = scale * undigits(tiles, high)
     logits[...] = value
-    errs[...] = spread(jax.nn.sigmoid(value) - labels[...], samples)
+    errors = jax.nn.sigmoid(value) - labels[...]
+    errs[...] = spread(errors, samples)
     total = real(got[0, 0:wide]) * down[:, 0:1]
     for i in range(1, got.shape[0]):
         total = total + real(got[i, 0:wide]) * down[:, i : i + 1]
@@ -292,28 +313,33 @@
     for b in range(few):
         mine = errs[pl.ds(tab[MY_OWN, 0] * few + b, 1)]
         grads[b] = sums[pl.ds(b, 16, stride=few)] * mine
+    earlier = jax.nn.sigmoid(scale * total_of(first_sums)) - labels[...]
+    errs[...] = spread(errors + earlier, samples)
 
     def step(j, carry):
         live = tab[LIVE, j].astype(f32)
         weighted = split(ft[tab[FIRST, j]].astype(f32) * errs[...])
-        mats[tab[SLOT, j]] = moved[j] - (rate * live) * dot_lhs(weighted, second[j], ATB)
+        slot = tab[SLOT, j]
+        mats[slot] = mats_in[slot] - (rate * live) * dot_lhs(weighted, second[j], ATB)
         return carry
 
     lax.fori_loop(0, second.shape[0], step, 0, unroll=4)
 
 
-def call(kernel, outs, n_in, scratch=(), smem=True):
+def call(kernel, outs, n_in, scratch=(), smem=True, far_in=(), far_out=False, room=16):
     specs = [pl.BlockSpec(memory_space=pltpu.VMEM)] * n_in
     if smem:
         specs[0] = pl.BlockSpec(memory_space=pltpu.SMEM)
-    out_specs = [pl.BlockSpec(memory_space=pltpu.VMEM)] * len(outs)
+    for i in far_in:
+        specs[i] = pl.BlockSpec(memory_space=pltpu.HBM)
+    space = pltpu.HBM if far_out else pltpu.VMEM
     return pl.pallas_call(
         kernel,
         out_shape=outs,
         in_specs=specs,
-        out_specs=out_specs,
+        out_specs=[pl.BlockSpec(memory_space=space)] * len(outs),
         scratch_shapes=list(scratch),
-        compiler_params=pltpu.CompilerParams(vmem_limit_bytes=16 << 20),
+        compiler_params=pltpu.CompilerParams(vmem_limit_bytes=room << 20),
     )
 
 
@@ -363,10 +389,9 @@
     rows, wide = samples // n_x, per_block * few
     size = per_block * rows
     side = shape((size + 8, feature), jnp.int16)
-    moved, out, own, *sides = call(
+    out, own, *sides = call(
         functools.partial(terms_kernel, scale, rate),
         [
-            shape(mats.shape),
             shape((groups * n_x, rows + 8, feature), jnp.int16),
             shape((size, feature)),
             side,
@@ -380,7 +405,12 @@
             pltpu.VMEM((slots, samples, feature), f32),
             acc,
             pltpu.VMEM((n_x, size, feature), f32),
+            pltpu.VMEM((groups * n_x, rows + 8, feature), jnp.int16),
+            pltpu.VMEM((n_x - 1, size + 8, feature), jnp.int16),
+            pltpu.SemaphoreType.DMA((n_x + 1,)),
         ],
+        far_out=True,
+        room=60,
     )(tab, ft, second, mats, sums, targets)
     got = swap(out, GRP + ("x",))
     sides = [
@@ -388,15 +418,22 @@
         for r, side in enumerate(sides, 1)
     ]
     out = [shape((n_z, wide + 16, feature), jnp.int16)]
-    room = [pltpu.VMEM((size, feature), f32), pltpu.VMEM((n_z, wide, feature), f32)]
-    got = call(across_kernel, out, 6, room)(near, got, own, *sides)[0]
+    room = [
+        pltpu.VMEM((size, feature), f32),
+        pltpu.VMEM((n_z, wide, feature), f32),
+        pltpu.VMEM((groups * n_x, rows + 8, feature), jnp.int16),
+        pltpu.VMEM((size, feature), f32),
+        pltpu.VMEM((n_x - 1, size + 8, feature), jnp.int16),
+        pltpu.SemaphoreType.DMA((n_x + 1,)),
+    ]
+    got = call(across_kernel, out, 6, room, far_in=range(1, 6), room=16)(near, got, own, *sides)[0]
     got = swap(got, "z")
     logits, grads, mats = call(
         functools.partial(last_kernel, scale, rate),
         [shape((2, 128)), shape((few, per_block, feature)), shape(mats.shape)],
-        6,
+        7,
         [acc, pltpu.VMEM((per_block * few, 128), f32)],
-    )(tab, ft, second, moved, got, targets)
+    )(tab, ft, second, mats, got, sums, targets)
     return logits.reshape(256)[:samples], grads, mats[None, None]
 
 

time: 145 us -> 145 us (level)
  local copies, waits for them, and re-layouts: 5.36 us -> 2.62 us
  Pallas kernels: 18.4 us -> 21 us
    unnamed x21 -> x37, local copies, waits for them, and re-layouts: 5.31 us -> 2.01 us
    pallas_call x2, Pallas kernels: 10.4 us -> 12.9 us  [the longest x1 9.43 us: on_device(): call(functools.partial(terms_kernel, scale, rate), [shape((groups * n_x,...]
  transfers between devices with their start and end apart: 6 -> 6, of which waited for: 5 -> 6; matrix products, arithmetic and copies ran while one was open for 0% -> 0% of each run, Pallas kernels for 0% -> 0%
where the time goes in v5:
time: 145 us; the launch traced here: 143 us
  blocking collectives  52 us (36%)
  starting transfers between devices  34.5 us (24%)
  waiting for transfers between devices  31.5 us (22%)
  Pallas kernels  21 us (14%)
  local copies, waits for them, and re-layouts  2.62 us (2%)
  between operations  1.63 us (1%)
    all_to_all x2, blocking collectives, swap(): return lax.all_to_all(x, axes, split_axis=0, concat_axis=0, tiled=True)  52 us
    all_to_all x3, starting transfers between devices, swap(): return lax.all_to_all(x, axes, split_axis=0, concat_axis=0, tiled=True)  23.8 us
    all_to_all x3, waiting for transfers between devices, swap(): return lax.all_to_all(x, axes, split_axis=0, concat_axis=0, tiled=True)  20.4 us
    ppermute x3, waiting for transfers between devices, on_device(): lax.ppermute(side, 'x', [(i, (i + r) % n_x) for i in range(n_x)])  11.1 us
    ppermute x3, starting transfers between devices, on_device(): lax.ppermute(side, 'x', [(i, (i + r) % n_x) for i in range(n_x)])  10.7 us
    pallas_call x1, Pallas kernels, on_device(): call(functools.partial(terms_kernel, scale, rate), [shape((groups * n_x,...  9.43 us
    pallas_call x1, Pallas kernels, on_device(): call(across_kernel, out, 6, room, far_in=range(1, 6), room=16)  3.49 us
    pallas_call x1, Pallas kernels, on_device(): call(functools.partial(last_kernel, scale, rate), [shape((2, 128)), shape...  3.4 us
  transfers between devices with their start and end apart: 6, of which 6 were waited for; matrix products, arithmetic and copies ran while one was open for 0% of the time, Pallas kernels for 0%

profile of v5, /device:TPU:1, one launch (start us, length us, event | category | flops | bytes accessed | tf_op | source)
XLA Modules:
  0.0 143.3 jit_solution(17428819560676848269)
XLA Ops:
  0.6 0.0 copy-start.12
  0.7 0.0 copy-start.17
  1.4 0.1 select_reduce_fusion
  1.5 1.3 copy.11
  2.9 0.1 select_reduce_fusion.1
  3.0 0.8 shard_map.85
  3.8 0.0 copy-start.4
  3.8 36.2 %all_to_all.25.second = bf16[16,192,128]{2,1,0:T(8,128)(2,1)S(1)} all-to-all(bf16[16,192,128]{2,1,0:T(8,128)(2,1)S(1)} %shard_map.85), channel_id=1, replica_groups=mesh['y'=8,'core'=2,'x'=4,'z'=12] {'y','core'}, dimensions={0} | all-to-all | bytes 1572864 | tf_op jit(solution)/shard_map/all_to_all | solution.py:351
  40.1 2.6 %shard_map.86 = f32[64,2,128]{2,1,0:T(2,128)} custom-call(s32[7,16]{1,0:T(8,128)S(1)} %stack.16.tab, bf16[16,192,128]{2,1,0:T(8,128)(2,1)S(1)} %bitcast.21, bf16[16,192,128]{2,1,0:T(8,128)(2,1)S(1)} %all_to_all.25.second, f32[16,128,128]{2,1,0:T(8,128)S(1)} %bitcast.25), custom_call_target="tpu_custom_call" | custom-call | tf_op jit(solution)/shard_map/pallas_call | solution.py:384
  42.7 4.3 %all-to-all-start.1 = ((f32[64,2,128]{2,1,0:T(2,128)}), f32[64,2,128]{2,1,0:T(2,128)S(1)}, u32[]{:S(2)}, u32[]{:S(2)}) async-start(f32[64,2,128]{2,1,0:T(2,128)} %shard_map.86), calls=%async_computation.1 | async-start | bytes 131072 | tf_op jit(solution)/shard_map/all_to_all | solution.py:351
  47.0 8.5 %all-to-all-done.1.parts = f32[64,2,128]{2,1,0:T(2,128)S(1)} async-done(((f32[64,2,128]{2,1,0:T(2,128)}), f32[64,2,128]{2,1,0:T(2,128)S(1)}, u32[]{:S(2)}, u32[]{:S(2)}) %all-to-all-start.1) | async-done | bytes 65568 | tf_op jit(solution)/shard_map/all_to_all | solution.py:351
  55.6 1.3 shard_map.87
  56.8 12.6 %all-to-all-start.2 = ((f32[12,2,128]{2,1,0:T(2,128)}), f32[12,2,128]{2,1,0:T(2,128)S(1)}, u32[]{:S(2)}, u32[]{:S(2)}) async-start(f32[12,2,128]{2,1,0:T(2,128)} %get-tuple-element.14), calls=%async_computation.2 | async-start | bytes 24576 | tf_op jit(solution)/shard_map/all_to_all | solution.py:351
  69.4 0.6 pad_bitcast_fusion.labels
  70.0 8.4 %all-to-all-done.2.sums.first_sums = f32[12,2,128]{2,1,0:T(2,128)S(1)} async-done(((f32[12,2,128]{2,1,0:T(2,128)}), f32[12,2,128]{2,1,0:T(2,128)S(1)}, u32[]{:S(2)}, u32[]{:S(2)}) %all-to-all-start.2) | async-done | bytes 12320 | tf_op jit(solution)/shard_map/all_to_all | solution.py:351
  78.4 0.6 copy-done.9
  79.0 9.4 %shard_map.88 = (s16[64,56,128]{2,1,0:T(8,128)(2,1)}, f32[768,128]{1,0:T(8,128)}, s16[776,128]{1,0:T(8,128)(2,1)}, s16[776,128]{1,0:T(8,128)(2,1)}, s16[776,128]{1,0:T(8,128)(2,1)}) custom-call(s32[7,16]{1,0:T(8,128)} %copy-done.7, bf16[16,192,128]{2,1,0:T(8,128)(2,1)} %bitcast.22, bf16[16,192,128]{2,1,0:T(8,128)(2,1)} %copy-done.2, ...), custom_call_target="tpu_custom_call" | custom-call | tf_op jit(solution)/shard_map/pallas_call | solution.py:392
  88.5 6.9 %all-to-all-start.3 = ((s16[64,56,128]{2,1,0:T(8,128)(2,1)}), s16[64,56,128]{2,1,0:T(8,128)(2,1)S(1)}, u32[]{:S(2)}, u32[]{:S(2)}) async-start(s16[64,56,128]{2,1,0:T(8,128)(2,1)} %get-tuple-element.15), calls=%async_computation.3 | async-start | bytes 1835008 | tf_op jit(solution)/shard_map/all_to_all | solution.py:351
  95.4 3.3 %collective-permute-start = (s16[776,128]{1,0:T(8,128)(2,1)S(1)}, s16[776,128]{1,0:T(8,128)(2,1)S(1)}, u32[]{:S(2)}, u32[]{:S(2)}) collective-permute-start(s16[776,128]{1,0:T(8,128)(2,1)S(1)} %copy-done.16), channel_id=1, source_target_pairs={{0,12},{12,24},{24,36},{36,0},{1,13},{13,25},{25,37},{37,1},{2,14}... | collective-permute-start | bytes 595976 | tf_op jit(solution)/shard_map/ppermute | solution.py:417
  98.7 4.3 %collective-permute-start.1 = (s16[776,128]{1,0:T(8,128)(2,1)S(1)}, s16[776,128]{1,0:T(8,128)(2,1)S(1)}, u32[]{:S(2)}, u32[]{:S(2)}) collective-permute-start(s16[776,128]{1,0:T(8,128)(2,1)S(1)} %copy-done.15), channel_id=1, source_target_pairs={{0,24},{12,36},{24,0},{36,12},{1,25},{13,37},{25,1},{37,13},{2,26}... | collective-permute-start | bytes 595976 | tf_op jit(solution)/shard_map/ppermute | solution.py:417
  103.0 0.0 copy-done.14
  103.0 3.1 %collective-permute-start.2 = (s16[776,128]{1,0:T(8,128)(2,1)S(1)}, s16[776,128]{1,0:T(8,128)(2,1)S(1)}, u32[]{:S(2)}, u32[]{:S(2)}) collective-permute-start(s16[776,128]{1,0:T(8,128)(2,1)S(1)} %copy-done.14), channel_id=1, source_target_pairs={{0,36},{12,0},{24,12},{36,24},{1,37},{13,1},{25,13},{37,25},{2,38}... | collective-permute-start | bytes 595976 | tf_op jit(solution)/shard_map/ppermute | solution.py:417
  106.1 2.0 %collective-permute-done.from_1 = s16[776,128]{1,0:T(8,128)(2,1)S(1)} collective-permute-done((s16[776,128]{1,0:T(8,128)(2,1)S(1)}, s16[776,128]{1,0:T(8,128)(2,1)S(1)}, u32[]{:S(2)}, u32[]{:S(2)}) %collective-permute-start) | collective-permute-done | bytes 198688 | tf_op jit(solution)/shard_map/ppermute | solution.py:417
  108.1 8.8 %collective-permute-done.1.from_2 = s16[776,128]{1,0:T(8,128)(2,1)S(1)} collective-permute-done((s16[776,128]{1,0:T(8,128)(2,1)S(1)}, s16[776,128]{1,0:T(8,128)(2,1)S(1)}, u32[]{:S(2)}, u32[]{:S(2)}) %collective-permute-start.1) | collective-permute-done | bytes 198688 | tf_op jit(solution)/shard_map/ppermute | solution.py:417
  116.9 0.3 collective-permute-done.2.from_3
  117.2 3.5 %all-to-all-done.3.got_hbm = s16[64,56,128]{2,1,0:T(8,128)(2,1)S(1)} async-done(((s16[64,56,128]{2,1,0:T(8,128)(2,1)}), s16[64,56,128]{2,1,0:T(8,128)(2,1)S(1)}, u32[]{:S(2)}, u32[]{:S(2)}) %all-to-all-start.3) | async-done | bytes 917536 | tf_op jit(solution)/shard_map/all_to_all | solution.py:351
  120.7 3.5 %shard_map.89 = s16[12,80,128]{2,1,0:T(8,128)(2,1)S(1)} custom-call(s32[4,128]{1,0:T(4,128)S(1)} %get-tuple-element.13.served, s16[64,56,128]{2,1,0:T(8,128)(2,1)S(1)} %all-to-all-done.3.got_hbm, f32[768,128]{1,0:T(8,128)S(1)} %copy-done.6, s16[776,128]{1,0:T(8,128)(2,1)S(1)} %collective-permute-done.from_1, ...), custom_call_target="tpu_custom_call" | custom-call | tf_op jit(solution)/shard_map/pallas_call | solution.py:429
  124.2 0.0 copy-start.10
  124.2 0.0 copy-start.11
  124.2 15.7 %all_to_all.26.got = s16[12,80,128]{2,1,0:T(8,128)(2,1)S(1)} all-to-all(s16[12,80,128]{2,1,0:T(8,128)(2,1)S(1)} %shard_map.89), channel_id=1, replica_groups=mesh['y'=8,'core'=2,'x'=4,'z'=12] {'z'}, dimensions={0} | all-to-all | bytes 491520 | tf_op jit(solution)/shard_map/all_to_all | solution.py:351
  139.9 0.0 copy-done.3
  139.9 3.4 %shard_map.90 = (f32[2,128]{1,0:T(2,128)}, f32[4,16,128]{2,1,0:T(8,128)}, f32[16,128,128]{2,1,0:T(8,128)}) custom-call(s32[7,16]{1,0:T(8,128)S(1)} %copy-done.8, bf16[16,192,128]{2,1,0:T(8,128)(2,1)S(1)} %bitcast.23, bf16[16,192,128]{2,1,0:T(8,128)(2,1)S(1)} %copy-done.3, f32[16,128,128]{2,1,0:T(8,128)S(1)} %bitcast.26, ...), custom_call_target="tpu_custom_call" | custom-call | tf_op jit(solution)/shard_map/pallas_call | solution.py:431
  (36 shorter events, 0.1 us)
Async XLA Ops:
  0.6 0.7 copy-start.12
  0.7 0.7 copy-start.17
  2.8 37.2 %copy-start = (bf16[192,16,128]{2,0,1:T(8,128)(2,1)}, bf16[192,16,128]{2,0,1:T(8,128)(2,1)S(1)}, u32[]{:S(2)}) copy-start(bf16[192,16,128]{2,0,1:T(8,128)(2,1)S(1)} %copy.11) | copy-start | bytes 2359300
  3.0 52.5 %copy-start.7 = (s32[7,16]{1,0:T(8,128)}, s32[7,16]{1,0:T(8,128)S(1)}, u32[]{:S(2)}) copy-start(s32[7,16]{1,0:T(8,128)S(1)} %stack.16.tab) | copy-start | bytes 1348
  3.8 36.3 %copy-start.4 = (f32[1,1,16,128,128]{4,3,2,1,0:T(8,128)S(1)}, f32[1,1,16,128,128]{4,3,2,1,0:T(8,128)}, u32[]{:S(2)}) copy-start(f32[1,1,16,128,128]{4,3,2,1,0:T(8,128)} %param.11) | copy-start | bytes 3145732
  40.1 2.6 %copy-start.2 = (bf16[16,192,128]{2,1,0:T(8,128)(2,1)}, bf16[16,192,128]{2,1,0:T(8,128)(2,1)S(1)}, u32[]{:S(2)}) copy-start(bf16[16,192,128]{2,1,0:T(8,128)(2,1)S(1)} %all_to_all.25.second) | copy-start | bytes 2359300
  42.7 4.3 %copy-start.13 = (s32[192]{0:T(256)S(1)}, s32[192]{0:T(256)}, u32[]{:S(2)}) copy-start(s32[192]{0:T(256)} %param.7) | copy-start | bytes 2308
  42.7 12.9 %all-to-all-start.1 = ((f32[64,2,128]{2,1,0:T(2,128)}), f32[64,2,128]{2,1,0:T(2,128)S(1)}, u32[]{:S(2)}, u32[]{:S(2)}) async-start(f32[64,2,128]{2,1,0:T(2,128)} %shard_map.86), calls=%async_computation.1 | async-start | bytes 131072 | tf_op jit(solution)/shard_map/all_to_all | solution.py:351
  56.8 21.5 %all-to-all-start.2 = ((f32[12,2,128]{2,1,0:T(2,128)}), f32[12,2,128]{2,1,0:T(2,128)S(1)}, u32[]{:S(2)}, u32[]{:S(2)}) async-start(f32[12,2,128]{2,1,0:T(2,128)} %get-tuple-element.14), calls=%async_computation.2 | async-start | bytes 24576 | tf_op jit(solution)/shard_map/all_to_all | solution.py:351
  78.4 0.6 copy-start.9
  88.4 7.0 %copy-start.16 = (s16[776,128]{1,0:T(8,128)(2,1)S(1)}, s16[776,128]{1,0:T(8,128)(2,1)}, u32[]{:S(2)}) copy-start(s16[776,128]{1,0:T(8,128)(2,1)} %get-tuple-element.17) | copy-start | bytes 595972
  88.4 10.3 %copy-start.15 = (s16[776,128]{1,0:T(8,128)(2,1)S(1)}, s16[776,128]{1,0:T(8,128)(2,1)}, u32[]{:S(2)}) copy-start(s16[776,128]{1,0:T(8,128)(2,1)} %get-tuple-element.18) | copy-start | bytes 595972
  88.4 14.6 %copy-start.14 = (s16[776,128]{1,0:T(8,128)(2,1)S(1)}, s16[776,128]{1,0:T(8,128)(2,1)}, u32[]{:S(2)}) copy-start(s16[776,128]{1,0:T(8,128)(2,1)} %get-tuple-element.19) | copy-start | bytes 595972
  88.4 32.2 %copy-start.6 = (f32[768,128]{1,0:T(8,128)S(1)}, f32[768,128]{1,0:T(8,128)}, u32[]{:S(2)}) copy-start(f32[768,128]{1,0:T(8,128)} %get-tuple-element.16.own_hbm) | copy-start | bytes 1179652
  88.5 32.2 %all-to-all-start.3 = ((s16[64,56,128]{2,1,0:T(8,128)(2,1)}), s16[64,56,128]{2,1,0:T(8,128)(2,1)S(1)}, u32[]{:S(2)}, u32[]{:S(2)}) async-start(s16[64,56,128]{2,1,0:T(8,128)(2,1)} %get-tuple-element.15), calls=%async_computation.3 | async-start | bytes 1835008 | tf_op jit(solution)/shard_map/all_to_all | solution.py:351
  95.4 12.7 %collective-permute-start = (s16[776,128]{1,0:T(8,128)(2,1)S(1)}, s16[776,128]{1,0:T(8,128)(2,1)S(1)}, u32[]{:S(2)}, u32[]{:S(2)}) collective-permute-start(s16[776,128]{1,0:T(8,128)(2,1)S(1)} %copy-done.16), channel_id=1, source_target_pairs={{0,12},{12,24},{24,36},{36,0},{1,13},{13,25},{25,37},{37,1},{2,14}... | collective-permute-start | bytes 595976 | tf_op jit(solution)/shard_map/ppermute | solution.py:417
  98.7 18.2 %collective-permute-start.1 = (s16[776,128]{1,0:T(8,128)(2,1)S(1)}, s16[776,128]{1,0:T(8,128)(2,1)S(1)}, u32[]{:S(2)}, u32[]{:S(2)}) collective-permute-start(s16[776,128]{1,0:T(8,128)(2,1)S(1)} %copy-done.15), channel_id=1, source_target_pairs={{0,24},{12,36},{24,0},{36,12},{1,25},{13,37},{25,1},{37,13},{2,26}... | collective-permute-start | bytes 595976 | tf_op jit(solution)/shard_map/ppermute | solution.py:417
  103.0 14.2 %collective-permute-start.2 = (s16[776,128]{1,0:T(8,128)(2,1)S(1)}, s16[776,128]{1,0:T(8,128)(2,1)S(1)}, u32[]{:S(2)}, u32[]{:S(2)}) collective-permute-start(s16[776,128]{1,0:T(8,128)(2,1)S(1)} %copy-done.14), channel_id=1, source_target_pairs={{0,36},{12,0},{24,12},{36,24},{1,37},{13,1},{25,13},{37,25},{2,38}... | collective-permute-start | bytes 595976 | tf_op jit(solution)/shard_map/ppermute | solution.py:417
  120.6 19.3 %copy-start.1 = (bf16[192,16,128]{2,0,1:T(8,128)(2,1)S(1)}, bf16[192,16,128]{2,0,1:T(8,128)(2,1)}, u32[]{:S(2)}) copy-start(bf16[192,16,128]{2,0,1:T(8,128)(2,1)} %copy-done) | copy-start | bytes 2359300
  120.6 19.3 %copy-start.3 = (bf16[16,192,128]{2,1,0:T(8,128)(2,1)S(1)}, bf16[16,192,128]{2,1,0:T(8,128)(2,1)}, u32[]{:S(2)}) copy-start(bf16[16,192,128]{2,1,0:T(8,128)(2,1)} %copy-done.2) | copy-start | bytes 2359300
  120.6 19.3 %copy-start.5 = (f32[1,1,16,128,128]{4,3,2,1,0:T(8,128)S(1)}, f32[1,1,16,128,128]{4,3,2,1,0:T(8,128)}, u32[]{:S(2)}) copy-start(f32[1,1,16,128,128]{4,3,2,1,0:T(8,128)} %param.11) | copy-start | bytes 3145732
  124.2 15.8 %copy-start.8 = (s32[7,16]{1,0:T(8,128)S(1)}, s32[7,16]{1,0:T(8,128)}, u32[]{:S(2)}) copy-start(s32[7,16]{1,0:T(8,128)} %copy-done.7) | copy-start | bytes 1348
  124.2 15.8 %copy-start.10 = (f32[12,2,128]{2,1,0:T(2,128)S(1)}, f32[12,2,128]{2,1,0:T(2,128)}, u32[]{:S(2)}) copy-start(f32[12,2,128]{2,1,0:T(2,128)} %copy-done.9) | copy-start | bytes 36868
  124.2 15.8 %copy-start.11 = (f32[2,128]{1,0:T(2,128)S(1)}, f32[2,128]{1,0:T(2,128)}, u32[]{:S(2)}) copy-start(f32[2,128]{1,0:T(2,128)} %pad_bitcast_fusion.labels) | copy-start | bytes 3076

commit v6 on v5

--- a/solution.py
+++ b/solution.py
@@ -16,7 +16,9 @@
 f32 = jnp.float32
 bf16 = jnp.bfloat16
 
-SLOT, FIRST, LIVE, SERVED, MY_OWN, MY_GRP, MY_X = range(7)
+SLOT, FIRST, LIVE, SERVED, MY_OWN, MY_X = range(6)
+
+PARTIAL_GROUP, TERMS_GROUP, LAST_GROUP = 16, 8, 16
 SPARE = 64
 
 
@@ -29,12 +31,12 @@
     return lax.dot_general(a, b, (dims, ((), ())), preferred_element_type=f32)
 
 
-def dot_rhs(a, pair, dims):
-    return dot(a, pair[0], dims) + dot(a, pair[1], dims)
-
-
-def dot_lhs(pair, b, dims):
-    return dot(pair[0], b, dims) + dot(pair[1], b, dims)
+def beside(x):
+    return jnp.concatenate(split(x), axis=1)
+
+
+def twice(x):
+    return jnp.concatenate([x, x], axis=1)
 
 
 AB, ABT, ATB = ((1,), (0,)), ((1,), (1,)), ((0,), (0,))
@@ -69,13 +71,22 @@
 def partial_kernel(tab, ft, second, mats, out, acc):
     acc[...] = jnp.zeros_like(acc)
 
-    def step(j, carry):
-        live = tab[LIVE, j].astype(f32)
-        mixed = dot_rhs(ft[tab[FIRST, j]], split(mats[tab[SLOT, j]] * live), AB)
-        acc[...] += mixed * second[j].astype(f32)
+    group = math.gcd(PARTIAL_GROUP, second.shape[0])
+
+    def step(q, carry):
+        js = [q * group + i for i in range(group)]
+        pairs = [split(mats[tab[SLOT, j]] * tab[LIVE, j].astype(f32)) for j in js]
+        mixed = [
+            dot(twice(ft[tab[FIRST, j]]), jnp.concatenate(pair, axis=0), AB)
+            for j, pair in zip(js, pairs)
+        ]
+        total = acc[...]
+        for j, m in zip(js, mixed):
+            total = total + m * second[j].astype(f32)
+        acc[...] = total
         return carry
 
-    lax.fori_loop(0, second.shape[0], step, 0, unroll=4)
+    lax.fori_loop(0, second.shape[0] // group, step, 0)
     chunk = row_sums(acc[...] * (1.0 / 128.0))
     lanes = iota((2, 128), 1) + 128 * (1 - iota((2, 128), 0))
     for j in range(second.shape[0]):
@@ -84,12 +95,12 @@
         out[i] = chunk
 
 
-def sum_kernel(tab, parts, out, served):
+def sum_kernel(parts, out, served):
     total = total_of(parts)
     for i in range(out.shape[0]):
         out[i] = total
     n_x = served.shape[0]
-    near = parts[pl.ds(tab[MY_GRP, 0] * n_x, n_x)]
+    near = parts[pl.ds(lax.axis_index(GRP) * n_x, n_x)]
     lanes = iota((1, 128), 1)
     mine = (lanes >= SPARE) & (lanes < SPARE + 16)
     for i in range(n_x):
@@ -174,24 +185,41 @@
     tops[...] = jnp.zeros_like(tops)
     lanes = iota((samples, 128), 1)
 
-    def step(j, carry):
-        live = tab[LIVE, j].astype(f32)
-        slot, first = tab[SLOT, j], tab[FIRST, j]
-        va, vb = ft[first], second[j]
-        gradient = dot_lhs(split(va.astype(f32) * errs[...]), vb, ATB)
-        updated = mats[slot] - (rate * live) * gradient
-        pair = split(updated * live)
-        mixed = dot_rhs(va, pair, AB)
-        acc[...] += mixed * vb.astype(f32)
-        stash[j] = mixed
-        tops[...] = jnp.where(lanes == j, peaks(mixed), tops[...])
-        toward = dot_rhs(vb, pair, ABT)
-        at = pl.ds(pl.multiple_of(first * rows, 8), rows)
-        for i in range(n_x):
-            dense[i, at] += toward[i * rows : (i + 1) * rows]
+    group = math.gcd(TERMS_GROUP, second.shape[0])
+
+    def step(q, carry):
+        js = [q * group + i for i in range(group)]
+        lives = [tab[LIVE, j].astype(f32) for j in js]
+        slots = [tab[SLOT, j] for j in js]
+        firsts = [tab[FIRST, j] for j in js]
+        vas, vbs = [ft[first] for first in firsts], [second[j] for j in js]
+        e = errs[...]
+        both = [dot(va, beside(vb.astype(f32) * e), ATB) for va, vb in zip(vas, vbs)]
+        updated = [
+            (mats[slot] - (rate * live) * (g[:, :128] + g[:, 128:])) * live
+            for slot, live, g in zip(slots, lives, both)
+        ]
+        pairs = [split(m) for m in updated]
+        mixed = [
+            dot(twice(va), jnp.concatenate(pair, axis=0), AB) for va, pair in zip(vas, pairs)
+        ]
+        toward = [
+            dot(twice(vb), jnp.concatenate(pair, axis=1), ABT) for vb, pair in zip(vbs, pairs)
+        ]
+        total, top = acc[...], tops[...]
+        for j, m, vb in zip(js, mixed, vbs):
+            stash[j] = m
+            total = total + m * vb.astype(f32)
+            top = jnp.where(lanes == j, peaks(m), top)
+        acc[...] = total
+        tops[...] = top
+        for first, t in zip(firsts, toward):
+            at = pl.ds(pl.multiple_of(first * rows, 8), rows)
+            for i in range(n_x):
+                dense[i, at] += t[i * rows : (i + 1) * rows]
         return carry
 
-    lax.fori_loop(0, second.shape[0], step, 0, unroll=2)
+    lax.fori_loop(0, second.shape[0] // group, step, 0)
 
     x = tab[MY_X, 0]
     copies = [pltpu.make_async_copy(dense.at[x], own_hbm, sems.at[0])]
@@ -267,11 +295,12 @@
     last.wait()
     tiles = [real(got[d, rows : rows + 8]) for d in range(got.shape[0])]
     down = scale_of(upright([t[0:1] for t in tiles], rows)) * (1.0 / LEVELS)
-    for d in range(got.shape[0]):
-        field = served[d % n_x, SPARE + d // n_x]
-        at = pl.ds(pl.multiple_of(field * rows, 8), rows)
-        sums[at] += real(got[d, 0:rows]) * down[:, d : d + 1]
-
+    for q in range(0, got.shape[0], 8):
+        values = [real(got[d, 0:rows]) * down[:, d : d + 1] for d in range(q, q + 8)]
+        for d, value in zip(range(q, q + 8), values):
+            field = served[d % n_x, SPARE + d // n_x]
+            at = pl.ds(pl.multiple_of(field * rows, 8), rows)
+            sums[at] += value
     for f in range(16):
         for z in range(n_z):
             start = f * rows + z * few
@@ -316,14 +345,18 @@
     earlier = jax.nn.sigmoid(scale * total_of(first_sums)) - labels[...]
     errs[...] = spread(errors + earlier, samples)
 
-    def step(j, carry):
-        live = tab[LIVE, j].astype(f32)
-        weighted = split(ft[tab[FIRST, j]].astype(f32) * errs[...])
-        slot = tab[SLOT, j]
-        mats[slot] = mats_in[slot] - (rate * live) * dot_lhs(weighted, second[j], ATB)
+    group = math.gcd(LAST_GROUP, second.shape[0])
+
+    def step(q, carry):
+        js = [q * group + i for i in range(group)]
+        e = errs[...]
+        both = [dot(ft[tab[FIRST, j]], beside(second[j].astype(f32) * e), ATB) for j in js]
+        for j, g in zip(js, both):
+            slot, live = tab[SLOT, j], tab[LIVE, j].astype(f32)
+            mats[slot] = mats_in[slot] - (rate * live) * (g[:, :128] + g[:, 128:])
         return carry
 
-    lax.fori_loop(0, second.shape[0], step, 0, unroll=4)
+    lax.fori_loop(0, second.shape[0] // group, step, 0)
 
 
 def call(kernel, outs, n_in, scratch=(), smem=True, far_in=(), far_out=False, room=16):
@@ -370,7 +403,7 @@
     slot_of = jnp.sum(jnp.where(picked, slot_ids, 0), axis=0)
     first_of = jnp.sum(jnp.where(picked, (pair_first[0, 0] - me * per_block)[:, None], 0), axis=0)
     live = (slot_of < pair_count[0, 0]).astype(jnp.int32)
-    places = [lax.axis_index(OWN), me, lax.axis_index("x")]
+    places = [lax.axis_index(OWN), lax.axis_index("x")]
     places = [jnp.full((slots,), place, jnp.int32) for place in places]
     tab = jnp.stack([slot_of, first_of, live, served] + places)
 
@@ -383,7 +416,7 @@
     acc = pltpu.VMEM((samples, 128), f32)
     part = call(partial_kernel, [shape((groups * n_x, 2, 128))], 4, [acc])(tab, ft, second, mats)[0]
     out = [shape((n_z, 2, 128)), shape((n_x, 128), jnp.int32)]
-    part, near = call(sum_kernel, out, 2)(tab, swap(part, GRP + ("x",)))
+    part, near = call(sum_kernel, out, 1, smem=False)(swap(part, GRP + ("x",)))
     sums = swap(part, "z")
 
     rows, wide = samples // n_x, per_block * few

time: 145 us -> 140 us (0.966)
  Pallas kernels: 21 us -> 15.3 us
    pallas_call x1, Pallas kernels: 9.43 us -> 5.96 us  [on_device(): call(functools.partial(terms_kernel, scale, rate), [shape((groups * n_x,...]
where the time goes in v6:
time: 140 us; the launch traced here: 138 us
  blocking collectives  52 us (37%)
  starting transfers between devices  34.5 us (25%)
  waiting for transfers between devices  31.5 us (22%)
  Pallas kernels  15.3 us (11%)
  local copies, waits for them, and re-layouts  2.62 us (2%)
  between operations  1.62 us (1%)
    all_to_all x2, blocking collectives, swap(): return lax.all_to_all(x, axes, split_axis=0, concat_axis=0, tiled=True)  52 us
    all_to_all x3, starting transfers between devices, swap(): return lax.all_to_all(x, axes, split_axis=0, concat_axis=0, tiled=True)  23.8 us
    all_to_all x3, waiting for transfers between devices, swap(): return lax.all_to_all(x, axes, split_axis=0, concat_axis=0, tiled=True)  20.4 us
    ppermute x3, waiting for transfers between devices, on_device(): lax.ppermute(side, 'x', [(i, (i + r) % n_x) for i in range(n_x)])  11.1 us
    ppermute x3, starting transfers between devices, on_device(): lax.ppermute(side, 'x', [(i, (i + r) % n_x) for i in range(n_x)])  10.7 us
    pallas_call x1, Pallas kernels, on_device(): call(functools.partial(terms_kernel, scale, rate), [shape((groups * n_x,...  5.96 us
    pallas_call x1, Pallas kernels, on_device(): call(across_kernel, out, 6, room, far_in=range(1, 6), room=16)  3.49 us
  transfers between devices with their start and end apart: 6, of which 6 were waited for; matrix products, arithmetic and copies ran while one was open for 0% of the time, Pallas kernels for 0%

profile of v6, /device:TPU:1, one launch (start us, length us, event | category | flops | bytes accessed | tf_op | source)
XLA Modules:
  0.0 137.7 jit_solution(18011437466262820679)
XLA Ops:
  1.4 0.1 select_reduce_fusion
  1.5 1.3 copy.11
  2.9 0.1 select_reduce_fusion.1
  3.0 0.8 shard_map.85
  3.8 0.0 copy-start.4
  3.8 36.2 %all_to_all.25.second = bf16[16,192,128]{2,1,0:T(8,128)(2,1)S(1)} all-to-all(bf16[16,192,128]{2,1,0:T(8,128)(2,1)S(1)} %shard_map.85), channel_id=1, replica_groups=mesh['y'=8,'core'=2,'x'=4,'z'=12] {'y','core'}, dimensions={0} | all-to-all | bytes 1572864 | tf_op jit(solution)/shard_map/all_to_all | solution.py:384
  40.0 0.0 copy-done.9
  40.1 2.1 %shard_map.86 = f32[64,2,128]{2,1,0:T(2,128)} custom-call(s32[6,16]{1,0:T(8,128)S(1)} %stack.16.tab, bf16[16,192,128]{2,1,0:T(8,128)(2,1)S(1)} %bitcast.21, bf16[16,192,128]{2,1,0:T(8,128)(2,1)S(1)} %all_to_all.25.second, f32[16,128,128]{2,1,0:T(8,128)S(1)} %bitcast.25), custom_call_target="tpu_custom_call" | custom-call | tf_op jit(solution)/shard_map/pallas_call | solution.py:417
  42.2 4.3 %all-to-all-start.1 = ((f32[64,2,128]{2,1,0:T(2,128)}), f32[64,2,128]{2,1,0:T(2,128)S(1)}, u32[]{:S(2)}, u32[]{:S(2)}) async-start(f32[64,2,128]{2,1,0:T(2,128)} %shard_map.86), calls=%async_computation.1 | async-start | bytes 131072 | tf_op jit(solution)/shard_map/all_to_all | solution.py:384
  46.6 8.5 %all-to-all-done.1.parts = f32[64,2,128]{2,1,0:T(2,128)S(1)} async-done(((f32[64,2,128]{2,1,0:T(2,128)}), f32[64,2,128]{2,1,0:T(2,128)S(1)}, u32[]{:S(2)}, u32[]{:S(2)}) %all-to-all-start.1) | async-done | bytes 65568 | tf_op jit(solution)/shard_map/all_to_all | solution.py:384
  55.1 0.7 shard_map.87
  55.8 12.6 %all-to-all-start.2 = ((f32[12,2,128]{2,1,0:T(2,128)}), f32[12,2,128]{2,1,0:T(2,128)S(1)}, u32[]{:S(2)}, u32[]{:S(2)}) async-start(f32[12,2,128]{2,1,0:T(2,128)} %get-tuple-element.14), calls=%async_computation.2 | async-start | bytes 24576 | tf_op jit(solution)/shard_map/all_to_all | solution.py:384
  68.3 0.6 pad_bitcast_fusion.labels
  68.9 8.4 %all-to-all-done.2.sums.first_sums = f32[12,2,128]{2,1,0:T(2,128)S(1)} async-done(((f32[12,2,128]{2,1,0:T(2,128)}), f32[12,2,128]{2,1,0:T(2,128)S(1)}, u32[]{:S(2)}, u32[]{:S(2)}) %all-to-all-start.2) | async-done | bytes 12320 | tf_op jit(solution)/shard_map/all_to_all | solution.py:384
  77.3 0.6 copy-done.7
  77.9 6.0 %shard_map.88 = (s16[64,56,128]{2,1,0:T(8,128)(2,1)}, f32[768,128]{1,0:T(8,128)}, s16[776,128]{1,0:T(8,128)(2,1)}, s16[776,128]{1,0:T(8,128)(2,1)}, s16[776,128]{1,0:T(8,128)(2,1)}) custom-call(s32[6,16]{1,0:T(8,128)} %copy-done.9, bf16[16,192,128]{2,1,0:T(8,128)(2,1)} %bitcast.22, bf16[16,192,128]{2,1,0:T(8,128)(2,1)} %copy-done.2, ...), custom_call_target="tpu_custom_call" | custom-call | tf_op jit(solution)/shard_map/pallas_call | solution.py:425
  83.9 6.9 %all-to-all-start.3 = ((s16[64,56,128]{2,1,0:T(8,128)(2,1)}), s16[64,56,128]{2,1,0:T(8,128)(2,1)S(1)}, u32[]{:S(2)}, u32[]{:S(2)}) async-start(s16[64,56,128]{2,1,0:T(8,128)(2,1)} %get-tuple-element.15), calls=%async_computation.3 | async-start | bytes 1835008 | tf_op jit(solution)/shard_map/all_to_all | solution.py:384
  90.8 0.0 copy-done.16
  90.9 3.3 %collective-permute-start = (s16[776,128]{1,0:T(8,128)(2,1)S(1)}, s16[776,128]{1,0:T(8,128)(2,1)S(1)}, u32[]{:S(2)}, u32[]{:S(2)}) collective-permute-start(s16[776,128]{1,0:T(8,128)(2,1)S(1)} %copy-done.16), channel_id=1, source_target_pairs={{0,12},{12,24},{24,36},{36,0},{1,13},{13,25},{25,37},{37,1},{2,14}... | collective-permute-start | bytes 595976 | tf_op jit(solution)/shard_map/ppermute | solution.py:450
  94.1 0.0 copy-done.15
  94.2 4.3 %collective-permute-start.1 = (s16[776,128]{1,0:T(8,128)(2,1)S(1)}, s16[776,128]{1,0:T(8,128)(2,1)S(1)}, u32[]{:S(2)}, u32[]{:S(2)}) collective-permute-start(s16[776,128]{1,0:T(8,128)(2,1)S(1)} %copy-done.15), channel_id=1, source_target_pairs={{0,24},{12,36},{24,0},{36,12},{1,25},{13,37},{25,1},{37,13},{2,26}... | collective-permute-start | bytes 595976 | tf_op jit(solution)/shard_map/ppermute | solution.py:450
  98.5 0.0 copy-done.14
  98.5 3.1 %collective-permute-start.2 = (s16[776,128]{1,0:T(8,128)(2,1)S(1)}, s16[776,128]{1,0:T(8,128)(2,1)S(1)}, u32[]{:S(2)}, u32[]{:S(2)}) collective-permute-start(s16[776,128]{1,0:T(8,128)(2,1)S(1)} %copy-done.14), channel_id=1, source_target_pairs={{0,36},{12,0},{24,12},{36,24},{1,37},{13,1},{25,13},{37,25},{2,38}... | collective-permute-start | bytes 595976 | tf_op jit(solution)/shard_map/ppermute | solution.py:450
  101.6 2.0 %collective-permute-done.from_1 = s16[776,128]{1,0:T(8,128)(2,1)S(1)} collective-permute-done((s16[776,128]{1,0:T(8,128)(2,1)S(1)}, s16[776,128]{1,0:T(8,128)(2,1)S(1)}, u32[]{:S(2)}, u32[]{:S(2)}) %collective-permute-start) | collective-permute-done | bytes 198688 | tf_op jit(solution)/shard_map/ppermute | solution.py:450
  103.6 8.8 %collective-permute-done.1.from_2 = s16[776,128]{1,0:T(8,128)(2,1)S(1)} collective-permute-done((s16[776,128]{1,0:T(8,128)(2,1)S(1)}, s16[776,128]{1,0:T(8,128)(2,1)S(1)}, u32[]{:S(2)}, u32[]{:S(2)}) %collective-permute-start.1) | collective-permute-done | bytes 198688 | tf_op jit(solution)/shard_map/ppermute | solution.py:450
  112.4 0.3 collective-permute-done.2.from_3
  112.6 3.5 %all-to-all-done.3.got_hbm = s16[64,56,128]{2,1,0:T(8,128)(2,1)S(1)} async-done(((s16[64,56,128]{2,1,0:T(8,128)(2,1)}), s16[64,56,128]{2,1,0:T(8,128)(2,1)S(1)}, u32[]{:S(2)}, u32[]{:S(2)}) %all-to-all-start.3) | async-done | bytes 917536 | tf_op jit(solution)/shard_map/all_to_all | solution.py:384
  116.1 3.5 %shard_map.89 = s16[12,80,128]{2,1,0:T(8,128)(2,1)S(1)} custom-call(s32[4,128]{1,0:T(4,128)S(1)} %get-tuple-element.13.served, s16[64,56,128]{2,1,0:T(8,128)(2,1)S(1)} %all-to-all-done.3.got_hbm, f32[768,128]{1,0:T(8,128)S(1)} %copy-done.6, s16[776,128]{1,0:T(8,128)(2,1)S(1)} %collective-permute-done.from_1, ...), custom_call_target="tpu_custom_call" | custom-call | tf_op jit(solution)/shard_map/pallas_call | solution.py:462
  119.6 0.0 copy-start.8
  119.6 0.0 copy-start.11
  119.6 15.7 %all_to_all.26.got = s16[12,80,128]{2,1,0:T(8,128)(2,1)S(1)} all-to-all(s16[12,80,128]{2,1,0:T(8,128)(2,1)S(1)} %shard_map.89), channel_id=1, replica_groups=mesh['y'=8,'core'=2,'x'=4,'z'=12] {'z'}, dimensions={0} | all-to-all | bytes 491520 | tf_op jit(solution)/shard_map/all_to_all | solution.py:384
  135.4 2.3 %shard_map.90 = (f32[2,128]{1,0:T(2,128)}, f32[4,16,128]{2,1,0:T(8,128)}, f32[16,128,128]{2,1,0:T(8,128)}) custom-call(s32[6,16]{1,0:T(8,128)S(1)} %copy-done.10, bf16[16,192,128]{2,1,0:T(8,128)(2,1)S(1)} %bitcast.23, bf16[16,192,128]{2,1,0:T(8,128)(2,1)S(1)} %copy-done.3, f32[16,128,128]{2,1,0:T(8,128)S(1)} %bitcast.26, ...), custom_call_target="tpu_custom_call" | custom-call | tf_op jit(solution)/shard_map/pallas_call | solution.py:464
  (35 shorter events, 0.1 us)
Async XLA Ops:
  0.6 0.7 copy-start.12
  0.7 0.7 copy-start.17
  2.8 37.2 %copy-start = (bf16[192,16,128]{2,0,1:T(8,128)(2,1)}, bf16[192,16,128]{2,0,1:T(8,128)(2,1)S(1)}, u32[]{:S(2)}) copy-start(bf16[192,16,128]{2,0,1:T(8,128)(2,1)S(1)} %copy.11) | copy-start | bytes 2359300
  3.0 37.0 %copy-start.9 = (s32[6,16]{1,0:T(8,128)}, s32[6,16]{1,0:T(8,128)S(1)}, u32[]{:S(2)}) copy-start(s32[6,16]{1,0:T(8,128)S(1)} %stack.16.tab) | copy-start | bytes 1156
  3.8 36.3 %copy-start.4 = (f32[1,1,16,128,128]{4,3,2,1,0:T(8,128)S(1)}, f32[1,1,16,128,128]{4,3,2,1,0:T(8,128)}, u32[]{:S(2)}) copy-start(f32[1,1,16,128,128]{4,3,2,1,0:T(8,128)} %param.11) | copy-start | bytes 3145732
  40.0 2.2 %copy-start.2 = (bf16[16,192,128]{2,1,0:T(8,128)(2,1)}, bf16[16,192,128]{2,1,0:T(8,128)(2,1)S(1)}, u32[]{:S(2)}) copy-start(bf16[16,192,128]{2,1,0:T(8,128)(2,1)S(1)} %all_to_all.25.second) | copy-start | bytes 2359300
  42.2 4.3 %copy-start.13 = (s32[192]{0:T(256)S(1)}, s32[192]{0:T(256)}, u32[]{:S(2)}) copy-start(s32[192]{0:T(256)} %param.7) | copy-start | bytes 2308
  42.2 12.9 %all-to-all-start.1 = ((f32[64,2,128]{2,1,0:T(2,128)}), f32[64,2,128]{2,1,0:T(2,128)S(1)}, u32[]{:S(2)}, u32[]{:S(2)}) async-start(f32[64,2,128]{2,1,0:T(2,128)} %shard_map.86), calls=%async_computation.1 | async-start | bytes 131072 | tf_op jit(solution)/shard_map/all_to_all | solution.py:384
  55.8 21.5 %all-to-all-start.2 = ((f32[12,2,128]{2,1,0:T(2,128)}), f32[12,2,128]{2,1,0:T(2,128)S(1)}, u32[]{:S(2)}, u32[]{:S(2)}) async-start(f32[12,2,128]{2,1,0:T(2,128)} %get-tuple-element.14), calls=%async_computation.2 | async-start | bytes 24576 | tf_op jit(solution)/shard_map/all_to_all | solution.py:384
  77.3 0.6 copy-start.7
  83.9 7.0 %copy-start.16 = (s16[776,128]{1,0:T(8,128)(2,1)S(1)}, s16[776,128]{1,0:T(8,128)(2,1)}, u32[]{:S(2)}) copy-start(s16[776,128]{1,0:T(8,128)(2,1)} %get-tuple-element.17) | copy-start | bytes 595972
  83.9 10.3 %copy-start.15 = (s16[776,128]{1,0:T(8,128)(2,1)S(1)}, s16[776,128]{1,0:T(8,128)(2,1)}, u32[]{:S(2)}) copy-start(s16[776,128]{1,0:T(8,128)(2,1)} %get-tuple-element.18) | copy-start | bytes 595972
  83.9 14.6 %copy-start.14 = (s16[776,128]{1,0:T(8,128)(2,1)S(1)}, s16[776,128]{1,0:T(8,128)(2,1)}, u32[]{:S(2)}) copy-start(s16[776,128]{1,0:T(8,128)(2,1)} %get-tuple-element.19) | copy-start | bytes 595972
  83.9 32.2 %copy-start.6 = (f32[768,128]{1,0:T(8,128)S(1)}, f32[768,128]{1,0:T(8,128)}, u32[]{:S(2)}) copy-start(f32[768,128]{1,0:T(8,128)} %get-tuple-element.16.own_hbm) | copy-start | bytes 1179652
  83.9 32.2 %all-to-all-start.3 = ((s16[64,56,128]{2,1,0:T(8,128)(2,1)}), s16[64,56,128]{2,1,0:T(8,128)(2,1)S(1)}, u32[]{:S(2)}, u32[]{:S(2)}) async-start(s16[64,56,128]{2,1,0:T(8,128)(2,1)} %get-tuple-element.15), calls=%async_computation.3 | async-start | bytes 1835008 | tf_op jit(solution)/shard_map/all_to_all | solution.py:384
  90.9 12.7 %collective-permute-start = (s16[776,128]{1,0:T(8,128)(2,1)S(1)}, s16[776,128]{1,0:T(8,128)(2,1)S(1)}, u32[]{:S(2)}, u32[]{:S(2)}) collective-permute-start(s16[776,128]{1,0:T(8,128)(2,1)S(1)} %copy-done.16), channel_id=1, source_target_pairs={{0,12},{12,24},{24,36},{36,0},{1,13},{13,25},{25,37},{37,1},{2,14}... | collective-permute-start | bytes 595976 | tf_op jit(solution)/shard_map/ppermute | solution.py:450
  94.2 18.2 %collective-permute-start.1 = (s16[776,128]{1,0:T(8,128)(2,1)S(1)}, s16[776,128]{1,0:T(8,128)(2,1)S(1)}, u32[]{:S(2)}, u32[]{:S(2)}) collective-permute-start(s16[776,128]{1,0:T(8,128)(2,1)S(1)} %copy-done.15), channel_id=1, source_target_pairs={{0,24},{12,36},{24,0},{36,12},{1,25},{13,37},{25,1},{37,13},{2,26}... | collective-permute-start | bytes 595976 | tf_op jit(solution)/shard_map/ppermute | solution.py:450
  98.5 14.2 %collective-permute-start.2 = (s16[776,128]{1,0:T(8,128)(2,1)S(1)}, s16[776,128]{1,0:T(8,128)(2,1)S(1)}, u32[]{:S(2)}, u32[]{:S(2)}) collective-permute-start(s16[776,128]{1,0:T(8,128)(2,1)S(1)} %copy-done.14), channel_id=1, source_target_pairs={{0,36},{12,0},{24,12},{36,24},{1,37},{13,1},{25,13},{37,25},{2,38}... | collective-permute-start | bytes 595976 | tf_op jit(solution)/shard_map/ppermute | solution.py:450
  116.1 19.3 %copy-start.1 = (bf16[192,16,128]{2,0,1:T(8,128)(2,1)S(1)}, bf16[192,16,128]{2,0,1:T(8,128)(2,1)}, u32[]{:S(2)}) copy-start(bf16[192,16,128]{2,0,1:T(8,128)(2,1)} %copy-done) | copy-start | bytes 2359300
  116.1 19.3 %copy-start.3 = (bf16[16,192,128]{2,1,0:T(8,128)(2,1)S(1)}, bf16[16,192,128]{2,1,0:T(8,128)(2,1)}, u32[]{:S(2)}) copy-start(bf16[16,192,128]{2,1,0:T(8,128)(2,1)} %copy-done.2) | copy-start | bytes 2359300
  116.1 19.3 %copy-start.5 = (f32[1,1,16,128,128]{4,3,2,1,0:T(8,128)S(1)}, f32[1,1,16,128,128]{4,3,2,1,0:T(8,128)}, u32[]{:S(2)}) copy-start(f32[1,1,16,128,128]{4,3,2,1,0:T(8,128)} %param.11) | copy-start | bytes 3145732
  119.6 15.8 %copy-start.8 = (f32[12,2,128]{2,1,0:T(2,128)S(1)}, f32[12,2,128]{2,1,0:T(2,128)}, u32[]{:S(2)}) copy-start(f32[12,2,128]{2,1,0:T(2,128)} %copy-done.7) | copy-start | bytes 36868
  119.6 15.8 %copy-start.10 = (s32[6,16]{1,0:T(8,128)S(1)}, s32[6,16]{1,0:T(8,128)}, u32[]{:S(2)}) copy-start(s32[6,16]{1,0:T(8,128)} %copy-done.9) | copy-start | bytes 1156
  119.6 15.8 %copy-start.11 = (f32[2,128]{1,0:T(2,128)S(1)}, f32[2,128]{1,0:T(2,128)}, u32[]{:S(2)}) copy-start(f32[2,128]{1,0:T(2,128)} %pad_bitcast_fusion.labels) | copy-start | bytes 3076

commit v7 on v6

--- a/solution.py
+++ b/solution.py
@@ -263,36 +263,25 @@
         copy.wait()
 
 
-def across_kernel(
-    served, got_hbm, own_hbm, from_1, from_2, from_3, out, sums, parted, got, own, from_all, sems
-):
-    copies = [pltpu.make_async_copy(own_hbm, own, sems.at[0])]
-    for i, ref in enumerate((from_1, from_2, from_3)):
-        copies.append(pltpu.make_async_copy(ref, from_all.at[i], sems.at[1 + i]))
-    last = pltpu.make_async_copy(got_hbm, got, sems.at[4])
-    for copy in copies + [last]:
-        copy.start()
-    for copy in copies:
-        copy.wait()
+def across_kernel(served, got, own, from_1, from_2, from_3, out, sums, parted):
     n_x, n_z = served.shape[0], out.shape[0]
     wide = out.shape[1] - 16
     few = wide // 16
     size, rows = own.shape[0], n_z * few
     parts = size // 128
 
-    sides = range(from_all.shape[0])
-    exps = [real(from_all[i, size : size + 8])[0:parts] for i in sides]
+    sides = (from_1, from_2, from_3)
+    exps = [real(ref[size : size + 8])[0:parts] for ref in sides]
     down = jnp.transpose(tile_of(128, exps))
     down = scale_of(down) * (1.0 / LEVELS)
     for t in range(parts):
         part = slice(t * 128, (t + 1) * 128)
         total = own[part]
-        for i in sides:
+        for i, ref in enumerate(sides):
             lane = i * parts + t
-            total = total + real(from_all[i, part]) * down[:, lane : lane + 1]
+            total = total + real(ref[part]) * down[:, lane : lane + 1]
         sums[part] = total
 
-    last.wait()
     tiles = [real(got[d, rows : rows + 8]) for d in range(got.shape[0])]
     down = scale_of(upright([t[0:1] for t in tiles], rows)) * (1.0 / LEVELS)
     for q in range(0, got.shape[0], 8):
@@ -359,12 +348,10 @@
     lax.fori_loop(0, second.shape[0] // group, step, 0)
 
 
-def call(kernel, outs, n_in, scratch=(), smem=True, far_in=(), far_out=False, room=16):
+def call(kernel, outs, n_in, scratch=(), smem=True, far_out=False, room=16):
     specs = [pl.BlockSpec(memory_space=pltpu.VMEM)] * n_in
     if smem:
         specs[0] = pl.BlockSpec(memory_space=pltpu.SMEM)
-    for i in far_in:
-        specs[i] = pl.BlockSpec(memory_space=pltpu.HBM)
     space = pltpu.HBM if far_out else pltpu.VMEM
     return pl.pallas_call(
         kernel,
@@ -412,6 +399,7 @@
     targets = jnp.pad(labels.astype(f32), (0, 256 - samples)).reshape(2, 128)
 
     sent = call(gather_kernel, [shape((slots, samples, feature), bf16)], 2)(tab, ft)[0]
+    sent, targets = lax.optimization_barrier((sent, targets))
     second = swap(sent, GRP)
     acc = pltpu.VMEM((samples, 128), f32)
     part = call(partial_kernel, [shape((groups * n_x, 2, 128))], 4, [acc])(tab, ft, second, mats)[0]
@@ -451,15 +439,8 @@
         for r, side in enumerate(sides, 1)
     ]
     out = [shape((n_z, wide + 16, feature), jnp.int16)]
-    room = [
-        pltpu.VMEM((size, feature), f32),
-        pltpu.VMEM((n_z, wide, feature), f32),
-        pltpu.VMEM((groups * n_x, rows + 8, feature), jnp.int16),
-        pltpu.VMEM((size, feature), f32),
-        pltpu.VMEM((n_x - 1, size + 8, feature), jnp.int16),
-        pltpu.SemaphoreType.DMA((n_x + 1,)),
-    ]
-    got = call(across_kernel, out, 6, room, far_in=range(1, 6), room=16)(near, got, own, *sides)[0]
+    room = [pltpu.VMEM((size, feature), f32), pltpu.VMEM((n_z, wide, feature), f32)]
+    got = call(across_kernel, out, 6, room, room=16)(near, got, own, *sides)[0]
     got = swap(got, "z")
     logits, grads, mats = call(
         functools.partial(last_kernel, scale, rate),

time: 140 us -> 137 us (0.979)
  blocking collectives: 52 us -> 86.1 us
  waiting for transfers between devices: 31.5 us -> 14.5 us
  starting transfers between devices: 34.5 us -> 17.6 us
  Pallas kernels: 15.3 us -> 12.6 us
    all_to_all x2 -> x4, blocking collectives: 52 us -> 86.1 us  [swap(): return lax.all_to_all(x, axes, split_axis=0, concat_axis=0, tiled=True)]
    all_to_all x3 -> x1, waiting for transfers between devices: 20.4 us -> 3.45 us  [swap(): return lax.all_to_all(x, axes, split_axis=0, concat_axis=0, tiled=True)]
    all_to_all x3 -> x1, starting transfers between devices: 23.8 us -> 6.92 us  [swap(): return lax.all_to_all(x, axes, split_axis=0, concat_axis=0, tiled=True)]
    pallas_call x1, Pallas kernels: 3.49 us -> 2.07 us  [on_device(): got = call(across_kernel, out, 6, room, room=16)(near, got, own, *sides)[0]]
  transfers between devices with their start and end apart: 6 -> 4, of which waited for: 6 -> 4; matrix products, arithmetic and copies ran while one was open for 0% -> 0% of each run, Pallas kernels for 0% -> 0%
where the time goes in v7:
time: 137 us; the launch traced here: 135 us
  blocking collectives  86.1 us (63%)
  starting transfers between devices  17.6 us (13%)
  waiting for transfers between devices  14.5 us (11%)
  Pallas kernels  12.6 us (9%)
  local copies, waits for them, and re-layouts  2.1 us (2%)
  between operations  1.6 us (1%)
    all_to_all x4, blocking collectives, swap(): return lax.all_to_all(x, axes, split_axis=0, concat_axis=0, tiled=True)  86.1 us
    ppermute x3, waiting for transfers between devices, on_device(): lax.ppermute(side, 'x', [(i, (i + r) % n_x) for i in range(n_x)])  11.1 us
    ppermute x3, starting transfers between devices, on_device(): lax.ppermute(side, 'x', [(i, (i + r) % n_x) for i in range(n_x)])  10.7 us
    all_to_all x1, starting transfers between devices, swap(): return lax.all_to_all(x, axes, split_axis=0, concat_axis=0, tiled=True)  6.92 us
    pallas_call x1, Pallas kernels, on_device(): call(functools.partial(terms_kernel, scale, rate), [shape((groups * n_x,...  5.96 us
    all_to_all x1, waiting for transfers between devices, swap(): return lax.all_to_all(x, axes, split_axis=0, concat_axis=0, tiled=True)  3.45 us
  transfers between devices with their start and end apart: 4, of which 4 were waited for; matrix products, arithmetic and copies ran while one was open for 0% of the time, Pallas kernels for 0%

profile of v7, /device:TPU:1, one launch (start us, length us, event | category | flops | bytes accessed | tf_op | source)
XLA Modules:
  0.0 134.8 jit_solution(15910516054237915007)
XLA Ops:
  1.4 0.0 copy-start.16
  1.4 0.6 pad_bitcast_fusion.labels
  1.9 0.1 copy-done.16
  2.0 0.1 select_reduce_fusion
  2.1 1.3 copy.11
  3.5 0.1 select_reduce_fusion.1
  3.7 0.0 copy-start.8
  3.7 0.8 shard_map.85
  4.4 0.0 copy-start.4
  4.5 36.2 %all_to_all.25.second = bf16[16,192,128]{2,1,0:T(8,128)(2,1)S(1)} all-to-all(bf16[16,192,128]{2,1,0:T(8,128)(2,1)S(1)} %shard_map.85), channel_id=1, replica_groups=mesh['y'=8,'core'=2,'x'=4,'z'=12] {'y','core'}, dimensions={0} | all-to-all | bytes 1572864 | tf_op jit(solution)/shard_map/all_to_all | solution.py:371
  40.7 0.0 copy-done.8
  40.7 1.5 %shard_map.86 = f32[64,2,128]{2,1,0:T(2,128)S(1)} custom-call(s32[6,16]{1,0:T(8,128)S(1)} %stack.16.tab, bf16[16,192,128]{2,1,0:T(8,128)(2,1)S(1)} %bitcast.21, bf16[16,192,128]{2,1,0:T(8,128)(2,1)S(1)} %all_to_all.25.second, f32[16,128,128]{2,1,0:T(8,128)S(1)} %bitcast.25), custom_call_target="tpu_custom_call" | custom-call | tf_op jit(solution)/shard_map/pallas_call | solution.py:405
  42.2 12.3 %all_to_all.26.parts = f32[64,2,128]{2,1,0:T(2,128)S(1)} all-to-all(f32[64,2,128]{2,1,0:T(2,128)S(1)} %shard_map.86), channel_id=1, replica_groups=mesh['y'=8,'core'=2,'x'=4,'z'=12] {'y','core','x'}, dimensions={0} | all-to-all | bytes 131072 | tf_op jit(solution)/shard_map/all_to_all | solution.py:371
  54.6 0.1 shard_map.87
  54.6 21.6 %all_to_all.27.sums.first_sums = f32[12,2,128]{2,1,0:T(2,128)} all-to-all(f32[12,2,128]{2,1,0:T(2,128)S(1)} %get-tuple-element.17), channel_id=1, replica_groups=mesh['y'=8,'core'=2,'x'=4,'z'=12] {'z'}, dimensions={0} | all-to-all | bytes 24576 | tf_op jit(solution)/shard_map/all_to_all | solution.py:371
  76.3 6.0 %shard_map.88 = (s16[64,56,128]{2,1,0:T(8,128)(2,1)}, f32[768,128]{1,0:T(8,128)}, s16[776,128]{1,0:T(8,128)(2,1)}, s16[776,128]{1,0:T(8,128)(2,1)}, s16[776,128]{1,0:T(8,128)(2,1)}) custom-call(s32[6,16]{1,0:T(8,128)} %copy-done.8, bf16[16,192,128]{2,1,0:T(8,128)(2,1)} %bitcast.22, bf16[16,192,128]{2,1,0:T(8,128)(2,1)} %copy-done.2, ...), custom_call_target="tpu_custom_call" | custom-call | tf_op jit(solution)/shard_map/pallas_call | solution.py:413
  82.3 6.9 %all-to-all-start.3 = ((s16[64,56,128]{2,1,0:T(8,128)(2,1)}), s16[64,56,128]{2,1,0:T(8,128)(2,1)S(1)}, u32[]{:S(2)}, u32[]{:S(2)}) async-start(s16[64,56,128]{2,1,0:T(8,128)(2,1)} %get-tuple-element.19), calls=%async_computation.3 | async-start | bytes 1835008 | tf_op jit(solution)/shard_map/all_to_all | solution.py:371
  89.2 3.3 %collective-permute-start = (s16[776,128]{1,0:T(8,128)(2,1)S(1)}, s16[776,128]{1,0:T(8,128)(2,1)S(1)}, u32[]{:S(2)}, u32[]{:S(2)}) collective-permute-start(s16[776,128]{1,0:T(8,128)(2,1)S(1)} %copy-done.15), channel_id=1, source_target_pairs={{0,12},{12,24},{24,36},{36,0},{1,13},{13,25},{25,37},{37,1},{2,14}... | collective-permute-start | bytes 595976 | tf_op jit(solution)/shard_map/ppermute | solution.py:438
  92.5 4.3 %collective-permute-start.1 = (s16[776,128]{1,0:T(8,128)(2,1)S(1)}, s16[776,128]{1,0:T(8,128)(2,1)S(1)}, u32[]{:S(2)}, u32[]{:S(2)}) collective-permute-start(s16[776,128]{1,0:T(8,128)(2,1)S(1)} %copy-done.14), channel_id=1, source_target_pairs={{0,24},{12,36},{24,0},{36,12},{1,25},{13,37},{25,1},{37,13},{2,26}... | collective-permute-start | bytes 595976 | tf_op jit(solution)/shard_map/ppermute | solution.py:438
  96.9 3.1 %collective-permute-start.2 = (s16[776,128]{1,0:T(8,128)(2,1)S(1)}, s16[776,128]{1,0:T(8,128)(2,1)S(1)}, u32[]{:S(2)}, u32[]{:S(2)}) collective-permute-start(s16[776,128]{1,0:T(8,128)(2,1)S(1)} %copy-done.13), channel_id=1, source_target_pairs={{0,36},{12,0},{24,12},{36,24},{1,37},{13,1},{25,13},{37,25},{2,38}... | collective-permute-start | bytes 595976 | tf_op jit(solution)/shard_map/ppermute | solution.py:438
  100.0 2.0 %collective-permute-done.from_1 = s16[776,128]{1,0:T(8,128)(2,1)S(1)} collective-permute-done((s16[776,128]{1,0:T(8,128)(2,1)S(1)}, s16[776,128]{1,0:T(8,128)(2,1)S(1)}, u32[]{:S(2)}, u32[]{:S(2)}) %collective-permute-start) | collective-permute-done | bytes 198688 | tf_op jit(solution)/shard_map/ppermute | solution.py:438
  102.0 8.8 %collective-permute-done.1.from_2 = s16[776,128]{1,0:T(8,128)(2,1)S(1)} collective-permute-done((s16[776,128]{1,0:T(8,128)(2,1)S(1)}, s16[776,128]{1,0:T(8,128)(2,1)S(1)}, u32[]{:S(2)}, u32[]{:S(2)}) %collective-permute-start.1) | collective-permute-done | bytes 198688 | tf_op jit(solution)/shard_map/ppermute | solution.py:438
  110.7 0.3 collective-permute-done.2.from_3
  111.0 3.5 %all-to-all-done.3.got = s16[64,56,128]{2,1,0:T(8,128)(2,1)S(1)} async-done(((s16[64,56,128]{2,1,0:T(8,128)(2,1)}), s16[64,56,128]{2,1,0:T(8,128)(2,1)S(1)}, u32[]{:S(2)}, u32[]{:S(2)}) %all-to-all-start.3) | async-done | bytes 917536 | tf_op jit(solution)/shard_map/all_to_all | solution.py:371
  114.5 2.1 %shard_map.89 = s16[12,80,128]{2,1,0:T(8,128)(2,1)S(1)} custom-call(s32[4,128]{1,0:T(4,128)S(1)} %get-tuple-element.16.served, s16[64,56,128]{2,1,0:T(8,128)(2,1)S(1)} %all-to-all-done.3.got, f32[768,128]{1,0:T(8,128)S(1)} %copy-done.6, s16[776,128]{1,0:T(8,128)(2,1)S(1)} %collective-permute-done.from_1, s16[776,128]{1,0:T(8,128)(2,1)S(1)} %collective-permute-done.1.from_2, ...), custom_call_target="tpu_custom_call" | custom-call | tf_op jit(solution)/shard_map/pallas_call | solution.py:443
  116.6 0.0 copy-start.9
  116.6 0.0 copy-start.10
  116.6 15.9 %all_to_all.28.got = s16[12,80,128]{2,1,0:T(8,128)(2,1)S(1)} all-to-all(s16[12,80,128]{2,1,0:T(8,128)(2,1)S(1)} %shard_map.89), channel_id=1, replica_groups=mesh['y'=8,'core'=2,'x'=4,'z'=12] {'z'}, dimensions={0} | all-to-all | bytes 491520 | tf_op jit(solution)/shard_map/all_to_all | solution.py:371
  132.5 0.0 copy-done.5
  132.5 0.0 copy-done.7
  132.5 0.0 copy-done.9
  132.5 2.3 %shard_map.90 = (f32[2,128]{1,0:T(2,128)}, f32[4,16,128]{2,1,0:T(8,128)}, f32[16,128,128]{2,1,0:T(8,128)}) custom-call(s32[6,16]{1,0:T(8,128)S(1)} %copy-done.9, bf16[16,192,128]{2,1,0:T(8,128)(2,1)S(1)} %bitcast.23, bf16[16,192,128]{2,1,0:T(8,128)(2,1)S(1)} %copy-done.3, f32[16,128,128]{2,1,0:T(8,128)S(1)} %bitcast.26, ...), custom_call_target="tpu_custom_call" | custom-call | tf_op jit(solution)/shard_map/pallas_call | solution.py:445
  (31 shorter events, 0.1 us)
Async XLA Ops:
  0.6 0.7 copy-start.12
  0.7 1.4 %copy-start.11 = (s32[16,1,16]{2,1,0:T(1,128)S(1)}, s32[16,1,16]{2,1,0:T(1,128)}, u32[]{:S(2)}) copy-start(s32[16,1,16]{2,1,0:T(1,128)} %param.9) | copy-start | bytes 3076
  1.4 0.7 copy-start.16
  3.5 37.2 %copy-start = (bf16[192,16,128]{2,0,1:T(8,128)(2,1)}, bf16[192,16,128]{2,0,1:T(8,128)(2,1)S(1)}, u32[]{:S(2)}) copy-start(bf16[192,16,128]{2,0,1:T(8,128)(2,1)S(1)} %copy.11) | copy-start | bytes 2359300
  3.7 37.0 %copy-start.8 = (s32[6,16]{1,0:T(8,128)}, s32[6,16]{1,0:T(8,128)S(1)}, u32[]{:S(2)}) copy-start(s32[6,16]{1,0:T(8,128)S(1)} %stack.16.tab) | copy-start | bytes 1156
  4.4 36.3 %copy-start.4 = (f32[1,1,16,128,128]{4,3,2,1,0:T(8,128)S(1)}, f32[1,1,16,128,128]{4,3,2,1,0:T(8,128)}, u32[]{:S(2)}) copy-start(f32[1,1,16,128,128]{4,3,2,1,0:T(8,128)} %param.11) | copy-start | bytes 3145732
  40.7 1.5 %copy-start.2 = (bf16[16,192,128]{2,1,0:T(8,128)(2,1)}, bf16[16,192,128]{2,1,0:T(8,128)(2,1)S(1)}, u32[]{:S(2)}) copy-start(bf16[16,192,128]{2,1,0:T(8,128)(2,1)S(1)} %all_to_all.25.second) | copy-start | bytes 2359300
  82.3 7.0 %copy-start.15 = (s16[776,128]{1,0:T(8,128)(2,1)S(1)}, s16[776,128]{1,0:T(8,128)(2,1)}, u32[]{:S(2)}) copy-start(s16[776,128]{1,0:T(8,128)(2,1)} %get-tuple-element.21) | copy-start | bytes 595972
  82.3 10.3 %copy-start.14 = (s16[776,128]{1,0:T(8,128)(2,1)S(1)}, s16[776,128]{1,0:T(8,128)(2,1)}, u32[]{:S(2)}) copy-start(s16[776,128]{1,0:T(8,128)(2,1)} %get-tuple-element.22) | copy-start | bytes 595972
  82.3 14.6 %copy-start.13 = (s16[776,128]{1,0:T(8,128)(2,1)S(1)}, s16[776,128]{1,0:T(8,128)(2,1)}, u32[]{:S(2)}) copy-start(s16[776,128]{1,0:T(8,128)(2,1)} %get-tuple-element.23) | copy-start | bytes 595972
  82.3 32.2 %copy-start.6 = (f32[768,128]{1,0:T(8,128)S(1)}, f32[768,128]{1,0:T(8,128)}, u32[]{:S(2)}) copy-start(f32[768,128]{1,0:T(8,128)} %get-tuple-element.20.own) | copy-start | bytes 1179652
  82.3 32.2 %all-to-all-start.3 = ((s16[64,56,128]{2,1,0:T(8,128)(2,1)}), s16[64,56,128]{2,1,0:T(8,128)(2,1)S(1)}, u32[]{:S(2)}, u32[]{:S(2)}) async-start(s16[64,56,128]{2,1,0:T(8,128)(2,1)} %get-tuple-element.19), calls=%async_computation.3 | async-start | bytes 1835008 | tf_op jit(solution)/shard_map/all_to_all | solution.py:371
  89.2 12.7 %collective-permute-start = (s16[776,128]{1,0:T(8,128)(2,1)S(1)}, s16[776,128]{1,0:T(8,128)(2,1)S(1)}, u32[]{:S(2)}, u32[]{:S(2)}) collective-permute-start(s16[776,128]{1,0:T(8,128)(2,1)S(1)} %copy-done.15), channel_id=1, source_target_pairs={{0,12},{12,24},{24,36},{36,0},{1,13},{13,25},{25,37},{37,1},{2,14}... | collective-permute-start | bytes 595976 | tf_op jit(solution)/shard_map/ppermute | solution.py:438
  92.5 18.2 %collective-permute-start.1 = (s16[776,128]{1,0:T(8,128)(2,1)S(1)}, s16[776,128]{1,0:T(8,128)(2,1)S(1)}, u32[]{:S(2)}, u32[]{:S(2)}) collective-permute-start(s16[776,128]{1,0:T(8,128)(2,1)S(1)} %copy-done.14), channel_id=1, source_target_pairs={{0,24},{12,36},{24,0},{36,12},{1,25},{13,37},{25,1},{37,13},{2,26}... | collective-permute-start | bytes 595976 | tf_op jit(solution)/shard_map/ppermute | solution.py:438
  96.9 14.2 %collective-permute-start.2 = (s16[776,128]{1,0:T(8,128)(2,1)S(1)}, s16[776,128]{1,0:T(8,128)(2,1)S(1)}, u32[]{:S(2)}, u32[]{:S(2)}) collective-permute-start(s16[776,128]{1,0:T(8,128)(2,1)S(1)} %copy-done.13), channel_id=1, source_target_pairs={{0,36},{12,0},{24,12},{36,24},{1,37},{13,1},{25,13},{37,25},{2,38}... | collective-permute-start | bytes 595976 | tf_op jit(solution)/shard_map/ppermute | solution.py:438
  114.5 18.0 %copy-start.1 = (bf16[192,16,128]{2,0,1:T(8,128)(2,1)S(1)}, bf16[192,16,128]{2,0,1:T(8,128)(2,1)}, u32[]{:S(2)}) copy-start(bf16[192,16,128]{2,0,1:T(8,128)(2,1)} %copy-done) | copy-start | bytes 2359300
  114.5 18.0 %copy-start.3 = (bf16[16,192,128]{2,1,0:T(8,128)(2,1)S(1)}, bf16[16,192,128]{2,1,0:T(8,128)(2,1)}, u32[]{:S(2)}) copy-start(bf16[16,192,128]{2,1,0:T(8,128)(2,1)} %copy-done.2) | copy-start | bytes 2359300
  114.5 18.0 %copy-start.5 = (f32[1,1,16,128,128]{4,3,2,1,0:T(8,128)S(1)}, f32[1,1,16,128,128]{4,3,2,1,0:T(8,128)}, u32[]{:S(2)}) copy-start(f32[1,1,16,128,128]{4,3,2,1,0:T(8,128)} %param.11) | copy-start | bytes 3145732
  116.6 15.9 %copy-start.7 = (f32[12,2,128]{2,1,0:T(2,128)S(1)}, f32[12,2,128]{2,1,0:T(2,128)}, u32[]{:S(2)}) copy-start(f32[12,2,128]{2,1,0:T(2,128)} %all_to_all.27.sums.first_sums) | copy-start | bytes 36868
  116.6 15.9 %copy-start.9 = (s32[6,16]{1,0:T(8,128)S(1)}, s32[6,16]{1,0:T(8,128)}, u32[]{:S(2)}) copy-start(s32[6,16]{1,0:T(8,128)} %copy-done.8) | copy-start | bytes 1156
  116.6 15.9 %copy-start.10 = (f32[2,128]{1,0:T(2,128)S(1)}, f32[2,128]{1,0:T(2,128)}, u32[]{:S(2)}) copy-start(f32[2,128]{1,0:T(2,128)} %pad_bitcast_fusion.labels) | copy-start | bytes 3076

commit v8 on v7

--- a/solution.py
+++ b/solution.py
@@ -18,7 +18,7 @@
 
 SLOT, FIRST, LIVE, SERVED, MY_OWN, MY_X = range(6)
 
-PARTIAL_GROUP, TERMS_GROUP, LAST_GROUP = 16, 8, 16
+PARTIAL_GROUP, TERMS_GROUP, LAST_GROUP = 16, 16, 16
 SPARE = 64
 
 
@@ -107,6 +107,12 @@
         served[i : i + 1] = jnp.where(mine, near[i, 1:2], 0.0).astype(jnp.int32)
 
 
+def folded(labels):
+    row = labels[...].astype(f32)
+    rest = jnp.zeros((1, 256 - row.shape[1]), f32)
+    return jnp.concatenate([row[:, :128], jnp.concatenate([row[:, 128:], rest], axis=1)], axis=0)
+
+
 def total_of(parts):
     total = parts[0]
     for i in range(1, parts.shape[0]):
@@ -172,18 +178,28 @@
 
 
 def terms_kernel(
-    scale, rate, tab, ft, second, mats, sums, labels,
-    out_hbm, own_hbm, to_1, to_2, to_3, acc, errs, stash, tops, dense, out, to_all, sems,
+    scale, rate, tab, ft_hbm, second_hbm, mats_hbm, sums, labels,
+    out_hbm, own_hbm, to_1, to_2, to_3,
+    acc, errs, stash, tops, dense, out, to_all, ft, second, mats, sems, load_sems,
 ):
+    loads = [
+        pltpu.make_async_copy(far, near, load_sems.at[i])
+        for i, (far, near) in enumerate(((ft_hbm, ft), (second_hbm, second), (mats_hbm, mats)))
+    ]
+    for load in loads:
+        load.start()
     samples = second.shape[1]
     n_x, size = dense.shape[0], dense.shape[1]
     rows, parts = samples // n_x, size // 128
-    errors = jax.nn.sigmoid(scale * total_of(sums)) - labels[...]
+    errors = jax.nn.sigmoid(scale * total_of(sums)) - folded(labels)
     errs[...] = spread(errors, samples)
     acc[...] = jnp.zeros_like(acc)
     dense[...] = jnp.zeros_like(dense)
     tops[...] = jnp.zeros_like(tops)
     lanes = iota((samples, 128), 1)
+
+    for load in loads:
+        load.wait()
 
     group = math.gcd(TERMS_GROUP, second.shape[0])
 
@@ -249,23 +265,25 @@
     zero = jnp.zeros((1, 128), f32)
     tail = tile_of(8, [zero] + digits(row_sums(acc[...] * (1.0 / 128.0))))
     top_row = iota((8, 128), 0) == 0
-    for i in range(n_x):
-        part = slice(i * rows, (i + 1) * rows)
-        lying = jnp.transpose(tile_of(128, [k[part]]))
-        for j in range(second.shape[0]):
-            d = j * n_x + i
-            out[d, 0:rows] = whole(stash[j, part] * up[part, j : j + 1])
-            out[d, rows : rows + 8] = whole(jnp.where(top_row, lying[j : j + 1], tail))
-
-    copies.append(pltpu.make_async_copy(out, out_hbm, sems.at[n_x]))
-    copies[-1].start()
+    lying = [jnp.transpose(tile_of(128, [k[i * rows : (i + 1) * rows]])) for i in range(n_x)]
+    quarter = max(1, second.shape[0] // 4)
+    for q in range(0, second.shape[0], quarter):
+        for j in range(q, q + quarter):
+            for i in range(n_x):
+                d, part = j * n_x + i, slice(i * rows, (i + 1) * rows)
+                out[d, 0:rows] = whole(stash[j, part] * up[part, j : j + 1])
+                out[d, rows : rows + 8] = whole(jnp.where(top_row, lying[i][j : j + 1], tail))
+        piece = slice(q * n_x, (q + quarter) * n_x)
+        sem = sems.at[n_x + q // quarter]
+        copies.append(pltpu.make_async_copy(out.at[piece], out_hbm.at[piece], sem))
+        copies[-1].start()
     for copy in copies:
         copy.wait()
 
 
 def across_kernel(served, got, own, from_1, from_2, from_3, out, sums, parted):
     n_x, n_z = served.shape[0], out.shape[0]
-    wide = out.shape[1] - 16
+    wide = out.shape[1] - 8
     few = wide // 16
     size, rows = own.shape[0], n_z * few
     parts = size // 128
@@ -307,7 +325,7 @@
     for z in range(n_z):
         out[z, 0:wide] = whole(parted[z] * up[:, z : z + 1])
         mine = [part[z : z + 1] for part in lying]
-        out[z, wide : wide + 16] = whole(tile_of(16, mine + common))
+        out[z, wide : wide + 8] = whole(tile_of(8, mine + common))
 
 
 def last_kernel(
@@ -316,13 +334,14 @@
     samples = second.shape[1]
     few = grads.shape[0]
     wide = 16 * few
-    tiles = [real(got[i, wide : wide + 16]) for i in range(got.shape[0])]
+    tiles = [real(got[i, wide : wide + 8]) for i in range(got.shape[0])]
     high = -(-wide // 128)
     exps = [upright([t[n : n + 1] for t in tiles], min(wide, 128)) for n in range(high)]
     down = scale_of(jnp.concatenate(exps, axis=0)) * (1.0 / LEVELS)
     value = scale * undigits(tiles, high)
     logits[...] = value
-    errors = jax.nn.sigmoid(value) - labels[...]
+    targets = folded(labels)
+    errors = jax.nn.sigmoid(value) - targets
     errs[...] = spread(errors, samples)
     total = real(got[0, 0:wide]) * down[:, 0:1]
     for i in range(1, got.shape[0]):
@@ -331,7 +350,7 @@
     for b in range(few):
         mine = errs[pl.ds(tab[MY_OWN, 0] * few + b, 1)]
         grads[b] = sums[pl.ds(b, 16, stride=few)] * mine
-    earlier = jax.nn.sigmoid(scale * total_of(first_sums)) - labels[...]
+    earlier = jax.nn.sigmoid(scale * total_of(first_sums)) - targets
     errs[...] = spread(errors + earlier, samples)
 
     group = math.gcd(LAST_GROUP, second.shape[0])
@@ -348,10 +367,12 @@
     lax.fori_loop(0, second.shape[0] // group, step, 0)
 
 
-def call(kernel, outs, n_in, scratch=(), smem=True, far_out=False, room=16):
+def call(kernel, outs, n_in, scratch=(), smem=True, far_in=(), far_out=False, room=16):
     specs = [pl.BlockSpec(memory_space=pltpu.VMEM)] * n_in
     if smem:
         specs[0] = pl.BlockSpec(memory_space=pltpu.SMEM)
+    for i in far_in:
+        specs[i] = pl.BlockSpec(memory_space=pltpu.HBM)
     space = pltpu.HBM if far_out else pltpu.VMEM
     return pl.pallas_call(
         kernel,
@@ -396,10 +417,9 @@
 
     ft = jnp.transpose(fields, (1, 0, 2))
     mats = pair_mats[0, 0]
-    targets = jnp.pad(labels.astype(f32), (0, 256 - samples)).reshape(2, 128)
+    targets = labels.reshape(1, samples)
 
     sent = call(gather_kernel, [shape((slots, samples, feature), bf16)], 2)(tab, ft)[0]
-    sent, targets = lax.optimization_barrier((sent, targets))
     second = swap(sent, GRP)
     acc = pltpu.VMEM((samples, 128), f32)
     part = call(partial_kernel, [shape((groups * n_x, 2, 128))], 4, [acc])(tab, ft, second, mats)[0]
@@ -428,8 +448,13 @@
             pltpu.VMEM((n_x, size, feature), f32),
             pltpu.VMEM((groups * n_x, rows + 8, feature), jnp.int16),
             pltpu.VMEM((n_x - 1, size + 8, feature), jnp.int16),
-            pltpu.SemaphoreType.DMA((n_x + 1,)),
+            pltpu.VMEM(ft.shape, bf16),
+            pltpu.VMEM(second.shape, bf16),
+            pltpu.VMEM(mats.shape, f32),
+            pltpu.SemaphoreType.DMA((n_x + 4,)),
+            pltpu.SemaphoreType.DMA((3,)),
         ],
+        far_in=(1, 2, 3),
         far_out=True,
         room=60,
     )(tab, ft, second, mats, sums, targets)
@@ -438,7 +463,7 @@
         lax.ppermute(side, "x", [(i, (i + r) % n_x) for i in range(n_x)])
         for r, side in enumerate(sides, 1)
     ]
-    out = [shape((n_z, wide + 16, feature), jnp.int16)]
+    out = [shape((n_z, wide + 8, feature), jnp.int16)]
     room = [pltpu.VMEM((size, feature), f32), pltpu.VMEM((n_z, wide, feature), f32)]
     got = call(across_kernel, out, 6, room, room=16)(near, got, own, *sides)[0]
     got = swap(got, "z")

time: 137 us -> 136 us (level)
  transfers between devices with their start and end apart: 4 -> 4, of which waited for: 4 -> 3; matrix products, arithmetic and copies ran while one was open for 0% -> 0% of each run, Pallas kernels for 0% -> 0%
where the time goes in v8:
time: 136 us; the launch traced here: 134 us
  blocking collectives  85.2 us (63%)
  starting transfers between devices  17.8 us (13%)
  waiting for transfers between devices  14.5 us (11%)
  Pallas kernels  12.9 us (9%)
  between operations  1.57 us (1%)
  local copies, waits for them, and re-layouts  1.45 us (1%)
    all_to_all x4, blocking collectives, swap(): return lax.all_to_all(x, axes, split_axis=0, concat_axis=0, tiled=True)  85.2 us
    ppermute x3, waiting for transfers between devices, on_device(): lax.ppermute(side, 'x', [(i, (i + r) % n_x) for i in range(n_x)])  11.3 us
    ppermute x3, starting transfers between devices, on_device(): lax.ppermute(side, 'x', [(i, (i + r) % n_x) for i in range(n_x)])  10.7 us
    all_to_all x1, starting transfers between devices, swap(): return lax.all_to_all(x, axes, split_axis=0, concat_axis=0, tiled=True)  7.1 us
    pallas_call x1, Pallas kernels, on_device(): call(functools.partial(terms_kernel, scale, rate), [shape((groups * n_x,...  6.15 us
    all_to_all x1, waiting for transfers between devices, swap(): return lax.all_to_all(x, axes, split_axis=0, concat_axis=0, tiled=True)  3.26 us
  transfers between devices with their start and end apart: 4, of which 3 were waited for; matrix products, arithmetic and copies ran while one was open for 0% of the time, Pallas kernels for 0%

profile of v8, /device:TPU:1, one launch (start us, length us, event | category | flops | bytes accessed | tf_op | source)
XLA Modules:
  0.0 133.6 jit_solution(3395116619404578204)
XLA Ops:
  0.6 0.0 copy-start.11
  0.7 0.0 copy-start.13
  1.3 0.0 copy-done.13
  1.4 0.0 copy-done.11
  1.4 0.1 select_reduce_fusion
  1.5 1.3 %copy.11 = bf16[192,16,128]{2,0,1:T(8,128)(2,1)S(1)} copy(bf16[192,16,128]{2,1,0:T(8,128)(2,1)} %param.6) | data formatting | bytes 1572864 | tf_op args[0]
  2.8 0.0 copy-start
  2.9 0.1 select_reduce_fusion.1
  3.0 0.0 copy-start.8
  3.0 0.8 shard_map.85
  3.8 0.0 copy-start.4
  3.8 36.2 %all_to_all.25.second.second_hbm = bf16[16,192,128]{2,1,0:T(8,128)(2,1)S(1)} all-to-all(bf16[16,192,128]{2,1,0:T(8,128)(2,1)S(1)} %shard_map.85), channel_id=1, replica_groups=mesh['y'=8,'core'=2,'x'=4,'z'=12] {'y','core'}, dimensions={0} | all-to-all | bytes 1572864 | tf_op jit(solution)/shard_map/all_to_all | solution.py:392
  40.1 0.0 copy-done.4
  40.1 1.5 %shard_map.86 = f32[64,2,128]{2,1,0:T(2,128)S(1)} custom-call(s32[6,16]{1,0:T(8,128)S(1)} %stack.16.tab, bf16[16,192,128]{2,1,0:T(8,128)(2,1)S(1)} %bitcast.20, bf16[16,192,128]{2,1,0:T(8,128)(2,1)S(1)} %all_to_all.25.second.second_hbm, f32[16,128,128]{2,1,0:T(8,128)S(1)} %bitcast.24), custom_call_target="tpu_custom_call" | custom-call | tf_op jit(solution)/shard_map/pallas_call | solution.py:425
  41.6 12.3 %all_to_all.26.parts = f32[64,2,128]{2,1,0:T(2,128)S(1)} all-to-all(f32[64,2,128]{2,1,0:T(2,128)S(1)} %shard_map.86), channel_id=1, replica_groups=mesh['y'=8,'core'=2,'x'=4,'z'=12] {'y','core','x'}, dimensions={0} | all-to-all | bytes 131072 | tf_op jit(solution)/shard_map/all_to_all | solution.py:392
  53.9 0.1 shard_map.87
  54.0 21.5 %all_to_all.27.sums.first_sums = f32[12,2,128]{2,1,0:T(2,128)} all-to-all(f32[12,2,128]{2,1,0:T(2,128)S(1)} %get-tuple-element.14), channel_id=1, replica_groups=mesh['y'=8,'core'=2,'x'=4,'z'=12] {'z'}, dimensions={0} | all-to-all | bytes 24576 | tf_op jit(solution)/shard_map/all_to_all | solution.py:392
  75.5 6.2 %shard_map.88 = (s16[64,56,128]{2,1,0:T(8,128)(2,1)}, f32[768,128]{1,0:T(8,128)}, s16[776,128]{1,0:T(8,128)(2,1)}, s16[776,128]{1,0:T(8,128)(2,1)}, s16[776,128]{1,0:T(8,128)(2,1)}) custom-call(s32[6,16]{1,0:T(8,128)} %copy-done.8, bf16[16,192,128]{2,1,0:T(8,128)(2,1)} %bitcast.21, bf16[16,192,128]{2,1,0:T(8,128)(2,1)} %copy-done.2, ...), custom_call_target="tpu_custom_call" | custom-call | tf_op jit(solution)/shard_map/pallas_call | solution.py:433
  81.7 0.0 copy-start.5
  81.7 7.1 %all-to-all-start.3 = ((s16[64,56,128]{2,1,0:T(8,128)(2,1)}), s16[64,56,128]{2,1,0:T(8,128)(2,1)S(1)}, u32[]{:S(2)}, u32[]{:S(2)}) async-start(s16[64,56,128]{2,1,0:T(8,128)(2,1)} %get-tuple-element.15), calls=%async_computation.3 | async-start | bytes 1835008 | tf_op jit(solution)/shard_map/all_to_all | solution.py:392
  88.8 3.3 %collective-permute-start = (s16[776,128]{1,0:T(8,128)(2,1)}, s16[776,128]{1,0:T(8,128)(2,1)S(1)}, u32[]{:S(2)}, u32[]{:S(2)}) collective-permute-start(s16[776,128]{1,0:T(8,128)(2,1)} %get-tuple-element.17), channel_id=1, source_target_pairs={{0,12},{12,24},{24,36},{36,0},{1,13},{13,25},{25,37},{37,1},{2,14}... | collective-permute-start | bytes 595976 | tf_op jit(solution)/shard_map/ppermute | solution.py:463
  92.1 4.3 %collective-permute-start.1 = (s16[776,128]{1,0:T(8,128)(2,1)}, s16[776,128]{1,0:T(8,128)(2,1)S(1)}, u32[]{:S(2)}, u32[]{:S(2)}) collective-permute-start(s16[776,128]{1,0:T(8,128)(2,1)} %get-tuple-element.18), channel_id=1, source_target_pairs={{0,24},{12,36},{24,0},{36,12},{1,25},{13,37},{25,1},{37,13},{2,26}... | collective-permute-start | bytes 595976 | tf_op jit(solution)/shard_map/ppermute | solution.py:463
  96.4 3.1 %collective-permute-start.2 = (s16[776,128]{1,0:T(8,128)(2,1)S(1)}, s16[776,128]{1,0:T(8,128)(2,1)S(1)}, u32[]{:S(2)}, u32[]{:S(2)}) collective-permute-start(s16[776,128]{1,0:T(8,128)(2,1)S(1)} %copy-done.12), channel_id=1, source_target_pairs={{0,36},{12,0},{24,12},{36,24},{1,37},{13,1},{25,13},{37,25},{2,38}... | collective-permute-start | bytes 595976 | tf_op jit(solution)/shard_map/ppermute | solution.py:463
  99.5 2.1 %collective-permute-done.from_1 = s16[776,128]{1,0:T(8,128)(2,1)S(1)} collective-permute-done((s16[776,128]{1,0:T(8,128)(2,1)}, s16[776,128]{1,0:T(8,128)(2,1)S(1)}, u32[]{:S(2)}, u32[]{:S(2)}) %collective-permute-start) | collective-permute-done | bytes 198688 | tf_op jit(solution)/shard_map/ppermute | solution.py:463
  101.6 9.2 %collective-permute-done.1.from_2 = s16[776,128]{1,0:T(8,128)(2,1)S(1)} collective-permute-done((s16[776,128]{1,0:T(8,128)(2,1)}, s16[776,128]{1,0:T(8,128)(2,1)S(1)}, u32[]{:S(2)}, u32[]{:S(2)}) %collective-permute-start.1) | collective-permute-done | bytes 198688 | tf_op jit(solution)/shard_map/ppermute | solution.py:463
  110.8 0.0 collective-permute-done.2.from_3
  110.8 3.3 %all-to-all-done.3.got = s16[64,56,128]{2,1,0:T(8,128)(2,1)S(1)} async-done(((s16[64,56,128]{2,1,0:T(8,128)(2,1)}), s16[64,56,128]{2,1,0:T(8,128)(2,1)S(1)}, u32[]{:S(2)}, u32[]{:S(2)}) %all-to-all-start.3) | async-done | bytes 917536 | tf_op jit(solution)/shard_map/all_to_all | solution.py:392
  114.0 2.1 %shard_map.89 = s16[12,72,128]{2,1,0:T(8,128)(2,1)S(1)} custom-call(s32[4,128]{1,0:T(4,128)S(1)} %get-tuple-element.13.served, s16[64,56,128]{2,1,0:T(8,128)(2,1)S(1)} %all-to-all-done.3.got, f32[768,128]{1,0:T(8,128)S(1)} %copy-done.6, s16[776,128]{1,0:T(8,128)(2,1)S(1)} %collective-permute-done.from_1, s16[776,128]{1,0:T(8,128)(2,1)S(1)} %collective-permute-done.1.from_2, ...), custom_call_target="tpu_custom_call" | custom-call | tf_op jit(solution)/shard_map/pallas_call | solution.py:468
  116.1 0.0 copy-start.9
  116.1 0.0 copy-start.10
  116.2 15.1 %all_to_all.28.got = s16[12,72,128]{2,1,0:T(8,128)(2,1)S(1)} all-to-all(s16[12,72,128]{2,1,0:T(8,128)(2,1)S(1)} %shard_map.89), channel_id=1, replica_groups=mesh['y'=8,'core'=2,'x'=4,'z'=12] {'z'}, dimensions={0} | all-to-all | bytes 442368 | tf_op jit(solution)/shard_map/all_to_all | solution.py:392
  131.3 2.3 %shard_map.90 = (f32[2,128]{1,0:T(2,128)}, f32[4,16,128]{2,1,0:T(8,128)}, f32[16,128,128]{2,1,0:T(8,128)}) custom-call(s32[6,16]{1,0:T(8,128)S(1)} %copy-done.9, bf16[16,192,128]{2,1,0:T(8,128)(2,1)S(1)} %bitcast.22, bf16[16,192,128]{2,1,0:T(8,128)(2,1)S(1)} %copy-done.3, f32[16,128,128]{2,1,0:T(8,128)S(1)} %bitcast.25, ...), custom_call_target="tpu_custom_call" | custom-call | tf_op jit(solution)/shard_map/pallas_call | solution.py:470
  (23 shorter events, 0.1 us)
Async XLA Ops:
  0.6 0.7 copy-start.11
  0.7 0.7 copy-start.13
  2.8 37.2 %copy-start = (bf16[192,16,128]{2,0,1:T(8,128)(2,1)}, bf16[192,16,128]{2,0,1:T(8,128)(2,1)S(1)}, u32[]{:S(2)}) copy-start(bf16[192,16,128]{2,0,1:T(8,128)(2,1)S(1)} %copy.11) | copy-start | bytes 2359300
  3.0 37.0 %copy-start.8 = (s32[6,16]{1,0:T(8,128)}, s32[6,16]{1,0:T(8,128)S(1)}, u32[]{:S(2)}) copy-start(s32[6,16]{1,0:T(8,128)S(1)} %stack.16.tab) | copy-start | bytes 1156
  3.8 36.3 %copy-start.4 = (f32[1,1,16,128,128]{4,3,2,1,0:T(8,128)S(1)}, f32[1,1,16,128,128]{4,3,2,1,0:T(8,128)}, u32[]{:S(2)}) copy-start(f32[1,1,16,128,128]{4,3,2,1,0:T(8,128)} %param.11) | copy-start | bytes 3145732
  40.0 1.5 %copy-start.2 = (bf16[16,192,128]{2,1,0:T(8,128)(2,1)}, bf16[16,192,128]{2,1,0:T(8,128)(2,1)S(1)}, u32[]{:S(2)}) copy-start(bf16[16,192,128]{2,1,0:T(8,128)(2,1)S(1)} %all_to_all.25.second.second_hbm) | copy-start | bytes 2359300
  81.7 14.8 %copy-start.12 = (s16[776,128]{1,0:T(8,128)(2,1)S(1)}, s16[776,128]{1,0:T(8,128)(2,1)}, u32[]{:S(2)}) copy-start(s16[776,128]{1,0:T(8,128)(2,1)} %get-tuple-element.19) | copy-start | bytes 595972
  81.7 32.4 %copy-start.6 = (f32[768,128]{1,0:T(8,128)S(1)}, f32[768,128]{1,0:T(8,128)}, u32[]{:S(2)}) copy-start(f32[768,128]{1,0:T(8,128)} %get-tuple-element.16.own) | copy-start | bytes 1179652
  81.7 49.6 %copy-start.5 = (f32[1,1,16,128,128]{4,3,2,1,0:T(8,128)S(1)}, f32[1,1,16,128,128]{4,3,2,1,0:T(8,128)}, u32[]{:S(2)}) copy-start(f32[1,1,16,128,128]{4,3,2,1,0:T(8,128)} %param.11) | copy-start | bytes 3145732
  81.7 32.4 %all-to-all-start.3 = ((s16[64,56,128]{2,1,0:T(8,128)(2,1)}), s16[64,56,128]{2,1,0:T(8,128)(2,1)S(1)}, u32[]{:S(2)}, u32[]{:S(2)}) async-start(s16[64,56,128]{2,1,0:T(8,128)(2,1)} %get-tuple-element.15), calls=%async_computation.3 | async-start | bytes 1835008 | tf_op jit(solution)/shard_map/all_to_all | solution.py:392
  88.8 12.8 %collective-permute-start = (s16[776,128]{1,0:T(8,128)(2,1)}, s16[776,128]{1,0:T(8,128)(2,1)S(1)}, u32[]{:S(2)}, u32[]{:S(2)}) collective-permute-start(s16[776,128]{1,0:T(8,128)(2,1)} %get-tuple-element.17), channel_id=1, source_target_pairs={{0,12},{12,24},{24,36},{36,0},{1,13},{13,25},{25,37},{37,1},{2,14}... | collective-permute-start | bytes 595976 | tf_op jit(solution)/shard_map/ppermute | solution.py:463
  92.1 18.7 %collective-permute-start.1 = (s16[776,128]{1,0:T(8,128)(2,1)}, s16[776,128]{1,0:T(8,128)(2,1)S(1)}, u32[]{:S(2)}, u32[]{:S(2)}) collective-permute-start(s16[776,128]{1,0:T(8,128)(2,1)} %get-tuple-element.18), channel_id=1, source_target_pairs={{0,24},{12,36},{24,0},{36,12},{1,25},{13,37},{25,1},{37,13},{2,26}... | collective-permute-start | bytes 595976 | tf_op jit(solution)/shard_map/ppermute | solution.py:463
  96.4 14.4 %collective-permute-start.2 = (s16[776,128]{1,0:T(8,128)(2,1)S(1)}, s16[776,128]{1,0:T(8,128)(2,1)S(1)}, u32[]{:S(2)}, u32[]{:S(2)}) collective-permute-start(s16[776,128]{1,0:T(8,128)(2,1)S(1)} %copy-done.12), channel_id=1, source_target_pairs={{0,36},{12,0},{24,12},{36,24},{1,37},{13,1},{25,13},{37,25},{2,38}... | collective-permute-start | bytes 595976 | tf_op jit(solution)/shard_map/ppermute | solution.py:463
  114.0 17.2 %copy-start.1 = (bf16[192,16,128]{2,0,1:T(8,128)(2,1)S(1)}, bf16[192,16,128]{2,0,1:T(8,128)(2,1)}, u32[]{:S(2)}) copy-start(bf16[192,16,128]{2,0,1:T(8,128)(2,1)} %copy-done) | copy-start | bytes 2359300
  114.0 17.2 %copy-start.3 = (bf16[16,192,128]{2,1,0:T(8,128)(2,1)S(1)}, bf16[16,192,128]{2,1,0:T(8,128)(2,1)}, u32[]{:S(2)}) copy-start(bf16[16,192,128]{2,1,0:T(8,128)(2,1)} %copy-done.2) | copy-start | bytes 2359300
  116.1 15.2 %copy-start.7 = (f32[12,2,128]{2,1,0:T(2,128)S(1)}, f32[12,2,128]{2,1,0:T(2,128)}, u32[]{:S(2)}) copy-start(f32[12,2,128]{2,1,0:T(2,128)} %all_to_all.27.sums.first_sums) | copy-start | bytes 36868
  116.1 15.2 %copy-start.9 = (s32[6,16]{1,0:T(8,128)S(1)}, s32[6,16]{1,0:T(8,128)}, u32[]{:S(2)}) copy-start(s32[6,16]{1,0:T(8,128)} %copy-done.8) | copy-start | bytes 1156
  116.1 15.2 %copy-start.10 = (s32[192]{0:T(256)S(1)}, s32[192]{0:T(256)}, u32[]{:S(2)}) copy-start(s32[192]{0:T(256)} %param.7) | copy-start | bytes 2308

commit v9 on v8

--- a/solution.py
+++ b/solution.py
@@ -68,7 +68,9 @@
         out[j] = ft[tab[SERVED, j]]
 
 
-def partial_kernel(tab, ft, second, mats, out, acc):
+def partial_kernel(tab, ft, second, mats, labels_hbm, out, targets, acc, labels, sem):
+    load = pltpu.make_async_copy(labels_hbm, labels, sem)
+    load.start()
     acc[...] = jnp.zeros_like(acc)
 
     group = math.gcd(PARTIAL_GROUP, second.shape[0])
@@ -93,6 +95,8 @@
         chunk = jnp.where(lanes == SPARE + j, tab[SERVED, j].astype(f32), chunk)
     for i in range(out.shape[0]):
         out[i] = chunk
+    load.wait()
+    targets[...] = folded(labels)
 
 
 def sum_kernel(parts, out, served):
@@ -178,28 +182,19 @@
 
 
 def terms_kernel(
-    scale, rate, tab, ft_hbm, second_hbm, mats_hbm, sums, labels,
+    scale, rate, tab, ft, second, mats, sums, targets,
     out_hbm, own_hbm, to_1, to_2, to_3,
-    acc, errs, stash, tops, dense, out, to_all, ft, second, mats, sems, load_sems,
+    acc, errs, stash, tops, dense, out, to_all, sems,
 ):
-    loads = [
-        pltpu.make_async_copy(far, near, load_sems.at[i])
-        for i, (far, near) in enumerate(((ft_hbm, ft), (second_hbm, second), (mats_hbm, mats)))
-    ]
-    for load in loads:
-        load.start()
     samples = second.shape[1]
     n_x, size = dense.shape[0], dense.shape[1]
     rows, parts = samples // n_x, size // 128
-    errors = jax.nn.sigmoid(scale * total_of(sums)) - folded(labels)
+    errors = jax.nn.sigmoid(scale * total_of(sums)) - targets[...]
     errs[...] = spread(errors, samples)
     acc[...] = jnp.zeros_like(acc)
     dense[...] = jnp.zeros_like(dense)
     tops[...] = jnp.zeros_like(tops)
     lanes = iota((samples, 128), 1)
-
-    for load in loads:
-        load.wait()
 
     group = math.gcd(TERMS_GROUP, second.shape[0])
 
@@ -329,8 +324,11 @@
 
 
 def last_kernel(
-    scale, rate, tab, ft, second, mats_in, got, first_sums, labels, logits, grads, mats, errs, sums
+    scale, rate, tab, ft, second, mats_hbm, got, first_sums, targets,
+    logits, grads, mats, errs, sums, mats_in, sem,
 ):
+    load = pltpu.make_async_copy(mats_hbm, mats_in, sem)
+    load.start()
     samples = second.shape[1]
     few = grads.shape[0]
     wide = 16 * few
@@ -340,8 +338,7 @@
     down = scale_of(jnp.concatenate(exps, axis=0)) * (1.0 / LEVELS)
     value = scale * undigits(tiles, high)
     logits[...] = value
-    targets = folded(labels)
-    errors = jax.nn.sigmoid(value) - targets
+    errors = jax.nn.sigmoid(value) - targets[...]
     errs[...] = spread(errors, samples)
     total = real(got[0, 0:wide]) * down[:, 0:1]
     for i in range(1, got.shape[0]):
@@ -350,10 +347,11 @@
     for b in range(few):
         mine = errs[pl.ds(tab[MY_OWN, 0] * few + b, 1)]
         grads[b] = sums[pl.ds(b, 16, stride=few)] * mine
-    earlier = jax.nn.sigmoid(scale * total_of(first_sums)) - targets
+    earlier = jax.nn.sigmoid(scale * total_of(first_sums)) - targets[...]
     errs[...] = spread(errors + earlier, samples)
 
     group = math.gcd(LAST_GROUP, second.shape[0])
+    load.wait()
 
     def step(q, carry):
         js = [q * group + i for i in range(group)]
@@ -376,7 +374,7 @@
     space = pltpu.HBM if far_out else pltpu.VMEM
     return pl.pallas_call(
         kernel,
-        out_shape=outs,
+        out_shape=[pltpu.HBM(o.shape, o.dtype) for o in outs] if far_out else outs,
         in_specs=specs,
         out_specs=[pl.BlockSpec(memory_space=space)] * len(outs),
         scratch_shapes=list(scratch),
@@ -417,12 +415,15 @@
 
     ft = jnp.transpose(fields, (1, 0, 2))
     mats = pair_mats[0, 0]
-    targets = labels.reshape(1, samples)
+    row = pltpu.with_memory_space_constraint(labels.reshape(1, samples), pltpu.HBM)
 
     sent = call(gather_kernel, [shape((slots, samples, feature), bf16)], 2)(tab, ft)[0]
     second = swap(sent, GRP)
     acc = pltpu.VMEM((samples, 128), f32)
-    part = call(partial_kernel, [shape((groups * n_x, 2, 128))], 4, [acc])(tab, ft, second, mats)[0]
+    out = [shape((groups * n_x, 2, 128)), shape((2, 128))]
+    room = [acc, pltpu.VMEM((1, samples), jnp.int32), pltpu.SemaphoreType.DMA(())]
+    call_partial = call(partial_kernel, out, 5, room, far_in=(4,))
+    part, targets = call_partial(tab, ft, second, mats, row)
     out = [shape((n_z, 2, 128)), shape((n_x, 128), jnp.int32)]
     part, near = call(sum_kernel, out, 1, smem=False)(swap(part, GRP + ("x",)))
     sums = swap(part, "z")
@@ -448,15 +449,10 @@
             pltpu.VMEM((n_x, size, feature), f32),
             pltpu.VMEM((groups * n_x, rows + 8, feature), jnp.int16),
             pltpu.VMEM((n_x - 1, size + 8, feature), jnp.int16),
-            pltpu.VMEM(ft.shape, bf16),
-            pltpu.VMEM(second.shape, bf16),
-            pltpu.VMEM(mats.shape, f32),
             pltpu.SemaphoreType.DMA((n_x + 4,)),
-            pltpu.SemaphoreType.DMA((3,)),
         ],
-        far_in=(1, 2, 3),
         far_out=True,
-        room=60,
+        room=24,
     )(tab, ft, second, mats, sums, targets)
     got = swap(out, GRP + ("x",))
     sides = [
@@ -471,8 +467,14 @@
         functools.partial(last_kernel, scale, rate),
         [shape((2, 128)), shape((few, per_block, feature)), shape(mats.shape)],
         7,
-        [acc, pltpu.VMEM((per_block * few, 128), f32)],
-    )(tab, ft, second, mats, got, sums, targets)
+        [
+            acc,
+            pltpu.VMEM((per_block * few, 128), f32),
+            pltpu.VMEM(mats.shape, f32),
+            pltpu.SemaphoreType.DMA(()),
+        ],
+        far_in=(3,),
+    )(tab, ft, second, pltpu.with_memory_space_constraint(pair_mats[0, 0], pltpu.HBM), got, sums, targets)
     return logits.reshape(256)[:samples], grads, mats[None, None]
 
 

time: 136 us -> 135 us (level)
    pallas_call x1, Pallas kernels: 6.15 us -> 4.53 us  [on_device(): call(functools.partial(terms_kernel, scale, rate), [shape((groups * n_x,...]
where the time goes in v9:
time: 135 us; the launch traced here: 133 us
  blocking collectives  85.1 us (63%)
  starting transfers between devices  17.6 us (13%)
  waiting for transfers between devices  14.5 us (11%)
  Pallas kernels  13 us (10%)
  between operations  1.47 us (1%)
  local copies, waits for them, and re-layouts  1.4 us (1%)
    all_to_all x4, blocking collectives, swap(): return lax.all_to_all(x, axes, split_axis=0, concat_axis=0, tiled=True)  85.1 us
    ppermute x3, waiting for transfers between devices, on_device(): lax.ppermute(side, 'x', [(i, (i + r) % n_x) for i in range(n_x)])  11.3 us
    ppermute x3, starting transfers between devices, on_device(): lax.ppermute(side, 'x', [(i, (i + r) % n_x) for i in range(n_x)])  10.7 us
    all_to_all x1, starting transfers between devices, swap(): return lax.all_to_all(x, axes, split_axis=0, concat_axis=0, tiled=True)  6.91 us
    pallas_call x1, Pallas kernels, on_device(): call(functools.partial(terms_kernel, scale, rate), [shape((groups * n_x,...  4.53 us
    pallas_call x1, Pallas kernels, on_device(): call(functools.partial(last_kernel, scale, rate), [shape((2, 128)), shape...  3.62 us
    all_to_all x1, waiting for transfers between devices, swap(): return lax.all_to_all(x, axes, split_axis=0, concat_axis=0, tiled=True)  3.26 us
  transfers between devices with their start and end apart: 4, of which 3 were waited for; matrix products, arithmetic and copies ran while one was open for 0% of the time, Pallas kernels for 0%

profile of v9, /device:TPU:1, one launch (start us, length us, event | category | flops | bytes accessed | tf_op | source)
XLA Modules:
  0.0 133.3 jit_solution(9965088231778293398)
XLA Ops:
  0.6 0.0 copy-start.2
  0.7 0.0 copy-start.3
  1.3 0.0 copy-done.3
  1.4 0.0 copy-done.2
  1.4 0.1 select_reduce_fusion
  1.5 1.3 %copy.11 = bf16[192,16,128]{2,0,1:T(8,128)(2,1)S(1)} copy(bf16[192,16,128]{2,1,0:T(8,128)(2,1)} %param.6) | data formatting | bytes 1572864 | tf_op args[0]
  2.9 0.1 select_reduce_fusion.1
  3.0 0.8 shard_map.85
  3.8 0.0 copy-start
  3.8 36.2 %all_to_all.25.second = bf16[16,192,128]{2,1,0:T(8,128)(2,1)S(1)} all-to-all(bf16[16,192,128]{2,1,0:T(8,128)(2,1)S(1)} %shard_map.85), channel_id=1, replica_groups=mesh['y'=8,'core'=2,'x'=4,'z'=12] {'y','core'}, dimensions={0} | all-to-all | bytes 1572864 | tf_op jit(solution)/shard_map/all_to_all | solution.py:390
  40.0 0.0 copy-done
  40.0 1.9 %shard_map.86 = (f32[64,2,128]{2,1,0:T(2,128)S(1)}, f32[2,128]{1,0:T(2,128)S(1)}) custom-call(s32[6,16]{1,0:T(8,128)S(1)} %stack.16.tab, bf16[16,192,128]{2,1,0:T(8,128)(2,1)S(1)} %bitcast.20, bf16[16,192,128]{2,1,0:T(8,128)(2,1)S(1)} %all_to_all.25.second, f32[16,128,128]{2,1,0:T(8,128)S(1)} %bitcast.24, s32[1,192]{1,0:T(1,128)} %bitcast.30), custom_call_target="tpu_custom_call" | custom-call | tf_op jit(solution)/shard_map/pallas_call | solution.py:426
  41.9 12.3 %all_to_all.26.parts = f32[64,2,128]{2,1,0:T(2,128)S(1)} all-to-all(f32[64,2,128]{2,1,0:T(2,128)S(1)} %get-tuple-element.15), channel_id=1, replica_groups=mesh['y'=8,'core'=2,'x'=4,'z'=12] {'y','core','x'}, dimensions={0} | all-to-all | bytes 131072 | tf_op jit(solution)/shard_map/all_to_all | solution.py:390
  54.3 0.1 shard_map.87
  54.4 21.5 %all_to_all.27.sums.first_sums = f32[12,2,128]{2,1,0:T(2,128)S(1)} all-to-all(f32[12,2,128]{2,1,0:T(2,128)S(1)} %get-tuple-element.17), channel_id=1, replica_groups=mesh['y'=8,'core'=2,'x'=4,'z'=12] {'z'}, dimensions={0} | all-to-all | bytes 24576 | tf_op jit(solution)/shard_map/all_to_all | solution.py:390
  75.9 4.5 %shard_map.88 = (s16[64,56,128]{2,1,0:T(8,128)(2,1)}, f32[768,128]{1,0:T(8,128)}, s16[776,128]{1,0:T(8,128)(2,1)}, s16[776,128]{1,0:T(8,128)(2,1)}, s16[776,128]{1,0:T(8,128)(2,1)}) custom-call(s32[6,16]{1,0:T(8,128)S(1)} %stack.16.tab, bf16[16,192,128]{2,1,0:T(8,128)(2,1)S(1)} %bitcast.21, bf16[16,192,128]{2,1,0:T(8,128)(2,1)S(1)} %all_to_all.25.second, ...), custom_call_target="tpu_custom_call" | custom-call | tf_op jit(solution)/shard_map/pallas_call | solution.py:434
  80.4 0.0 copy-start.1
  80.4 6.9 %all-to-all-start.3 = ((s16[64,56,128]{2,1,0:T(8,128)(2,1)}), s16[64,56,128]{2,1,0:T(8,128)(2,1)S(1)}, u32[]{:S(2)}, u32[]{:S(2)}) async-start(s16[64,56,128]{2,1,0:T(8,128)(2,1)} %get-tuple-element.19), calls=%async_computation.3 | async-start | bytes 1835008 | tf_op jit(solution)/shard_map/all_to_all | solution.py:390
  87.4 3.3 %collective-permute-start = (s16[776,128]{1,0:T(8,128)(2,1)}, s16[776,128]{1,0:T(8,128)(2,1)S(1)}, u32[]{:S(2)}, u32[]{:S(2)}) collective-permute-start(s16[776,128]{1,0:T(8,128)(2,1)} %get-tuple-element.21), channel_id=1, source_target_pairs={{0,12},{12,24},{24,36},{36,0},{1,13},{13,25},{25,37},{37,1},{2,14}... | collective-permute-start | bytes 595976 | tf_op jit(solution)/shard_map/ppermute | solution.py:459
  90.6 4.3 %collective-permute-start.1 = (s16[776,128]{1,0:T(8,128)(2,1)}, s16[776,128]{1,0:T(8,128)(2,1)S(1)}, u32[]{:S(2)}, u32[]{:S(2)}) collective-permute-start(s16[776,128]{1,0:T(8,128)(2,1)} %get-tuple-element.22), channel_id=1, source_target_pairs={{0,24},{12,36},{24,0},{36,12},{1,25},{13,37},{25,1},{37,13},{2,26}... | collective-permute-start | bytes 595976 | tf_op jit(solution)/shard_map/ppermute | solution.py:459
  95.0 3.1 %collective-permute-start.2 = (s16[776,128]{1,0:T(8,128)(2,1)}, s16[776,128]{1,0:T(8,128)(2,1)S(1)}, u32[]{:S(2)}, u32[]{:S(2)}) collective-permute-start(s16[776,128]{1,0:T(8,128)(2,1)} %get-tuple-element.23), channel_id=1, source_target_pairs={{0,36},{12,0},{24,12},{36,24},{1,37},{13,1},{25,13},{37,25},{2,38}... | collective-permute-start | bytes 595976 | tf_op jit(solution)/shard_map/ppermute | solution.py:459
  98.1 2.1 %collective-permute-done.from_1 = s16[776,128]{1,0:T(8,128)(2,1)S(1)} collective-permute-done((s16[776,128]{1,0:T(8,128)(2,1)}, s16[776,128]{1,0:T(8,128)(2,1)S(1)}, u32[]{:S(2)}, u32[]{:S(2)}) %collective-permute-start) | collective-permute-done | bytes 198688 | tf_op jit(solution)/shard_map/ppermute | solution.py:459
  100.1 9.2 %collective-permute-done.1.from_2 = s16[776,128]{1,0:T(8,128)(2,1)S(1)} collective-permute-done((s16[776,128]{1,0:T(8,128)(2,1)}, s16[776,128]{1,0:T(8,128)(2,1)S(1)}, u32[]{:S(2)}, u32[]{:S(2)}) %collective-permute-start.1) | collective-permute-done | bytes 198688 | tf_op jit(solution)/shard_map/ppermute | solution.py:459
  109.3 0.0 collective-permute-done.2.from_3
  109.3 3.3 %all-to-all-done.3.got = s16[64,56,128]{2,1,0:T(8,128)(2,1)S(1)} async-done(((s16[64,56,128]{2,1,0:T(8,128)(2,1)}), s16[64,56,128]{2,1,0:T(8,128)(2,1)S(1)}, u32[]{:S(2)}, u32[]{:S(2)}) %all-to-all-start.3) | async-done | bytes 917536 | tf_op jit(solution)/shard_map/all_to_all | solution.py:390
  112.6 0.0 copy-done.1
  112.6 2.1 %shard_map.89 = s16[12,72,128]{2,1,0:T(8,128)(2,1)S(1)} custom-call(s32[4,128]{1,0:T(4,128)S(1)} %get-tuple-element.16.served, s16[64,56,128]{2,1,0:T(8,128)(2,1)S(1)} %all-to-all-done.3.got, f32[768,128]{1,0:T(8,128)S(1)} %copy-done.1, s16[776,128]{1,0:T(8,128)(2,1)S(1)} %collective-permute-done.from_1, s16[776,128]{1,0:T(8,128)(2,1)S(1)} %collective-permute-done.1.from_2, ...), custom_call_target="tpu_custom_call" | custom-call | tf_op jit(solution)/shard_map/pallas_call | solution.py:464
  114.7 15.0 %all_to_all.28.got = s16[12,72,128]{2,1,0:T(8,128)(2,1)S(1)} all-to-all(s16[12,72,128]{2,1,0:T(8,128)(2,1)S(1)} %shard_map.89), channel_id=1, replica_groups=mesh['y'=8,'core'=2,'x'=4,'z'=12] {'z'}, dimensions={0} | all-to-all | bytes 442368 | tf_op jit(solution)/shard_map/all_to_all | solution.py:390
  129.7 3.6 %shard_map.90 = (f32[2,128]{1,0:T(2,128)}, f32[4,16,128]{2,1,0:T(8,128)}, f32[16,128,128]{2,1,0:T(8,128)}) custom-call(s32[6,16]{1,0:T(8,128)S(1)} %stack.16.tab, bf16[16,192,128]{2,1,0:T(8,128)(2,1)S(1)} %bitcast.22, bf16[16,192,128]{2,1,0:T(8,128)(2,1)S(1)} %all_to_all.25.second, f32[16,128,128]{2,1,0:T(8,128)} %bitcast.23, ...), custom_call_target="tpu_custom_call" | custom-call | tf_op jit(solution)/shard_map/pallas_call | solution.py:466
  (6 shorter events, 0.1 us)
Async XLA Ops:
  0.6 0.7 copy-start.2
  0.7 0.7 copy-start.3
  3.8 36.3 %copy-start = (f32[1,1,16,128,128]{4,3,2,1,0:T(8,128)S(1)}, f32[1,1,16,128,128]{4,3,2,1,0:T(8,128)}, u32[]{:S(2)}) copy-start(f32[1,1,16,128,128]{4,3,2,1,0:T(8,128)} %param.11) | copy-start | bytes 3145732
  80.4 32.2 %copy-start.1 = (f32[768,128]{1,0:T(8,128)S(1)}, f32[768,128]{1,0:T(8,128)}, u32[]{:S(2)}) copy-start(f32[768,128]{1,0:T(8,128)} %get-tuple-element.20.own) | copy-start | bytes 1179652
  80.4 32.2 %all-to-all-start.3 = ((s16[64,56,128]{2,1,0:T(8,128)(2,1)}), s16[64,56,128]{2,1,0:T(8,128)(2,1)S(1)}, u32[]{:S(2)}, u32[]{:S(2)}) async-start(s16[64,56,128]{2,1,0:T(8,128)(2,1)} %get-tuple-element.19), calls=%async_computation.3 | async-start | bytes 1835008 | tf_op jit(solution)/shard_map/all_to_all | solution.py:390
  87.4 12.8 %collective-permute-start = (s16[776,128]{1,0:T(8,128)(2,1)}, s16[776,128]{1,0:T(8,128)(2,1)S(1)}, u32[]{:S(2)}, u32[]{:S(2)}) collective-permute-start(s16[776,128]{1,0:T(8,128)(2,1)} %get-tuple-element.21), channel_id=1, source_target_pairs={{0,12},{12,24},{24,36},{36,0},{1,13},{13,25},{25,37},{37,1},{2,14}... | collective-permute-start | bytes 595976 | tf_op jit(solution)/shard_map/ppermute | solution.py:459
  90.6 18.7 %collective-permute-start.1 = (s16[776,128]{1,0:T(8,128)(2,1)}, s16[776,128]{1,0:T(8,128)(2,1)S(1)}, u32[]{:S(2)}, u32[]{:S(2)}) collective-permute-start(s16[776,128]{1,0:T(8,128)(2,1)} %get-tuple-element.22), channel_id=1, source_target_pairs={{0,24},{12,36},{24,0},{36,12},{1,25},{13,37},{25,1},{37,13},{2,26}... | collective-permute-start | bytes 595976 | tf_op jit(solution)/shard_map/ppermute | solution.py:459
  95.0 14.4 %collective-permute-start.2 = (s16[776,128]{1,0:T(8,128)(2,1)}, s16[776,128]{1,0:T(8,128)(2,1)S(1)}, u32[]{:S(2)}, u32[]{:S(2)}) collective-permute-start(s16[776,128]{1,0:T(8,128)(2,1)} %get-tuple-element.23), channel_id=1, source_target_pairs={{0,36},{12,0},{24,12},{36,24},{1,37},{13,1},{25,13},{37,25},{2,38}... | collective-permute-start | bytes 595976 | tf_op jit(solution)/shard_map/ppermute | solution.py:459

commit v10 on v9

--- a/solution.py
+++ b/solution.py
@@ -325,10 +325,15 @@
 
 def last_kernel(
     scale, rate, tab, ft, second, mats_hbm, got, first_sums, targets,
-    logits, grads, mats, errs, sums, mats_in, sem,
+    logits, grads, mats, errs, sums, mats_in, sems,
 ):
-    load = pltpu.make_async_copy(mats_hbm, mats_in, sem)
-    load.start()
+    count = mats_in.shape[0] // sems.shape[0]
+    loads = [
+        pltpu.make_async_copy(mats_hbm.at[part], mats_in.at[part], sems.at[i])
+        for i, part in enumerate(pl.ds(i * count, count) for i in range(sems.shape[0]))
+    ]
+    for load in loads:
+        load.start()
     samples = second.shape[1]
     few = grads.shape[0]
     wide = 16 * few
@@ -351,7 +356,8 @@
     errs[...] = spread(errors + earlier, samples)
 
     group = math.gcd(LAST_GROUP, second.shape[0])
-    load.wait()
+    for load in loads:
+        load.wait()
 
     def step(q, carry):
         js = [q * group + i for i in range(group)]
@@ -471,7 +477,7 @@
             acc,
             pltpu.VMEM((per_block * few, 128), f32),
             pltpu.VMEM(mats.shape, f32),
-            pltpu.SemaphoreType.DMA(()),
+            pltpu.SemaphoreType.DMA((math.gcd(4, slots),)),
         ],
         far_in=(3,),
     )(tab, ft, second, pltpu.with_memory_space_constraint(pair_mats[0, 0], pltpu.HBM), got, sums, targets)

time: 135 us -> 135 us (level)
  no operation moved by 1% of the time
where the time goes in v10:
time: 135 us; the launch traced here: 133 us
  blocking collectives  85.1 us (63%)
  starting transfers between devices  17.6 us (13%)
  waiting for transfers between devices  14.5 us (11%)
  Pallas kernels  12.7 us (9%)
  between operations  1.47 us (1%)
  local copies, waits for them, and re-layouts  1.4 us (1%)
    all_to_all x4, blocking collectives, swap(): return lax.all_to_all(x, axes, split_axis=0, concat_axis=0, tiled=True)  85.1 us
    ppermute x3, waiting for transfers between devices, on_device(): lax.ppermute(side, 'x', [(i, (i + r) % n_x) for i in range(n_x)])  11.3 us
    ppermute x3, starting transfers between devices, on_device(): lax.ppermute(side, 'x', [(i, (i + r) % n_x) for i in range(n_x)])  10.7 us
    all_to_all x1, starting transfers between devices, swap(): return lax.all_to_all(x, axes, split_axis=0, concat_axis=0, tiled=True)  6.93 us
    pallas_call x1, Pallas kernels, on_device(): call(functools.partial(terms_kernel, scale, rate), [shape((groups * n_x,...  4.52 us
    pallas_call x1, Pallas kernels, on_device(): call(functools.partial(last_kernel, scale, rate), [shape((2, 128)), shape...  3.41 us
    all_to_all x1, waiting for transfers between devices, swap(): return lax.all_to_all(x, axes, split_axis=0, concat_axis=0, tiled=True)  3.26 us
  transfers between devices with their start and end apart: 4, of which 3 were waited for; matrix products, arithmetic and copies ran while one was open for 0% of the time, Pallas kernels for 0%

profile of v10, /device:TPU:1, one launch (start us, length us, event | category | flops | bytes accessed | tf_op | source)
XLA Modules:
  0.0 133.1 jit_solution(2464492092316991622)
XLA Ops:
  0.6 0.0 copy-start.2
  0.7 0.0 copy-start.3
  1.3 0.0 copy-done.3
  1.4 0.0 copy-done.2
  1.4 0.1 select_reduce_fusion
  1.5 1.3 %copy.11 = bf16[192,16,128]{2,0,1:T(8,128)(2,1)S(1)} copy(bf16[192,16,128]{2,1,0:T(8,128)(2,1)} %param.6) | data formatting | bytes 1572864 | tf_op args[0]
  2.9 0.1 select_reduce_fusion.1
  3.0 0.8 shard_map.85
  3.8 0.0 copy-start
  3.8 36.2 %all_to_all.25.second = bf16[16,192,128]{2,1,0:T(8,128)(2,1)S(1)} all-to-all(bf16[16,192,128]{2,1,0:T(8,128)(2,1)S(1)} %shard_map.85), channel_id=1, replica_groups=mesh['y'=8,'core'=2,'x'=4,'z'=12] {'y','core'}, dimensions={0} | all-to-all | bytes 1572864 | tf_op jit(solution)/shard_map/all_to_all | solution.py:396
  40.0 0.0 copy-done
  40.0 1.9 %shard_map.86 = (f32[64,2,128]{2,1,0:T(2,128)S(1)}, f32[2,128]{1,0:T(2,128)S(1)}) custom-call(s32[6,16]{1,0:T(8,128)S(1)} %stack.16.tab, bf16[16,192,128]{2,1,0:T(8,128)(2,1)S(1)} %bitcast.20, bf16[16,192,128]{2,1,0:T(8,128)(2,1)S(1)} %all_to_all.25.second, f32[16,128,128]{2,1,0:T(8,128)S(1)} %bitcast.24, s32[1,192]{1,0:T(1,128)} %bitcast.30), custom_call_target="tpu_custom_call" | custom-call | tf_op jit(solution)/shard_map/pallas_call | solution.py:432
  41.9 12.3 %all_to_all.26.parts = f32[64,2,128]{2,1,0:T(2,128)S(1)} all-to-all(f32[64,2,128]{2,1,0:T(2,128)S(1)} %get-tuple-element.15), channel_id=1, replica_groups=mesh['y'=8,'core'=2,'x'=4,'z'=12] {'y','core','x'}, dimensions={0} | all-to-all | bytes 131072 | tf_op jit(solution)/shard_map/all_to_all | solution.py:396
  54.3 0.1 shard_map.87
  54.4 21.5 %all_to_all.27.sums.first_sums = f32[12,2,128]{2,1,0:T(2,128)S(1)} all-to-all(f32[12,2,128]{2,1,0:T(2,128)S(1)} %get-tuple-element.17), channel_id=1, replica_groups=mesh['y'=8,'core'=2,'x'=4,'z'=12] {'z'}, dimensions={0} | all-to-all | bytes 24576 | tf_op jit(solution)/shard_map/all_to_all | solution.py:396
  75.9 4.5 %shard_map.88 = (s16[64,56,128]{2,1,0:T(8,128)(2,1)}, f32[768,128]{1,0:T(8,128)}, s16[776,128]{1,0:T(8,128)(2,1)}, s16[776,128]{1,0:T(8,128)(2,1)}, s16[776,128]{1,0:T(8,128)(2,1)}) custom-call(s32[6,16]{1,0:T(8,128)S(1)} %stack.16.tab, bf16[16,192,128]{2,1,0:T(8,128)(2,1)S(1)} %bitcast.21, bf16[16,192,128]{2,1,0:T(8,128)(2,1)S(1)} %all_to_all.25.second, ...), custom_call_target="tpu_custom_call" | custom-call | tf_op jit(solution)/shard_map/pallas_call | solution.py:440
  80.4 0.0 copy-start.1
  80.4 6.9 %all-to-all-start.3 = ((s16[64,56,128]{2,1,0:T(8,128)(2,1)}), s16[64,56,128]{2,1,0:T(8,128)(2,1)S(1)}, u32[]{:S(2)}, u32[]{:S(2)}) async-start(s16[64,56,128]{2,1,0:T(8,128)(2,1)} %get-tuple-element.19), calls=%async_computation.3 | async-start | bytes 1835008 | tf_op jit(solution)/shard_map/all_to_all | solution.py:396
  87.4 3.3 %collective-permute-start = (s16[776,128]{1,0:T(8,128)(2,1)}, s16[776,128]{1,0:T(8,128)(2,1)S(1)}, u32[]{:S(2)}, u32[]{:S(2)}) collective-permute-start(s16[776,128]{1,0:T(8,128)(2,1)} %get-tuple-element.21), channel_id=1, source_target_pairs={{0,12},{12,24},{24,36},{36,0},{1,13},{13,25},{25,37},{37,1},{2,14}... | collective-permute-start | bytes 595976 | tf_op jit(solution)/shard_map/ppermute | solution.py:465
  90.6 4.3 %collective-permute-start.1 = (s16[776,128]{1,0:T(8,128)(2,1)}, s16[776,128]{1,0:T(8,128)(2,1)S(1)}, u32[]{:S(2)}, u32[]{:S(2)}) collective-permute-start(s16[776,128]{1,0:T(8,128)(2,1)} %get-tuple-element.22), channel_id=1, source_target_pairs={{0,24},{12,36},{24,0},{36,12},{1,25},{13,37},{25,1},{37,13},{2,26}... | collective-permute-start | bytes 595976 | tf_op jit(solution)/shard_map/ppermute | solution.py:465
  95.0 3.1 %collective-permute-start.2 = (s16[776,128]{1,0:T(8,128)(2,1)}, s16[776,128]{1,0:T(8,128)(2,1)S(1)}, u32[]{:S(2)}, u32[]{:S(2)}) collective-permute-start(s16[776,128]{1,0:T(8,128)(2,1)} %get-tuple-element.23), channel_id=1, source_target_pairs={{0,36},{12,0},{24,12},{36,24},{1,37},{13,1},{25,13},{37,25},{2,38}... | collective-permute-start | bytes 595976 | tf_op jit(solution)/shard_map/ppermute | solution.py:465
  98.1 2.1 %collective-permute-done.from_1 = s16[776,128]{1,0:T(8,128)(2,1)S(1)} collective-permute-done((s16[776,128]{1,0:T(8,128)(2,1)}, s16[776,128]{1,0:T(8,128)(2,1)S(1)}, u32[]{:S(2)}, u32[]{:S(2)}) %collective-permute-start) | collective-permute-done | bytes 198688 | tf_op jit(solution)/shard_map/ppermute | solution.py:465
  100.1 9.2 %collective-permute-done.1.from_2 = s16[776,128]{1,0:T(8,128)(2,1)S(1)} collective-permute-done((s16[776,128]{1,0:T(8,128)(2,1)}, s16[776,128]{1,0:T(8,128)(2,1)S(1)}, u32[]{:S(2)}, u32[]{:S(2)}) %collective-permute-start.1) | collective-permute-done | bytes 198688 | tf_op jit(solution)/shard_map/ppermute | solution.py:465
  109.4 0.0 collective-permute-done.2.from_3
  109.4 3.3 %all-to-all-done.3.got = s16[64,56,128]{2,1,0:T(8,128)(2,1)S(1)} async-done(((s16[64,56,128]{2,1,0:T(8,128)(2,1)}), s16[64,56,128]{2,1,0:T(8,128)(2,1)S(1)}, u32[]{:S(2)}, u32[]{:S(2)}) %all-to-all-start.3) | async-done | bytes 917536 | tf_op jit(solution)/shard_map/all_to_all | solution.py:396
  112.6 0.0 copy-done.1
  112.6 2.1 %shard_map.89 = s16[12,72,128]{2,1,0:T(8,128)(2,1)S(1)} custom-call(s32[4,128]{1,0:T(4,128)S(1)} %get-tuple-element.16.served, s16[64,56,128]{2,1,0:T(8,128)(2,1)S(1)} %all-to-all-done.3.got, f32[768,128]{1,0:T(8,128)S(1)} %copy-done.1, s16[776,128]{1,0:T(8,128)(2,1)S(1)} %collective-permute-done.from_1, s16[776,128]{1,0:T(8,128)(2,1)S(1)} %collective-permute-done.1.from_2, ...), custom_call_target="tpu_custom_call" | custom-call | tf_op jit(solution)/shard_map/pallas_call | solution.py:470
  114.7 15.0 %all_to_all.28.got = s16[12,72,128]{2,1,0:T(8,128)(2,1)S(1)} all-to-all(s16[12,72,128]{2,1,0:T(8,128)(2,1)S(1)} %shard_map.89), channel_id=1, replica_groups=mesh['y'=8,'core'=2,'x'=4,'z'=12] {'z'}, dimensions={0} | all-to-all | bytes 442368 | tf_op jit(solution)/shard_map/all_to_all | solution.py:396
  129.7 3.4 %shard_map.90 = (f32[2,128]{1,0:T(2,128)}, f32[4,16,128]{2,1,0:T(8,128)}, f32[16,128,128]{2,1,0:T(8,128)}) custom-call(s32[6,16]{1,0:T(8,128)S(1)} %stack.16.tab, bf16[16,192,128]{2,1,0:T(8,128)(2,1)S(1)} %bitcast.22, bf16[16,192,128]{2,1,0:T(8,128)(2,1)S(1)} %all_to_all.25.second, f32[16,128,128]{2,1,0:T(8,128)} %bitcast.23, ...), custom_call_target="tpu_custom_call" | custom-call | tf_op jit(solution)/shard_map/pallas_call | solution.py:472
  (6 shorter events, 0.1 us)
Async XLA Ops:
  0.6 0.7 copy-start.2
  0.7 0.7 copy-start.3
  3.8 36.3 %copy-start = (f32[1,1,16,128,128]{4,3,2,1,0:T(8,128)S(1)}, f32[1,1,16,128,128]{4,3,2,1,0:T(8,128)}, u32[]{:S(2)}) copy-start(f32[1,1,16,128,128]{4,3,2,1,0:T(8,128)} %param.11) | copy-start | bytes 3145732
  80.4 32.2 %copy-start.1 = (f32[768,128]{1,0:T(8,128)S(1)}, f32[768,128]{1,0:T(8,128)}, u32[]{:S(2)}) copy-start(f32[768,128]{1,0:T(8,128)} %get-tuple-element.20.own) | copy-start | bytes 1179652
  80.4 32.2 %all-to-all-start.3 = ((s16[64,56,128]{2,1,0:T(8,128)(2,1)}), s16[64,56,128]{2,1,0:T(8,128)(2,1)S(1)}, u32[]{:S(2)}, u32[]{:S(2)}) async-start(s16[64,56,128]{2,1,0:T(8,128)(2,1)} %get-tuple-element.19), calls=%async_computation.3 | async-start | bytes 1835008 | tf_op jit(solution)/shard_map/all_to_all | solution.py:396
  87.4 12.8 %collective-permute-start = (s16[776,128]{1,0:T(8,128)(2,1)}, s16[776,128]{1,0:T(8,128)(2,1)S(1)}, u32[]{:S(2)}, u32[]{:S(2)}) collective-permute-start(s16[776,128]{1,0:T(8,128)(2,1)} %get-tuple-element.21), channel_id=1, source_target_pairs={{0,12},{12,24},{24,36},{36,0},{1,13},{13,25},{25,37},{37,1},{2,14}... | collective-permute-start | bytes 595976 | tf_op jit(solution)/shard_map/ppermute | solution.py:465
  90.6 18.7 %collective-permute-start.1 = (s16[776,128]{1,0:T(8,128)(2,1)}, s16[776,128]{1,0:T(8,128)(2,1)S(1)}, u32[]{:S(2)}, u32[]{:S(2)}) collective-permute-start(s16[776,128]{1,0:T(8,128)(2,1)} %get-tuple-element.22), channel_id=1, source_target_pairs={{0,24},{12,36},{24,0},{36,12},{1,25},{13,37},{25,1},{37,13},{2,26}... | collective-permute-start | bytes 595976 | tf_op jit(solution)/shard_map/ppermute | solution.py:465
  95.0 14.4 %collective-permute-start.2 = (s16[776,128]{1,0:T(8,128)(2,1)}, s16[776,128]{1,0:T(8,128)(2,1)S(1)}, u32[]{:S(2)}, u32[]{:S(2)}) collective-permute-start(s16[776,128]{1,0:T(8,128)(2,1)} %get-tuple-element.23), channel_id=1, source_target_pairs={{0,36},{12,0},{24,12},{36,24},{1,37},{13,1},{25,13},{37,25},{2,38}... | collective-permute-start | bytes 595976 | tf_op jit(solution)/shard_map/ppermute | solution.py:465
